TPU v7x, 32 devices: a whole 2x2x4 slice. The times are simulated.
32 devices in a mesh: db: 16 (over z, x, core), mp: 2 (over y).
Axes of the slice: x: 2, y: 2, z: 4, core: 2. Of those that a mesh axis runs over, the one named last changes fastest.
Arguments:
- queries: bfloat16 [32768, 2048], P('db', 'mp'), may hold values from -400 to 400, as said below
- encodings: bfloat16 [512, 128, 896], P(('db', 'mp')), may hold values from -6 to 6
- key_weight: bfloat16 [896, 2048], P('db', 'mp'), may hold values from -0.1875 to 0.1875
- value_weight: bfloat16 [896, 2048], P('db', 'mp'), may hold values from -0.1875 to 0.1875
- nbr_shard: int32 [512, 2], P('db'), may hold values from 0 to 15, all different within a row; in each aligned block of 32 rows (0 to 31, 32 to 63, ...) at most 8 rows name the same one
- nbr_row: int32 [512, 2], P('db'), may hold values from 0 to 31
Outputs:
- cross_out: bfloat16 [32768, 2048], P('db', 'mp')
Inputs may be any that keep to these rules, and one draw needn't show every extreme that they name: `queries`: some query rows may be far larger than the rest. `nbr_shard`: among the spans of one index of db no shard is named by more than 8 spans; the 2 shards of one span differ.
All inputs are finite; a program needn't handle non-finite values.
Results may differ from a plain program's by a relative error of at most 0.025.
Values may be sent and summed in bfloat16 or wider, within the bound.
No kernel may reach another device: no remote copies, remote signals or barrier semaphores. Data moves between devices by JAX's collectives and lax.ppermute only.
A program may use at most 256 MiB of HBM per device.

v0:
```python
import functools
import math

import jax
import jax.numpy as jnp
from jax import lax
from jax.experimental import pallas as pl
from jax.experimental.pallas import tpu as pltpu
from jax.sharding import PartitionSpec as P


DH = 128
SPAN = 64
SEQ = 128
LANES = 8
CHUNKS = 2
MOST_SHIFTS = 8
TAIL = 16
FAST_SLOTS = 48
BF16 = jnp.bfloat16
F32 = jnp.float32
SCALE = 1.0 / math.sqrt(DH)
BOTH = ("db", "mp")
CONTRACT_LAST = (((1,), (1,)), ((), ()))


def project_body(rows_ref, weight_ref, out_ref):
    lanes, count, piece, width = rows_ref.shape
    rows = rows_ref[...]
    stacked = jnp.concatenate([rows[:, j].reshape(lanes * piece, width) for j in range(count)], axis=0)
    out_ref[...] = jnp.dot(stacked, weight_ref[...], preferred_element_type=F32).astype(BF16)


def project(rows, weights):
    lanes, count, piece, width = rows.shape
    per_step = math.gcd(count, 8)
    tokens = lanes * piece
    return pl.pallas_call(
        project_body,
        out_shape=jax.ShapeDtypeStruct((count * tokens, weights.shape[1]), BF16),
        grid=(count // per_step,),
        in_specs=[
            pl.BlockSpec((lanes, per_step, piece, width), lambda i: (0, i, 0, 0)),
            pl.BlockSpec(weights.shape, lambda i: (0, 0)),
        ],
        out_specs=pl.BlockSpec((per_step * tokens, weights.shape[1]), lambda i: (i, 0)),
        name="project",
    )(rows, weights)


def even_body(query_ref, rows_ref, weight_ref, *refs, per_step, neighbours):
    early_refs, out_ref = refs[:-1], refs[-1]
    columns = query_ref.shape[1]
    heads = columns // DH
    lanes, _, piece, width = rows_ref.shape
    tokens = lanes * piece
    first = SPAN - 1
    low = first // 16 * 16
    rows = rows_ref[...]
    stacked = jnp.concatenate(
        [rows[:, j].reshape(tokens, width) for j in range(per_step * neighbours)], axis=0
    )
    late = jnp.dot(stacked, weight_ref[...], preferred_element_type=F32).astype(BF16)
    position = low + lax.broadcasted_iota(jnp.int32, (SEQ - low, DH), 0)
    span = neighbours * tokens
    for s in range(per_step):
        out_ref[s * SEQ : s * SEQ + low, :] = jnp.zeros((low, columns), BF16)
        for h in range(heads):
            lo, hi = h * DH, (h + 1) * DH
            parts = [(r, s * span, span) for r in (*early_refs, late)]
            keys = jnp.concatenate([r[b : b + n, lo:hi] for r, b, n in parts], axis=0)
            values = jnp.concatenate([r[b : b + n, columns + lo : columns + hi] for r, b, n in parts], axis=0)
            query = query_ref[s * SEQ + low : (s + 1) * SEQ, lo:hi]
            scores = lax.dot_general(query, keys, CONTRACT_LAST, preferred_element_type=F32) * SCALE
            largest = jnp.max(scores, axis=1, keepdims=True)
            expscore = jnp.exp(scores - largest)
            total = jnp.sum(expscore, axis=1, keepdims=True)
            mixed = jnp.dot(expscore.astype(BF16), values, preferred_element_type=F32)
            attended = mixed / total
            attended = jnp.where(position < first, 0.0, attended)
            out_ref[s * SEQ + low : (s + 1) * SEQ, lo:hi] = attended.astype(BF16)


def even_attention(queries, rows, weights, early):
    tokens, columns = queries.shape
    sequences = tokens // SEQ
    lanes, count, piece, width = rows.shape
    neighbours = count // sequences
    per_step = math.gcd(sequences, 2)
    early_rows = lanes * piece * per_step * neighbours
    early_spec = pl.BlockSpec((early_rows, weights.shape[1]), lambda i: (i, 0))
    return pl.pallas_call(
        functools.partial(even_body, per_step=per_step, neighbours=neighbours),
        out_shape=jax.ShapeDtypeStruct(queries.shape, BF16),
        grid=(sequences // per_step,),
        in_specs=[
            pl.BlockSpec((per_step * SEQ, columns), lambda i: (i, 0)),
            pl.BlockSpec((lanes, per_step * neighbours, piece, width), lambda i: (0, i, 0, 0)),
            pl.BlockSpec(weights.shape, lambda i: (0, 0)),
            *[early_spec for _ in early],
        ],
        out_specs=pl.BlockSpec((per_step * SEQ, columns), lambda i: (i, 0)),
        name="even_attention",
    )(queries, rows, weights, *early)


def patch_body(slot_ref, out_in_ref, odd_ref, out_ref, *, neighbours):
    columns = out_ref.shape[1]
    heads = columns // DH
    sequence = pl.program_id(0)
    picked = [odd_ref[pl.ds(slot_ref[sequence * neighbours + j], 1), :] for j in range(neighbours)]
    last = lax.broadcasted_iota(jnp.int32, (TAIL, DH), 0) == TAIL - 1
    for h in range(heads):
        lo, hi = h * DH, (h + 1) * DH
        maxima = [p[:, columns + h : columns + h + 1] for p in picked]
        sums = [p[:, columns + DH // 2 + h : columns + DH // 2 + h + 1] for p in picked]
        top = functools.reduce(jnp.maximum, maxima)
        each = [jnp.exp(m - top) for m in maxima]
        under = sum(e * t for e, t in zip(each, sums))
        over = sum(e * p[:, lo:hi] for e, p in zip(each, picked))
        out_ref[:, lo:hi] = jnp.where(last, (over / under).astype(BF16), out_in_ref[:, lo:hi])


def patch(slots, out, odd):
    tokens, columns = out.shape
    sequences = tokens // SEQ
    tail = pl.BlockSpec((TAIL, columns), lambda i, s: (i * (SEQ // TAIL) + SEQ // TAIL - 1, 0))
    return pl.pallas_call(
        functools.partial(patch_body, neighbours=slots.shape[0] // sequences),
        out_shape=jax.ShapeDtypeStruct(out.shape, BF16),
        grid_spec=pltpu.PrefetchScalarGridSpec(
            num_scalar_prefetch=1,
            grid=(sequences,),
            in_specs=[tail, pl.BlockSpec(odd.shape, lambda i, s: (0, 0))],
            out_specs=tail,
        ),
        input_output_aliases={1: 0},
        name="patch",
    )(slots, out, odd)


def gather_body(index_ref, *refs, rows, copies):
    sources, out_ref, sem = refs[:-2], refs[-2], refs[-1]
    size = sources[0].shape[0]
    wanted = out_ref.shape[0] // (rows * copies)

    def step(i, carry):
        at = index_ref[i]
        base = i // wanted * (copies * wanted) + i % wanted
        for k, source in enumerate(sources):
            @pl.when((at >= k * size) & (at < (k + 1) * size))
            def _():
                for c in range(copies):
                    pltpu.make_async_copy(
                        source.at[at - k * size], out_ref.at[base + c * wanted], sem
                    ).start()

        return carry

    lax.fori_loop(0, rows * wanted, step, 0)
    whole = out_ref.at[pl.ds(0, rows * wanted * copies)]
    pltpu.make_async_copy(whole, whole, sem).wait()


def gather_rows(index, sources, groups, copies):
    total = index.shape[0] * copies
    return pl.pallas_call(
        functools.partial(gather_body, rows=groups, copies=copies),
        out_shape=jax.ShapeDtypeStruct((total,) + sources[0].shape[1:], sources[0].dtype),
        grid_spec=pltpu.PrefetchScalarGridSpec(
            num_scalar_prefetch=1,
            grid=(1,),
            in_specs=[pl.BlockSpec(memory_space=pl.ANY) for _ in sources],
            out_specs=pl.BlockSpec(memory_space=pl.ANY),
            scratch_shapes=[pltpu.SemaphoreType.DMA],
        ),
        name="gather_rows",
    )(index, *sources)


def odd_body(query_ref, want_ref, rows_ref, weight_ref, out_ref):
    columns = query_ref.shape[1]
    heads = columns // DH
    per_step, tokens, width = rows_ref.shape
    base = pl.program_id(0) * per_step
    projected = jnp.dot(
        rows_ref[...].reshape(per_step * tokens, width), weight_ref[...], preferred_element_type=F32
    ).astype(BF16)
    want = want_ref[...] - base
    here = [want == r for r in range(per_step)]
    inside = (want >= 0) & (want < per_step)
    lane = lax.broadcasted_iota(jnp.int32, (want.shape[0], DH), 1)
    stats = out_ref[:, columns:]
    for h in range(heads):
        lo, hi = h * DH, (h + 1) * DH
        scores = (
            lax.dot_general(
                query_ref[:, lo:hi], projected[:, lo:hi], CONTRACT_LAST, preferred_element_type=F32
            )
            * SCALE
        )
        mine = jnp.zeros((want.shape[0], tokens), F32)
        for r in range(per_step):
            mine = jnp.where(here[r], scores[:, r * tokens : (r + 1) * tokens], mine)
        largest = jnp.max(mine, axis=1, keepdims=True)
        expscore = jnp.exp(mine - largest)
        total = jnp.sum(expscore, axis=1, keepdims=True)
        spread = jnp.concatenate([jnp.where(here[r], expscore, 0.0) for r in range(per_step)], axis=1)
        mixed = jnp.dot(spread.astype(BF16), projected[:, columns + lo : columns + hi], preferred_element_type=F32)
        out_ref[:, lo:hi] = jnp.where(inside, mixed, out_ref[:, lo:hi])
        stats = jnp.where(inside & (lane == h), largest, stats)
        stats = jnp.where(inside & (lane == DH // 2 + h), total, stats)
    out_ref[:, columns:] = stats


def odd_attention(queries, want, rows, weights):
    slots, columns = queries.shape
    count, tokens, width = rows.shape
    per_step = math.gcd(count, 4)
    return pl.pallas_call(
        odd_body,
        out_shape=jax.ShapeDtypeStruct((slots, columns + DH), F32),
        grid=(count // per_step,),
        in_specs=[
            pl.BlockSpec((slots, columns), lambda i: (0, 0)),
            pl.BlockSpec((slots, DH), lambda i: (0, 0)),
            pl.BlockSpec((per_step, tokens, width), lambda i: (i, 0, 0)),
            pl.BlockSpec(weights.shape, lambda i: (0, 0)),
        ],
        out_specs=pl.BlockSpec((slots, columns + DH), lambda i: (0, 0)),
        name="odd_attention",
    )(queries, want, rows, weights)


def local(queries, encodings, key_weight, value_weight, nbr_shard, nbr_row):
    shards = lax.axis_size("db")
    parts = lax.axis_size("mp")
    group = max(1, LANES // parts)
    lanes = group * parts
    planes = shards // group
    columns = queries.shape[1]
    held, tokens, width = encodings.shape
    piece = tokens // (lanes * CHUNKS)
    shard_rows = held * parts
    plane_rows = group * shard_rows
    span_count, neighbours = nbr_shard.shape
    sequences = queries.shape[0] // SEQ
    wanted = sequences * neighbours
    capacity = max(2, 4 * span_count // shards)
    most = min(plane_rows, group * wanted, group * group * capacity)
    fast = min(most, FAST_SLOTS)
    plane_groups = [[a * lanes + b for b in range(lanes)] for a in range(planes)]
    lane_groups = [[a * lanes + b for a in range(planes)] for b in range(lanes)]
    db_index = lax.axis_index("db")
    plane_index = db_index // group

    def swap(x, groups):
        return lax.all_to_all(x, BOTH, 0, 0, axis_index_groups=groups, tiled=True)

    def across(blocks):
        if planes > MOST_SHIFTS:
            stacked = jnp.stack(blocks)
            ordered = jnp.take(stacked, (jnp.arange(planes) - plane_index) % planes, axis=0, mode="clip")
            ordered = swap(ordered.reshape((-1,) + stacked.shape[2:]), lane_groups).reshape(stacked.shape)
            moved = jnp.take(ordered, (plane_index - jnp.arange(planes)) % planes, axis=0, mode="clip")
            return [moved.reshape((-1,) + stacked.shape[2:])]
        moved = [blocks[0]]
        for k in range(1, planes):
            pairs = [
                (a * lanes + b, (a + k) % planes * lanes + b) for a in range(planes) for b in range(lanes)
            ]
            moved.append(lax.ppermute(blocks[k], BOTH, pairs))
        return moved

    table = jnp.concatenate([nbr_shard.reshape(-1), nbr_row.reshape(-1)])
    table = jnp.broadcast_to(table[None, None], (shards, 1, table.shape[0]))
    table = lax.all_to_all(table, "db", 0, 0, tiled=True).reshape(
        shards, 2, sequences, SEQ // SPAN, neighbours
    )
    table_shard, table_row = table[:, 0], table[:, 1]

    weights = lax.all_gather(
        jnp.concatenate([key_weight, value_weight], axis=1), "db", axis=0, tiled=True
    )

    pieces = jnp.transpose(encodings.reshape(held, lanes, CHUNKS, piece, width), (2, 1, 0, 3, 4))
    plane_pieces = []

    def spread(chunk, after):
        sending, _ = lax.optimization_barrier((pieces[chunk].reshape(lanes * held, piece, width), after))
        plane_pieces.append(swap(sending, plane_groups))

    spread(0, table)

    odd_shard = table_shard[:, :, 1].reshape(shards, wanted)
    odd_row = table_row[:, :, 1].reshape(shards, wanted)
    earlier = jnp.arange(wanted)
    same = (odd_shard[:, :, None] == odd_shard[:, None, :]) & (earlier[None, None, :] < earlier[None, :, None])
    odd_rank = jnp.sum(same.astype(jnp.int32), axis=2)
    arriving = (odd_shard == db_index)[:, None, :] & (
        odd_rank[:, None, :] == jnp.arange(capacity, dtype=jnp.int32)[None, :, None]
    )
    slot_row = jnp.sum(jnp.where(arriving, odd_row[:, None, :] + 1, 0), axis=2) - 1
    my_slot = lax.dynamic_index_in_dim(odd_shard * capacity + odd_rank, db_index, 0, keepdims=False)
    slots = jnp.arange(shards * capacity, dtype=jnp.int32)
    chosen = my_slot[None, :] == slots[:, None]
    sender = jnp.sum(jnp.where(chosen, (earlier // neighbours).astype(jnp.int32)[None, :], 0), axis=1)
    last_rows = queries.reshape(sequences, SEQ, columns)[:, SEQ - 1]
    odd_query = jnp.take(last_rows, sender, axis=0, mode="clip").reshape(shards, capacity, columns)
    odd_query, _ = lax.optimization_barrier((odd_query, plane_pieces[0]))
    odd_query = lax.all_to_all(odd_query, "db", 0, 0, tiled=True)
    odd_query = odd_query.reshape(shards * capacity, columns)

    for chunk in range(1, CHUNKS):
        spread(chunk, odd_query if chunk == 1 else plane_pieces[-1])

    even_id = (table_shard[:, :, 0] * shard_rows + table_row[:, :, 0]).reshape(planes, group * wanted)
    ids = jnp.arange(planes * plane_rows, dtype=jnp.int32)
    want = jnp.any(even_id[:, :, None] == ids[None, None, :], axis=1).reshape(planes, planes, plane_rows)
    below = jnp.arange(plane_rows)
    before = (below[:, None] < below[None, :]).astype(BF16)
    rank = jnp.dot(want.astype(BF16), before, preferred_element_type=F32).astype(jnp.int32)
    fits = jnp.max(jnp.sum(want.astype(jnp.int32), axis=2)) <= fast
    mine_want = lax.dynamic_index_in_dim(want, plane_index, 1, keepdims=False)
    mine_rank = lax.dynamic_index_in_dim(rank, plane_index, 1, keepdims=False)
    picks = mine_want[:, None, :] & (
        mine_rank[:, None, :] == jnp.arange(fast, dtype=jnp.int32)[None, :, None]
    )
    send_rows = jnp.sum(jnp.where(picks, below[None, None, :].astype(jnp.int32), 0), axis=2)
    steps = jnp.arange(planes, dtype=jnp.int32)
    upward = (plane_index + steps) % planes
    send_rows = jnp.sum(
        jnp.where(upward[:, None, None] == steps[None, :, None], send_rows[None], 0), axis=1
    )
    my_ids = lax.dynamic_index_in_dim(even_id, plane_index, 0, keepdims=False)
    my_rank = lax.dynamic_index_in_dim(rank, plane_index, 0, keepdims=False).reshape(-1)
    place = jnp.sum(jnp.where(my_ids[:, None] == ids[None, :], my_rank[None, :], 0), axis=1)
    my_step = (plane_index + planes - my_ids // plane_rows) % planes

    def exact(source):
        return [jnp.take(source, send_rows[k], axis=0, mode="clip") for k in range(planes)]

    def whole(source):
        return [source] * planes

    def exchange(sources, select, index):
        received, arrived = [], []
        for source in sources:
            sending = select(source)
            if received:
                sending, _ = lax.optimization_barrier((sending, received[-1]))
            received.append(across(sending))
            outgoing = gather_rows(index, received[-1], group, parts)
            if arrived:
                outgoing, _ = lax.optimization_barrier((outgoing, arrived[-1]))
            arrived.append(swap(outgoing, plane_groups))
        return [a.reshape(lanes, wanted, piece, width) for a in arrived]

    part_index = lax.axis_index("mp")
    sharing, _ = lax.optimization_barrier((encodings, plane_pieces[0]))
    shared = [encodings]
    for k in range(1, parts):
        shared.append(lax.ppermute(sharing, "mp", [(m, (m + k) % parts) for m in range(parts)]))
    shard_enc = jnp.concatenate(shared, axis=0)
    slot_step = (part_index + parts - slot_row // held) % parts
    slot_row = jnp.where(slot_row >= 0, slot_step * held + slot_row % held, -1)
    slot_lanes = jnp.broadcast_to(slot_row.reshape(-1, 1), (shards * capacity, DH))
    odd_part = odd_attention(odd_query, slot_lanes, shard_enc, weights)

    def attend(select, index):
        *early, late = exchange(plane_pieces, select, index)
        early = [project(e, weights) for e in early]
        return even_attention(queries, late, weights, early), late

    result, last = attend(exact, my_step * fast + jnp.minimum(place, fast - 1))
    odd_part, _ = lax.optimization_barrier((odd_part, last))
    odd_part = lax.all_to_all(odd_part.reshape(shards, capacity, columns + DH), "db", 0, 0, tiled=True)
    odd_part = odd_part.reshape(shards * capacity, columns + DH)
    if fast < most:
        result, odd_part = lax.optimization_barrier((result, odd_part))
        result = lax.cond(
            fits,
            lambda done: done,
            lambda done: attend(whole, my_step * plane_rows + my_ids % plane_rows)[0],
            result,
        )
    return patch(my_slot, result, odd_part)


def solution(mesh):
    placed = (
        P("db", "mp"),
        P(("db", "mp"), None, None),
        P("db", "mp"),
        P("db", "mp"),
        P("db", None),
        P("db", None),
    )

    return jax.shard_map(local, mesh=mesh, in_specs=placed, out_specs=P("db", "mp"), check_vma=False)
```

profile of v0, /device:TPU:11, one launch (start us, length us, event | category | flops | bytes accessed | tf_op | source)
XLA Modules:
  0.0 578.1 jit_solution(605298976669688075)
XLA Ops:
  6.5 0.8 copy.58
  7.3 0.1 reshape.204
  7.4 0.8 copy.59
  8.2 0.1 reshape.205
  8.3 0.6 broadcast_in_dim.124
  9.0 6.5 %all-to-all-start.2 = ((s32[16,1,128]{2,1,0:T(1,128)}), s32[16,1,128]{2,1,0:T(1,128)S(1)}, u32[]{:S(2)}, u32[]{:S(2)}) async-start(s32[16,1,128]{2,1,0:T(1,128)} %broadcast_in_dim.124), calls=%async_computation.2 | async-start | bytes 16384 | tf_op jit(solution)/shard_map/all_to_all | solution.py:277
  15.5 2.6 copy.80
  18.1 2.2 fusion.16
  20.3 0.1 copy.60
  20.4 4.3 all-to-all-start.3
  24.7 1.0 slice.81
  25.9 0.1 copy.76
  26.2 0.2 copy.67
  26.4 0.1 add.128
  26.5 0.5 convert_reduce_fusion
  27.0 0.1 select_reduce_fusion.3
  27.1 1.6 gather_fusion
  28.7 18.2 %all-to-all-done.3 = bf16[128,8,896]{2,1,0:T(8,128)(2,1)S(1)} async-done(((bf16[128,8,896]{2,1,0:T(8,128)(2,1)}), bf16[128,8,896]{2,1,0:T(8,128)(2,1)S(1)}, u32[]{:S(2)}, u32[]{:S(2)}) %all-to-all-start.3) | async-done | bytes 1835040 | tf_op jit(solution)/shard_map/all_to_all | solution.py:258
  46.9 6.0 %all-to-all-start.4 = ((bf16[16,8,1024]{2,1,0:T(8,128)(2,1)}), bf16[16,8,1024]{2,1,0:T(8,128)(2,1)S(1)}, u32[]{:S(2)}, u32[]{:S(2)}) async-start(bf16[16,8,1024]{2,1,0:T(8,128)(2,1)} %bitcast.15), calls=%async_computation.4 | async-start | bytes 524288 | tf_op jit(solution)/shard_map/all_to_all | solution.py:311
  52.9 0.2 fusion.2
  53.2 0.1 convolution_convert_fusion
  53.3 7.5 %all-to-all-done.4 = bf16[16,8,1024]{2,1,0:T(8,128)(2,1)S(1)} async-done(((bf16[16,8,1024]{2,1,0:T(8,128)(2,1)}), bf16[16,8,1024]{2,1,0:T(8,128)(2,1)S(1)}, u32[]{:S(2)}, u32[]{:S(2)}) %all-to-all-start.4) | async-done | bytes 262176 | tf_op jit(solution)/shard_map/all_to_all | solution.py:311
  60.9 4.4 all-to-all-start.5
  65.3 0.1 select_reduce_fusion.1
  65.4 0.1 select_reduce_fusion.4
  65.6 1.5 gather_fusion.6
  67.1 1.9 collective-permute-start.6
  69.0 1.5 gather_fusion.7
  70.5 2.5 collective-permute-start.7
  73.0 1.5 gather_fusion.8
  74.5 1.7 pad_maximum_fusion.1
  76.2 0.2 select_reduce_fusion
  76.4 0.6 minimum_add_fusion
  77.0 1.5 gather_fusion.5
  78.5 6.6 %collective-permute-done.6.refs_1_ = bf16[48,8,896]{2,1,0:T(8,128)(2,1)S(1)} collective-permute-done((bf16[48,8,896]{2,1,0:T(8,128)(2,1)}, bf16[48,8,896]{2,1,0:T(8,128)(2,1)S(1)}, u32[]{:S(2)}, u32[]{:S(2)}) %collective-permute-start.6) | collective-permute-done | bytes 688160 | tf_op jit(solution)/shard_map/ppermute | solution.py:272
  85.1 50.2 %collective-permute-done.7.refs_2_ = bf16[48,8,896]{2,1,0:T(8,128)(2,1)S(1)} collective-permute-done((bf16[48,8,896]{2,1,0:T(8,128)(2,1)}, bf16[48,8,896]{2,1,0:T(8,128)(2,1)S(1)}, u32[]{:S(2)}, u32[]{:S(2)}) %collective-permute-start.7) | collective-permute-done | bytes 688160 | tf_op jit(solution)/shard_map/ppermute | solution.py:272
  135.3 4.1 collective-permute-done.8.refs_3_
  139.4 113.1 %gather_rows.7 = bf16[256,8,896]{2,1,0:T(8,128)(2,1)} custom-call(s32[128]{0:T(128)} %get-tuple-element.56.index_ref, bf16[48,8,896]{2,1,0:T(8,128)(2,1)} %gather_fusion.5, bf16[48,8,896]{2,1,0:T(8,128)(2,1)} %copy-done.5, bf16[48,8,896]{2,1,0:T(8,128)(2,1)} %copy-done.6, bf16[48,8,896]{2,1,0:T(8,128)(2,1)} %collective-permute-done.8.refs_3_), custom_call_target="tpu_custom_call" | custom-call | tf_op jit(solution)/shard_map/gather_rows/pallas_call | solution.py:167
  252.5 4.9 all-to-all-start.6
  257.4 1.2 collective-permute-start.12
  258.6 3.0 gather_fusion.1
  261.6 3.0 gather_fusion.4
  264.6 3.0 gather_fusion.3
  267.6 3.0 gather_fusion.2
  270.6 0.5 collective-permute-start.10
  271.2 1.5 collective-permute-start.11
  272.6 14.6 %collective-permute-done.9.refs_1_ = bf16[48,8,896]{2,1,0:T(8,128)(2,1)S(1)} collective-permute-done((bf16[48,8,896]{2,1,0:T(8,128)(2,1)}, bf16[48,8,896]{2,1,0:T(8,128)(2,1)S(1)}, u32[]{:S(2)}, u32[]{:S(2)}) %collective-permute-start.9) | collective-permute-done | bytes 688160 | tf_op jit(solution)/shard_map/ppermute | solution.py:272
  287.3 42.3 %collective-permute-done.10.refs_2_ = bf16[48,8,896]{2,1,0:T(8,128)(2,1)S(1)} collective-permute-done((bf16[48,8,896]{2,1,0:T(8,128)(2,1)}, bf16[48,8,896]{2,1,0:T(8,128)(2,1)S(1)}, u32[]{:S(2)}, u32[]{:S(2)}) %collective-permute-start.10) | collective-permute-done | bytes 688160 | tf_op jit(solution)/shard_map/ppermute | solution.py:272
  329.6 2.1 collective-permute-done.11.refs_3_
  331.6 113.1 %gather_rows.6 = bf16[256,8,896]{2,1,0:T(8,128)(2,1)} custom-call(s32[128]{0:T(128)} %get-tuple-element.56.index_ref, bf16[48,8,896]{2,1,0:T(8,128)(2,1)} %gather_fusion.1, bf16[48,8,896]{2,1,0:T(8,128)(2,1)} %copy-done.7, bf16[48,8,896]{2,1,0:T(8,128)(2,1)} %copy-done.8, bf16[48,8,896]{2,1,0:T(8,128)(2,1)} %collective-permute-done.11.refs_3_), custom_call_target="tpu_custom_call" | custom-call | tf_op jit(solution)/shard_map/gather_rows/pallas_call | solution.py:167
  444.7 5.1 all-to-all-start.7
  449.9 0.1 copy.72
  450.0 0.4 select_reduce_fusion.2
  450.4 0.1 sub.50
  450.5 6.8 %pad_maximum_fusion.rows_ref = bf16[32,128,896]{2,1,0:T(8,128)(2,1)} fusion(bf16[16,128,896]{2,1,0:T(8,128)(2,1)} %collective-permute-done.12, bf16[16,128,896]{2,1,0:T(8,128)(2,1)} %param.9), kind=kLoop, calls=%fused_computation.14 | loop fusion | flops 3670016 | bytes 14680064 | tf_op jit(solution)/shard_map/concatenate | solution.py:364
  457.3 0.7 broadcast_in_dim.142.want_ref
  458.0 38.7 %odd_attention.1 = f32[128,1152]{1,0:T(8,128)} custom-call(bf16[128,1024]{1,0:T(8,128)(2,1)} %bitcast.61, s32[128,128]{1,0:T(8,128)} %broadcast_in_dim.142.want_ref, bf16[32,128,896]{2,1,0:T(8,128)(2,1)} %pad_maximum_fusion.rows_ref, bf16[896,2048]{1,0:T(8,128)(2,1)} %all-gather.2.cloned.1.call-done.weight_ref), custom_call_target="tpu_custom_call" | custom-call | tf_op jit(solution)/shard_map/odd_attention/pallas_call | solution.py:220
  496.7 6.4 %all-to-all-start.8 = ((f32[16,8,1152]{2,1,0:T(8,128)}), f32[16,8,1152]{2,1,0:T(8,128)S(1)}, u32[]{:S(2)}, u32[]{:S(2)}) async-start(f32[16,8,1152]{2,1,0:T(8,128)} %bitcast.60), calls=%async_computation.8 | async-start | bytes 1179648 | tf_op jit(solution)/shard_map/all_to_all | solution.py:377
  503.2 0.1 convert_reduce_fusion.1
  503.3 0.6 reduce_max.9
  504.6 13.1 %project.3.refs_0_ = bf16[2048,2048]{1,0:T(8,128)(2,1)} custom-call(bf16[8,32,8,896]{3,2,1,0:T(8,128)(2,1)} %bitcast.27.rows_ref, bf16[896,2048]{1,0:T(8,128)(2,1)} %all-gather.2.cloned.1.call-done.weight_ref), custom_call_target="tpu_custom_call" | custom-call | tf_op jit(solution)/shard_map/project/pallas_call | solution.py:38
  517.8 42.4 %even_attention.3 = bf16[2048,1024]{1,0:T(8,128)(2,1)} custom-call(bf16[2048,1024]{1,0:T(8,128)(2,1)} %query_ref.1, bf16[8,32,8,896]{3,2,1,0:T(8,128)(2,1)} %bitcast.26.rows_ref, bf16[896,2048]{1,0:T(8,128)(2,1)} %all-gather.2.cloned.1.call-done.weight_ref, bf16[2048,2048]{1,0:T(8,128)(2,1)} %project.3.refs_0_), custom_call_target="tpu_custom_call" | custom-call | tf_op jit(solution)/shard_map/even_attention/pallas_call | solution.py:92
  560.2 0.8 copy-done
  561.0 10.2 %patch.1 = bf16[2048,1024]{1,0:T(8,128)(2,1)} custom-call(s32[32]{0:T(128)} %copy-done.9, bf16[2048,1024]{1,0:T(8,128)(2,1)} %get-tuple-element.69.out_in_ref, f32[128,1152]{1,0:T(8,128)} %bitcast.59), custom_call_target="tpu_custom_call", output_to_operand_aliasing={{}: (1, {})} | custom-call | tf_op jit(solution)/shard_map/patch/pallas_call | solution.py:128
  (53 shorter events, 0.8 us)
Async XLA Ops:
  9.0 11.3 %all-to-all-start.2 = ((s32[16,1,128]{2,1,0:T(1,128)}), s32[16,1,128]{2,1,0:T(1,128)S(1)}, u32[]{:S(2)}, u32[]{:S(2)}) async-start(s32[16,1,128]{2,1,0:T(1,128)} %broadcast_in_dim.124), calls=%async_computation.2 | async-start | bytes 16384 | tf_op jit(solution)/shard_map/all_to_all | solution.py:277
  20.4 26.5 %all-to-all-start.3 = ((bf16[128,8,896]{2,1,0:T(8,128)(2,1)}), bf16[128,8,896]{2,1,0:T(8,128)(2,1)S(1)}, u32[]{:S(2)}, u32[]{:S(2)}) async-start(bf16[128,8,896]{2,1,0:T(8,128)(2,1)} %bitcast.58), calls=%async_computation.3 | async-start | bytes 3670016 | tf_op jit(solution)/shard_map/all_to_all | solution.py:258
  27.0 40.1 %copy-start.9 = (s32[32]{0:T(128)}, s32[32]{0:T(128)S(1)}, u32[]{:S(2)}) copy-start(s32[32]{0:T(128)S(1)} %fusion.9.slot_ref) | copy-start | bytes 388
  46.9 14.0 %all-to-all-start.4 = ((bf16[16,8,1024]{2,1,0:T(8,128)(2,1)}), bf16[16,8,1024]{2,1,0:T(8,128)(2,1)S(1)}, u32[]{:S(2)}, u32[]{:S(2)}) async-start(bf16[16,8,1024]{2,1,0:T(8,128)(2,1)} %bitcast.15), calls=%async_computation.4 | async-start | bytes 524288 | tf_op jit(solution)/shard_map/all_to_all | solution.py:311
  60.9 13.6 %copy-start.4 = (bf16[16,8,1024]{2,1,0:T(8,128)(2,1)}, bf16[16,8,1024]{2,1,0:T(8,128)(2,1)S(1)}, u32[]{:S(2)}) copy-start(bf16[16,8,1024]{2,1,0:T(8,128)(2,1)S(1)} %all-to-all-done.4) | copy-start | bytes 786436
  60.9 191.6 %all-to-all-start.5 = ((bf16[128,8,896]{2,1,0:T(8,128)(2,1)}), bf16[128,8,896]{2,1,0:T(8,128)(2,1)}, u32[]{:S(2)}, u32[]{:S(2)}) async-start(bf16[128,8,896]{2,1,0:T(8,128)(2,1)} %bitcast.57), calls=%async_computation.5 | async-start | bytes 3670016 | tf_op jit(solution)/shard_map/all_to_all | solution.py:258
  65.3 392.0 %all-gather.2.cloned.1.call-start = ((), (), s32[]{:S(2)}) async-start(), calls=%async_computation.9 | async-start | bytes 3899392 | tf_op jit(solution)/shard_map/all_gather | solution.py:282
  67.1 18.0 %collective-permute-start.6 = (bf16[48,8,896]{2,1,0:T(8,128)(2,1)}, bf16[48,8,896]{2,1,0:T(8,128)(2,1)S(1)}, u32[]{:S(2)}, u32[]{:S(2)}) collective-permute-start(bf16[48,8,896]{2,1,0:T(8,128)(2,1)} %gather_fusion.6), channel_id=1, source_target_pairs={{0,8},{1,9},{2,10},{3,11},{4,12},{5,13},{6,14},{7,15},{8,16},{9,17... | collective-permute-start | bytes 2064392 | tf_op jit(solution)/shard_map/ppermute | solution.py:272
  70.5 64.8 %collective-permute-start.7 = (bf16[48,8,896]{2,1,0:T(8,128)(2,1)}, bf16[48,8,896]{2,1,0:T(8,128)(2,1)S(1)}, u32[]{:S(2)}, u32[]{:S(2)}) collective-permute-start(bf16[48,8,896]{2,1,0:T(8,128)(2,1)} %gather_fusion.7), channel_id=1, source_target_pairs={{0,16},{1,17},{2,18},{3,19},{4,20},{5,21},{6,22},{7,23},{8,24},{9,... | collective-permute-start | bytes 2064392 | tf_op jit(solution)/shard_map/ppermute | solution.py:272
  74.5 64.9 %collective-permute-start.8 = (bf16[48,8,896]{2,1,0:T(8,128)(2,1)}, bf16[48,8,896]{2,1,0:T(8,128)(2,1)}, u32[]{:S(2)}, u32[]{:S(2)}) collective-permute-start(bf16[48,8,896]{2,1,0:T(8,128)(2,1)} %gather_fusion.8), channel_id=1, source_target_pairs={{0,24},{1,25},{2,26},{3,27},{4,28},{5,29},{6,30},{7,31},{8,0},{9,1... | collective-permute-start | bytes 2064392 | tf_op jit(solution)/shard_map/ppermute | solution.py:272
  85.1 54.3 %copy-start.5 = (bf16[48,8,896]{2,1,0:T(8,128)(2,1)}, bf16[48,8,896]{2,1,0:T(8,128)(2,1)S(1)}, u32[]{:S(2)}) copy-start(bf16[48,8,896]{2,1,0:T(8,128)(2,1)S(1)} %collective-permute-done.6.refs_1_) | copy-start | bytes 2064388
  135.3 4.1 copy-start.6
  252.5 192.2 %all-to-all-start.6 = ((bf16[256,8,896]{2,1,0:T(8,128)(2,1)}), bf16[256,8,896]{2,1,0:T(8,128)(2,1)}, u32[]{:S(2)}, u32[]{:S(2)}) async-start(bf16[256,8,896]{2,1,0:T(8,128)(2,1)} %gather_rows.7), calls=%async_computation.6 | async-start | bytes 7340032 | tf_op jit(solution)/shard_map/all_to_all | solution.py:258
  257.4 193.2 %collective-permute-start.12 = (bf16[16,128,896]{2,1,0:T(8,128)(2,1)}, bf16[16,128,896]{2,1,0:T(8,128)(2,1)}, u32[]{:S(2)}, u32[]{:S(2)}) collective-permute-start(bf16[16,128,896]{2,1,0:T(8,128)(2,1)} %param.9), channel_id=1, source_target_pairs={{0,1},{1,0},{2,3},{3,2},{4,5},{5,4},{6,7},{7,6},{8,9},{9,8},{10,11... | collective-permute-start | bytes 11010056 | tf_op jit(solution)/shard_map/ppermute | solution.py:363
  270.6 16.6 %collective-permute-start.9 = (bf16[48,8,896]{2,1,0:T(8,128)(2,1)}, bf16[48,8,896]{2,1,0:T(8,128)(2,1)S(1)}, u32[]{:S(2)}, u32[]{:S(2)}) collective-permute-start(bf16[48,8,896]{2,1,0:T(8,128)(2,1)} %gather_fusion.2), channel_id=1, source_target_pairs={{0,8},{1,9},{2,10},{3,11},{4,12},{5,13},{6,14},{7,15},{8,16},{9,17... | collective-permute-start | bytes 2064392 | tf_op jit(solution)/shard_map/ppermute | solution.py:272
  270.6 59.0 %collective-permute-start.10 = (bf16[48,8,896]{2,1,0:T(8,128)(2,1)}, bf16[48,8,896]{2,1,0:T(8,128)(2,1)S(1)}, u32[]{:S(2)}, u32[]{:S(2)}) collective-permute-start(bf16[48,8,896]{2,1,0:T(8,128)(2,1)} %gather_fusion.3), channel_id=1, source_target_pairs={{0,16},{1,17},{2,18},{3,19},{4,20},{5,21},{6,22},{7,23},{8,24},{9,... | collective-permute-start | bytes 2064392 | tf_op jit(solution)/shard_map/ppermute | solution.py:272
  271.2 60.5 %collective-permute-start.11 = (bf16[48,8,896]{2,1,0:T(8,128)(2,1)}, bf16[48,8,896]{2,1,0:T(8,128)(2,1)}, u32[]{:S(2)}, u32[]{:S(2)}) collective-permute-start(bf16[48,8,896]{2,1,0:T(8,128)(2,1)} %gather_fusion.4), channel_id=1, source_target_pairs={{0,24},{1,25},{2,26},{3,27},{4,28},{5,29},{6,30},{7,31},{8,0},{9,1... | collective-permute-start | bytes 2064392 | tf_op jit(solution)/shard_map/ppermute | solution.py:272
  287.3 44.4 %copy-start.7 = (bf16[48,8,896]{2,1,0:T(8,128)(2,1)}, bf16[48,8,896]{2,1,0:T(8,128)(2,1)S(1)}, u32[]{:S(2)}) copy-start(bf16[48,8,896]{2,1,0:T(8,128)(2,1)S(1)} %collective-permute-done.9.refs_1_) | copy-start | bytes 2064388
  329.6 2.1 copy-start.8
  444.7 52.0 %all-to-all-start.7 = ((bf16[256,8,896]{2,1,0:T(8,128)(2,1)}), bf16[256,8,896]{2,1,0:T(8,128)(2,1)}, u32[]{:S(2)}, u32[]{:S(2)}) async-start(bf16[256,8,896]{2,1,0:T(8,128)(2,1)} %gather_rows.6), calls=%async_computation.7 | async-start | bytes 7340032 | tf_op jit(solution)/shard_map/all_to_all | solution.py:258
  496.7 63.4 %all-to-all-start.8 = ((f32[16,8,1152]{2,1,0:T(8,128)}), f32[16,8,1152]{2,1,0:T(8,128)S(1)}, u32[]{:S(2)}, u32[]{:S(2)}) async-start(f32[16,8,1152]{2,1,0:T(8,128)} %bitcast.60), calls=%async_computation.8 | async-start | bytes 1179648 | tf_op jit(solution)/shard_map/all_to_all | solution.py:377
  560.2 0.9 copy-start
Sparse Core Ops, SparseCore 0:
  76.3 88.1 all-gather.1
where the time goes:
time: 581 us; the launch traced here: 578 us
  Pallas kernels  331 us (57%)
  waiting for transfers between devices  146 us (25%)
  starting transfers between devices  45.2 us (8%)
  local copies, waits for them, and re-layouts  30.6 us (5%)
  between operations  14.3 us (2%)
  other arithmetic  11.6 us (2%)
    pallas_call x2, Pallas kernels, gather_rows(): pl.pallas_call(functools.partial(gather_body, rows=groups, copies=copies)...  226 us
    ppermute x6, waiting for transfers between devices, across(): moved.append(lax.ppermute(blocks[k], BOTH, pairs))  120 us
    pallas_call x1, Pallas kernels, even_attention(): pl.pallas_call(functools.partial(even_body, per_step=per_step, neighbours...  42.4 us
    pallas_call x1, Pallas kernels, odd_attention(): pl.pallas_call(odd_body, out_shape=jax.ShapeDtypeStruct((slots, columns +...  38.7 us
    all_to_all x4, starting transfers between devices, swap(): return lax.all_to_all(x, BOTH, 0, 0, axis_index_groups=groups, tiled=True)  18.6 us
    all_to_all x4, waiting for transfers between devices, swap(): return lax.all_to_all(x, BOTH, 0, 0, axis_index_groups=groups, tiled=True)  18.3 us
    gather x8, local copies, waits for them, and re-layouts, exact(): jnp.take(source, send_rows[k], axis=0, mode='clip')  18.1 us
    pallas_call x1, Pallas kernels, project(): pl.pallas_call(project_body, out_shape=jax.ShapeDtypeStruct((count * toke...  13.1 us
  transfers between devices with their start and end apart: 15, of which 8 were waited for; matrix products, arithmetic and copies ran while one was open for 7% of the time, Pallas kernels for 55%

commit v1 on v0

--- a/solution.py
+++ b/solution.py
@@ -104,78 +104,118 @@
     )(queries, rows, weights, *early)
 
 
-def patch_body(slot_ref, out_in_ref, odd_ref, out_ref, *, neighbours):
-    columns = out_ref.shape[1]
+def patch_body(slot_ref, out_in_ref, odd_ref, out_ref, *rest, neighbours):
+    picked_refs, row_ref = rest[:-1], rest[-1]
+    per_step, _, tail, columns = out_ref.shape
     heads = columns // DH
-    sequence = pl.program_id(0)
-    picked = [odd_ref[pl.ds(slot_ref[sequence * neighbours + j], 1), :] for j in range(neighbours)]
-    last = lax.broadcasted_iota(jnp.int32, (TAIL, DH), 0) == TAIL - 1
-    for h in range(heads):
-        lo, hi = h * DH, (h + 1) * DH
-        maxima = [p[:, columns + h : columns + h + 1] for p in picked]
-        sums = [p[:, columns + DH // 2 + h : columns + DH // 2 + h + 1] for p in picked]
-        top = functools.reduce(jnp.maximum, maxima)
-        each = [jnp.exp(m - top) for m in maxima]
-        under = sum(e * t for e, t in zip(each, sums))
-        over = sum(e * p[:, lo:hi] for e, p in zip(each, picked))
-        out_ref[:, lo:hi] = jnp.where(last, (over / under).astype(BF16), out_in_ref[:, lo:hi])
+    sequences = row_ref.shape[0]
+    step = pl.program_id(0)
+
+    @pl.when(step == 0)
+    def _():
+        for i in range(sequences):
+            for j, picked_ref in enumerate(picked_refs):
+                picked_ref[i : i + 1, :] = odd_ref[pl.ds(slot_ref[i * neighbours + j], 1), :]
+        for h in range(heads):
+            lo, hi = h * DH, (h + 1) * DH
+            maxima = [p[:, columns + h : columns + h + 1] for p in picked_refs]
+            sums = [p[:, columns + DH // 2 + h : columns + DH // 2 + h + 1] for p in picked_refs]
+            top = functools.reduce(jnp.maximum, maxima)
+            each = [jnp.exp(m - top) for m in maxima]
+            under = sum(e * t for e, t in zip(each, sums))
+            over = sum(e * p[:, lo:hi] for e, p in zip(each, picked_refs))
+            row_ref[:, lo:hi] = over / under
+
+    last = lax.broadcasted_iota(jnp.int32, (tail, columns), 0) == tail - 1
+    for i in range(per_step):
+        row = row_ref[pl.ds(step * per_step + i, 1), :]
+        out_ref[i, 0] = jnp.where(last, row, out_in_ref[i, 0].astype(F32)).astype(BF16)
 
 
 def patch(slots, out, odd):
     tokens, columns = out.shape
     sequences = tokens // SEQ
-    tail = pl.BlockSpec((TAIL, columns), lambda i, s: (i * (SEQ // TAIL) + SEQ // TAIL - 1, 0))
-    return pl.pallas_call(
-        functools.partial(patch_body, neighbours=slots.shape[0] // sequences),
-        out_shape=jax.ShapeDtypeStruct(out.shape, BF16),
+    neighbours = slots.shape[0] // sequences
+    per_step = math.gcd(sequences, 4)
+    blocks = SEQ // TAIL
+    tail = pl.BlockSpec((per_step, 1, TAIL, columns), lambda i, s: (i, blocks - 1, 0, 0))
+    shape = (sequences, blocks, TAIL, columns)
+    return pl.pallas_call(
+        functools.partial(patch_body, neighbours=neighbours),
+        out_shape=jax.ShapeDtypeStruct(shape, BF16),
         grid_spec=pltpu.PrefetchScalarGridSpec(
             num_scalar_prefetch=1,
-            grid=(sequences,),
+            grid=(sequences // per_step,),
             in_specs=[tail, pl.BlockSpec(odd.shape, lambda i, s: (0, 0))],
             out_specs=tail,
+            scratch_shapes=[pltpu.VMEM((sequences, odd.shape[1]), F32)] * neighbours
+            + [pltpu.VMEM((sequences, columns), F32)],
         ),
         input_output_aliases={1: 0},
         name="patch",
-    )(slots, out, odd)
-
-
-def gather_body(index_ref, *refs, rows, copies):
-    sources, out_ref, sem = refs[:-2], refs[-2], refs[-1]
+    )(slots, out.reshape(shape), odd).reshape(out.shape)
+
+
+def gather_body(index_ref, *refs, copies):
+    sources, out_ref = refs[:-1], refs[-1]
     size = sources[0].shape[0]
-    wanted = out_ref.shape[0] // (rows * copies)
+    wanted = out_ref.shape[0]
+    base = pl.program_id(0) // copies * wanted
 
     def step(i, carry):
-        at = index_ref[i]
-        base = i // wanted * (copies * wanted) + i % wanted
+        at = index_ref[base + i]
         for k, source in enumerate(sources):
             @pl.when((at >= k * size) & (at < (k + 1) * size))
             def _():
-                for c in range(copies):
-                    pltpu.make_async_copy(
-                        source.at[at - k * size], out_ref.at[base + c * wanted], sem
-                    ).start()
+                out_ref[i] = source[at - k * size]
 
         return carry
 
-    lax.fori_loop(0, rows * wanted, step, 0)
-    whole = out_ref.at[pl.ds(0, rows * wanted * copies)]
-    pltpu.make_async_copy(whole, whole, sem).wait()
+    lax.fori_loop(0, wanted, step, 0, unroll=4)
 
 
 def gather_rows(index, sources, groups, copies):
-    total = index.shape[0] * copies
-    return pl.pallas_call(
-        functools.partial(gather_body, rows=groups, copies=copies),
-        out_shape=jax.ShapeDtypeStruct((total,) + sources[0].shape[1:], sources[0].dtype),
+    wanted = index.shape[0] // groups
+    shape = sources[0].shape
+    whole = pl.BlockSpec(shape, lambda i, s: (0, 0, 0))
+    return pl.pallas_call(
+        functools.partial(gather_body, copies=copies),
+        out_shape=jax.ShapeDtypeStruct((index.shape[0] * copies,) + shape[1:], sources[0].dtype),
+        grid_spec=pltpu.PrefetchScalarGridSpec(
+            num_scalar_prefetch=1,
+            grid=(groups * copies,),
+            in_specs=[whole for _ in sources],
+            out_specs=pl.BlockSpec((wanted,) + shape[1:], lambda i, s: (i, 0, 0)),
+        ),
+        name="gather_rows",
+    )(index, *sources)
+
+
+def select_body(index_ref, source_ref, *out_refs):
+    fast = out_refs[0].shape[0]
+
+    def step(i, carry):
+        for k, out_ref in enumerate(out_refs):
+            out_ref[i] = source_ref[index_ref[k * fast + i]]
+        return carry
+
+    lax.fori_loop(0, fast, step, 0, unroll=2)
+
+
+def select_rows(index, source):
+    count, fast = index.shape
+    block = pl.BlockSpec((fast,) + source.shape[1:], lambda i, s: (0, 0, 0))
+    return pl.pallas_call(
+        select_body,
+        out_shape=[jax.ShapeDtypeStruct((fast,) + source.shape[1:], source.dtype)] * count,
         grid_spec=pltpu.PrefetchScalarGridSpec(
             num_scalar_prefetch=1,
             grid=(1,),
-            in_specs=[pl.BlockSpec(memory_space=pl.ANY) for _ in sources],
-            out_specs=pl.BlockSpec(memory_space=pl.ANY),
-            scratch_shapes=[pltpu.SemaphoreType.DMA],
+            in_specs=[pl.BlockSpec(source.shape, lambda i, s: (0, 0, 0))],
+            out_specs=[block] * count,
         ),
-        name="gather_rows",
-    )(index, *sources)
+        name="select_rows",
+    )(index.reshape(-1), source)
 
 
 def odd_body(query_ref, want_ref, rows_ref, weight_ref, out_ref):
@@ -338,7 +378,9 @@
     my_step = (plane_index + planes - my_ids // plane_rows) % planes
 
     def exact(source):
-        return [jnp.take(source, send_rows[k], axis=0, mode="clip") for k in range(planes)]
+        if planes > MOST_SHIFTS:
+            return [jnp.take(source, send_rows[k], axis=0, mode="clip") for k in range(planes)]
+        return select_rows(send_rows, source)
 
     def whole(source):
         return [source] * planes

time: 581 us -> 431 us (0.74)
  Pallas kernels: 331 us -> 126 us
  waiting for transfers between devices: 146 us -> 217 us
  local copies, waits for them, and re-layouts: 30.6 us -> 13.1 us
    pallas_call x3 -> x5, Pallas kernels: 236 us -> 32.2 us  [the longest x2 21.1 us: gather_rows(): pl.pallas_call(functools.partial(gather_body, copies=copies), out_shape=j...]
    ppermute x1, waiting for transfers between devices: 0.01 us -> 58.1 us  [local(): lax.ppermute(sharing, 'mp', [(m, (m + k) % parts) for m in range(parts)])]
    gather x8 -> x0, local copies, waits for them, and re-layouts: 18.1 us -> none  [exact(): jnp.take(source, send_rows[k], axis=0, mode='clip')]
    ppermute x6, waiting for transfers between devices: 120 us -> 132 us  [across(): moved.append(lax.ppermute(blocks[k], BOTH, pairs))]
  transfers between devices with their start and end apart: 15 -> 15, of which waited for: 8 -> 9; matrix products, arithmetic and copies ran while one was open for 7% -> 5% of each run, Pallas kernels for 55% -> 28%
where the time goes in v1:
time: 431 us; the launch traced here: 429 us
  waiting for transfers between devices  217 us (50%)
  Pallas kernels  126 us (29%)
  starting transfers between devices  46.7 us (11%)
  between operations  14.2 us (3%)
  local copies, waits for them, and re-layouts  13.1 us (3%)
  other arithmetic  11.6 us (3%)
    ppermute x6, waiting for transfers between devices, across(): moved.append(lax.ppermute(blocks[k], BOTH, pairs))  132 us
    ppermute x1, waiting for transfers between devices, local(): lax.ppermute(sharing, 'mp', [(m, (m + k) % parts) for m in range(parts)])  58.1 us
    pallas_call x1, Pallas kernels, even_attention(): pl.pallas_call(functools.partial(even_body, per_step=per_step, neighbours...  42.4 us
    pallas_call x1, Pallas kernels, odd_attention(): pl.pallas_call(odd_body, out_shape=jax.ShapeDtypeStruct((slots, columns +...  38.7 us
    all_to_all x4, starting transfers between devices, swap(): return lax.all_to_all(x, BOTH, 0, 0, axis_index_groups=groups, tiled=True)  22.8 us
    pallas_call x2, Pallas kernels, gather_rows(): pl.pallas_call(functools.partial(gather_body, copies=copies), out_shape=j...  21.1 us
    all_to_all x4, waiting for transfers between devices, swap(): return lax.all_to_all(x, BOTH, 0, 0, axis_index_groups=groups, tiled=True)  18.7 us
    pallas_call x1, Pallas kernels, project(): pl.pallas_call(project_body, out_shape=jax.ShapeDtypeStruct((count * toke...  13.1 us
  transfers between devices with their start and end apart: 15, of which 9 were waited for; matrix products, arithmetic and copies ran while one was open for 5% of the time, Pallas kernels for 28%

profile of v1, /device:TPU:11, one launch (start us, length us, event | category | flops | bytes accessed | tf_op | source)
XLA Modules:
  0.0 429.1 jit_solution(3264734251468897033)
XLA Ops:
  6.5 0.8 copy.58
  7.3 0.1 reshape.212
  7.4 0.8 copy.59
  8.2 0.1 reshape.213
  8.3 0.1 pad_add_fusion
  8.3 0.6 broadcast_in_dim.107
  9.0 6.5 %all-to-all-start.2 = ((s32[16,1,128]{2,1,0:T(1,128)}), s32[16,1,128]{2,1,0:T(1,128)S(1)}, u32[]{:S(2)}, u32[]{:S(2)}) async-start(s32[16,1,128]{2,1,0:T(1,128)} %broadcast_in_dim.107), calls=%async_computation.2 | async-start | bytes 16384 | tf_op jit(solution)/shard_map/all_to_all | solution.py:317
  15.5 2.6 copy.80
  18.1 2.2 fusion.16
  20.3 0.1 copy.60
  20.4 4.3 all-to-all-start.3
  24.7 1.0 slice.45
  25.8 0.1 copy.76
  25.9 0.1 copy.75
  25.9 0.1 copy.62
  26.1 0.5 convert_reduce_fusion
  26.6 0.1 select_reduce_fusion.3
  26.7 1.6 gather_fusion
  28.3 18.7 %all-to-all-done.3.source_ref = bf16[128,8,896]{2,1,0:T(8,128)(2,1)S(1)} async-done(((bf16[128,8,896]{2,1,0:T(8,128)(2,1)}), bf16[128,8,896]{2,1,0:T(8,128)(2,1)S(1)}, u32[]{:S(2)}, u32[]{:S(2)}) %all-to-all-start.3) | async-done | bytes 1835040 | tf_op jit(solution)/shard_map/all_to_all | solution.py:298
  46.9 6.0 %all-to-all-start.4 = ((bf16[16,8,1024]{2,1,0:T(8,128)(2,1)}), bf16[16,8,1024]{2,1,0:T(8,128)(2,1)S(1)}, u32[]{:S(2)}, u32[]{:S(2)}) async-start(bf16[16,8,1024]{2,1,0:T(8,128)(2,1)} %bitcast.17), calls=%async_computation.4 | async-start | bytes 524288 | tf_op jit(solution)/shard_map/all_to_all | solution.py:351
  52.9 7.9 %all-to-all-done.4 = bf16[16,8,1024]{2,1,0:T(8,128)(2,1)S(1)} async-done(((bf16[16,8,1024]{2,1,0:T(8,128)(2,1)}), bf16[16,8,1024]{2,1,0:T(8,128)(2,1)S(1)}, u32[]{:S(2)}, u32[]{:S(2)}) %all-to-all-start.4) | async-done | bytes 262176 | tf_op jit(solution)/shard_map/all_to_all | solution.py:351
  60.9 4.4 %all-to-all-start.5 = ((bf16[128,8,896]{2,1,0:T(8,128)(2,1)}), bf16[128,8,896]{2,1,0:T(8,128)(2,1)}, u32[]{:S(2)}, u32[]{:S(2)}) async-start(bf16[128,8,896]{2,1,0:T(8,128)(2,1)} %bitcast.54), calls=%async_computation.5 | async-start | bytes 3670016 | tf_op jit(solution)/shard_map/all_to_all | solution.py:298
  65.3 0.1 iota_compare_fusion.7
  65.4 0.2 copy.67
  65.5 0.1 add.128
  65.7 0.2 fusion.2
  65.9 0.1 convolution_convert_fusion
  66.1 0.1 select_reduce_fusion.1
  66.2 0.1 select_reduce_fusion.4
  66.3 0.7 reshape.220.index_ref
  67.0 2.6 select_rows.3
  69.6 1.9 collective-permute-start.6
  71.5 2.5 collective-permute-start.7
  73.9 1.7 pad_maximum_fusion.1
  75.7 0.2 select_reduce_fusion
  75.8 0.6 minimum_add_fusion
  76.4 11.9 %collective-permute-done.6.refs_1_ = bf16[48,8,896]{2,1,0:T(8,128)(2,1)S(1)} collective-permute-done((bf16[48,8,896]{2,1,0:T(8,128)(2,1)}, bf16[48,8,896]{2,1,0:T(8,128)(2,1)S(1)}, u32[]{:S(2)}, u32[]{:S(2)}) %collective-permute-start.6) | collective-permute-done | bytes 688160 | tf_op jit(solution)/shard_map/ppermute | solution.py:312
  88.4 57.2 %collective-permute-done.7.refs_2_ = bf16[48,8,896]{2,1,0:T(8,128)(2,1)S(1)} collective-permute-done((bf16[48,8,896]{2,1,0:T(8,128)(2,1)}, bf16[48,8,896]{2,1,0:T(8,128)(2,1)S(1)}, u32[]{:S(2)}, u32[]{:S(2)}) %collective-permute-start.7) | collective-permute-done | bytes 688160 | tf_op jit(solution)/shard_map/ppermute | solution.py:312
  145.6 4.2 collective-permute-done.8.refs_3_
  149.8 10.5 %gather_rows.7 = bf16[256,8,896]{2,1,0:T(8,128)(2,1)} custom-call(s32[128]{0:T(128)} %get-tuple-element.74.index_ref, bf16[48,8,896]{2,1,0:T(8,128)(2,1)} %get-tuple-element.61.refs_0_, bf16[48,8,896]{2,1,0:T(8,128)(2,1)} %copy-done.5, bf16[48,8,896]{2,1,0:T(8,128)(2,1)} %copy-done.6, bf16[48,8,896]{2,1,0:T(8,128)(2,1)} %collective-permute-done.8.refs_3_), custom_call_target="tpu_custom_call" | custom-call | tf_op jit(solution)/shard_map/gather_rows/pallas_call | solution.py:181
  160.4 8.9 %all-to-all-start.6 = ((bf16[256,8,896]{2,1,0:T(8,128)(2,1)}), bf16[256,8,896]{2,1,0:T(8,128)(2,1)}, u32[]{:S(2)}, u32[]{:S(2)}) async-start(bf16[256,8,896]{2,1,0:T(8,128)(2,1)} %gather_rows.7), calls=%async_computation.6 | async-start | bytes 7340032 | tf_op jit(solution)/shard_map/all_to_all | solution.py:298
  169.3 1.2 collective-permute-start.12
  170.4 4.1 select_rows.2
  174.6 1.5 collective-permute-start.11
  176.0 15.1 %collective-permute-done.9.refs_1_ = bf16[48,8,896]{2,1,0:T(8,128)(2,1)S(1)} collective-permute-done((bf16[48,8,896]{2,1,0:T(8,128)(2,1)}, bf16[48,8,896]{2,1,0:T(8,128)(2,1)S(1)}, u32[]{:S(2)}, u32[]{:S(2)}) %collective-permute-start.9) | collective-permute-done | bytes 688160 | tf_op jit(solution)/shard_map/ppermute | solution.py:312
  191.1 42.3 %collective-permute-done.10.refs_2_ = bf16[48,8,896]{2,1,0:T(8,128)(2,1)S(1)} collective-permute-done((bf16[48,8,896]{2,1,0:T(8,128)(2,1)}, bf16[48,8,896]{2,1,0:T(8,128)(2,1)S(1)}, u32[]{:S(2)}, u32[]{:S(2)}) %collective-permute-start.10) | collective-permute-done | bytes 688160 | tf_op jit(solution)/shard_map/ppermute | solution.py:312
  233.5 1.4 collective-permute-done.11.refs_3_
  234.9 10.5 %gather_rows.6 = bf16[256,8,896]{2,1,0:T(8,128)(2,1)} custom-call(s32[128]{0:T(128)} %get-tuple-element.74.index_ref, bf16[48,8,896]{2,1,0:T(8,128)(2,1)} %get-tuple-element.65.refs_0_, bf16[48,8,896]{2,1,0:T(8,128)(2,1)} %copy-done.7, bf16[48,8,896]{2,1,0:T(8,128)(2,1)} %copy-done.8, bf16[48,8,896]{2,1,0:T(8,128)(2,1)} %collective-permute-done.11.refs_3_), custom_call_target="tpu_custom_call" | custom-call | tf_op jit(solution)/shard_map/gather_rows/pallas_call | solution.py:181
  245.5 5.3 %all-to-all-start.7 = ((bf16[256,8,896]{2,1,0:T(8,128)(2,1)}), bf16[256,8,896]{2,1,0:T(8,128)(2,1)}, u32[]{:S(2)}, u32[]{:S(2)}) async-start(bf16[256,8,896]{2,1,0:T(8,128)(2,1)} %gather_rows.6), calls=%async_computation.7 | async-start | bytes 7340032 | tf_op jit(solution)/shard_map/all_to_all | solution.py:298
  250.7 0.1 copy.73
  250.9 0.1 copy.72
  251.0 0.4 select_reduce_fusion.2
  251.3 0.1 sub.50
  251.4 58.1 %collective-permute-done.12 = bf16[16,128,896]{2,1,0:T(8,128)(2,1)} collective-permute-done((bf16[16,128,896]{2,1,0:T(8,128)(2,1)}, bf16[16,128,896]{2,1,0:T(8,128)(2,1)}, u32[]{:S(2)}, u32[]{:S(2)}) %collective-permute-start.12) | collective-permute-done | bytes 3670048 | tf_op jit(solution)/shard_map/ppermute | solution.py:405
  309.6 6.8 %pad_maximum_fusion.rows_ref = bf16[32,128,896]{2,1,0:T(8,128)(2,1)} fusion(bf16[16,128,896]{2,1,0:T(8,128)(2,1)} %collective-permute-done.12, bf16[16,128,896]{2,1,0:T(8,128)(2,1)} %param.9), kind=kLoop, calls=%fused_computation.6 | loop fusion | flops 3670016 | bytes 14680064 | tf_op jit(solution)/shard_map/concatenate | solution.py:406
  316.4 0.7 broadcast_in_dim.121.want_ref
  317.1 38.7 %odd_attention.1 = f32[128,1152]{1,0:T(8,128)} custom-call(bf16[128,1024]{1,0:T(8,128)(2,1)} %bitcast.58, s32[128,128]{1,0:T(8,128)} %broadcast_in_dim.121.want_ref, bf16[32,128,896]{2,1,0:T(8,128)(2,1)} %pad_maximum_fusion.rows_ref, bf16[896,2048]{1,0:T(8,128)(2,1)} %all-gather.2.cloned.1.call-done.weight_ref), custom_call_target="tpu_custom_call" | custom-call | tf_op jit(solution)/shard_map/odd_attention/pallas_call | solution.py:260
  355.7 4.3 %all-to-all-start.8 = ((f32[16,8,1152]{2,1,0:T(8,128)}), f32[16,8,1152]{2,1,0:T(8,128)S(1)}, u32[]{:S(2)}, u32[]{:S(2)}) async-start(f32[16,8,1152]{2,1,0:T(8,128)} %bitcast.57), calls=%async_computation.8 | async-start | bytes 1179648 | tf_op jit(solution)/shard_map/all_to_all | solution.py:419
  360.1 0.1 convert_reduce_fusion.1
  360.2 0.6 reduce_max.9
  361.5 13.1 %project.3.refs_0_ = bf16[2048,2048]{1,0:T(8,128)(2,1)} custom-call(bf16[8,32,8,896]{3,2,1,0:T(8,128)(2,1)} %bitcast.25.rows_ref, bf16[896,2048]{1,0:T(8,128)(2,1)} %all-gather.2.cloned.1.call-done.weight_ref), custom_call_target="tpu_custom_call" | custom-call | tf_op jit(solution)/shard_map/project/pallas_call | solution.py:38
  374.6 42.4 %even_attention.3 = bf16[2048,1024]{1,0:T(8,128)(2,1)} custom-call(bf16[2048,1024]{1,0:T(8,128)(2,1)} %query_ref.1, bf16[8,32,8,896]{3,2,1,0:T(8,128)(2,1)} %bitcast.24.rows_ref, bf16[896,2048]{1,0:T(8,128)(2,1)} %all-gather.2.cloned.1.call-done.weight_ref, bf16[2048,2048]{1,0:T(8,128)(2,1)} %project.3.refs_0_), custom_call_target="tpu_custom_call" | custom-call | tf_op jit(solution)/shard_map/even_attention/pallas_call | solution.py:92
  417.1 0.8 copy-done
  417.9 4.4 %patch.1 = bf16[16,8,16,1024]{3,2,1,0:T(8,128)(2,1)} custom-call(s32[32]{0:T(128)} %copy-done.9, bf16[16,8,16,1024]{3,2,1,0:T(8,128)(2,1)} %get-tuple-element.83.out_in_ref, f32[128,1152]{1,0:T(8,128)} %bitcast.56), custom_call_target="tpu_custom_call", output_to_operand_aliasing={{}: (1, {})} | custom-call | tf_op jit(solution)/shard_map/patch/pallas_call | solution.py:143
  (43 shorter events, 0.4 us)
Async XLA Ops:
  9.0 11.3 %all-to-all-start.2 = ((s32[16,1,128]{2,1,0:T(1,128)}), s32[16,1,128]{2,1,0:T(1,128)S(1)}, u32[]{:S(2)}, u32[]{:S(2)}) async-start(s32[16,1,128]{2,1,0:T(1,128)} %broadcast_in_dim.107), calls=%async_computation.2 | async-start | bytes 16384 | tf_op jit(solution)/shard_map/all_to_all | solution.py:317
  20.4 26.5 %all-to-all-start.3 = ((bf16[128,8,896]{2,1,0:T(8,128)(2,1)}), bf16[128,8,896]{2,1,0:T(8,128)(2,1)S(1)}, u32[]{:S(2)}, u32[]{:S(2)}) async-start(bf16[128,8,896]{2,1,0:T(8,128)(2,1)} %bitcast.55), calls=%async_computation.3 | async-start | bytes 3670016 | tf_op jit(solution)/shard_map/all_to_all | solution.py:298
  26.6 43.0 %copy-start.9 = (s32[32]{0:T(128)}, s32[32]{0:T(128)S(1)}, u32[]{:S(2)}) copy-start(s32[32]{0:T(128)S(1)} %fusion.9.slot_ref) | copy-start | bytes 388
  46.9 14.0 %all-to-all-start.4 = ((bf16[16,8,1024]{2,1,0:T(8,128)(2,1)}), bf16[16,8,1024]{2,1,0:T(8,128)(2,1)S(1)}, u32[]{:S(2)}, u32[]{:S(2)}) async-start(bf16[16,8,1024]{2,1,0:T(8,128)(2,1)} %bitcast.17), calls=%async_computation.4 | async-start | bytes 524288 | tf_op jit(solution)/shard_map/all_to_all | solution.py:351
  60.9 99.5 %copy-start.4 = (bf16[16,8,1024]{2,1,0:T(8,128)(2,1)}, bf16[16,8,1024]{2,1,0:T(8,128)(2,1)S(1)}, u32[]{:S(2)}) copy-start(bf16[16,8,1024]{2,1,0:T(8,128)(2,1)S(1)} %all-to-all-done.4) | copy-start | bytes 786436
  60.9 99.5 %all-to-all-start.5 = ((bf16[128,8,896]{2,1,0:T(8,128)(2,1)}), bf16[128,8,896]{2,1,0:T(8,128)(2,1)}, u32[]{:S(2)}, u32[]{:S(2)}) async-start(bf16[128,8,896]{2,1,0:T(8,128)(2,1)} %bitcast.54), calls=%async_computation.5 | async-start | bytes 3670016 | tf_op jit(solution)/shard_map/all_to_all | solution.py:298
  65.3 251.1 %all-gather.2.cloned.1.call-start = ((), (), s32[]{:S(2)}) async-start(), calls=%async_computation.9 | async-start | bytes 3899392 | tf_op jit(solution)/shard_map/all_gather | solution.py:322
  69.6 18.8 %collective-permute-start.6 = (bf16[48,8,896]{2,1,0:T(8,128)(2,1)}, bf16[48,8,896]{2,1,0:T(8,128)(2,1)S(1)}, u32[]{:S(2)}, u32[]{:S(2)}) collective-permute-start(bf16[48,8,896]{2,1,0:T(8,128)(2,1)} %get-tuple-element.62), channel_id=1, source_target_pairs={{0,8},{1,9},{2,10},{3,11},{4,12},{5,13},{6,14},{7,15},{8,16},{9,17... | collective-permute-start | bytes 2064392 | tf_op jit(solution)/shard_map/ppermute | solution.py:312
  71.5 74.1 %collective-permute-start.7 = (bf16[48,8,896]{2,1,0:T(8,128)(2,1)}, bf16[48,8,896]{2,1,0:T(8,128)(2,1)S(1)}, u32[]{:S(2)}, u32[]{:S(2)}) collective-permute-start(bf16[48,8,896]{2,1,0:T(8,128)(2,1)} %get-tuple-element.63), channel_id=1, source_target_pairs={{0,16},{1,17},{2,18},{3,19},{4,20},{5,21},{6,22},{7,23},{8,24},{9,... | collective-permute-start | bytes 2064392 | tf_op jit(solution)/shard_map/ppermute | solution.py:312
  73.9 75.9 %collective-permute-start.8 = (bf16[48,8,896]{2,1,0:T(8,128)(2,1)}, bf16[48,8,896]{2,1,0:T(8,128)(2,1)}, u32[]{:S(2)}, u32[]{:S(2)}) collective-permute-start(bf16[48,8,896]{2,1,0:T(8,128)(2,1)} %get-tuple-element.64), channel_id=1, source_target_pairs={{0,24},{1,25},{2,26},{3,27},{4,28},{5,29},{6,30},{7,31},{8,0},{9,1... | collective-permute-start | bytes 2064392 | tf_op jit(solution)/shard_map/ppermute | solution.py:312
  88.4 61.4 %copy-start.5 = (bf16[48,8,896]{2,1,0:T(8,128)(2,1)}, bf16[48,8,896]{2,1,0:T(8,128)(2,1)S(1)}, u32[]{:S(2)}) copy-start(bf16[48,8,896]{2,1,0:T(8,128)(2,1)S(1)} %collective-permute-done.6.refs_1_) | copy-start | bytes 2064388
  145.6 4.2 copy-start.6
  160.4 85.1 %all-to-all-start.6 = ((bf16[256,8,896]{2,1,0:T(8,128)(2,1)}), bf16[256,8,896]{2,1,0:T(8,128)(2,1)}, u32[]{:S(2)}, u32[]{:S(2)}) async-start(bf16[256,8,896]{2,1,0:T(8,128)(2,1)} %gather_rows.7), calls=%async_computation.6 | async-start | bytes 7340032 | tf_op jit(solution)/shard_map/all_to_all | solution.py:298
  169.3 140.3 %collective-permute-start.12 = (bf16[16,128,896]{2,1,0:T(8,128)(2,1)}, bf16[16,128,896]{2,1,0:T(8,128)(2,1)}, u32[]{:S(2)}, u32[]{:S(2)}) collective-permute-start(bf16[16,128,896]{2,1,0:T(8,128)(2,1)} %param.9), channel_id=1, source_target_pairs={{0,1},{1,0},{2,3},{3,2},{4,5},{5,4},{6,7},{7,6},{8,9},{9,8},{10,11... | collective-permute-start | bytes 11010056 | tf_op jit(solution)/shard_map/ppermute | solution.py:405
  174.5 16.6 %collective-permute-start.9 = (bf16[48,8,896]{2,1,0:T(8,128)(2,1)}, bf16[48,8,896]{2,1,0:T(8,128)(2,1)S(1)}, u32[]{:S(2)}, u32[]{:S(2)}) collective-permute-start(bf16[48,8,896]{2,1,0:T(8,128)(2,1)} %get-tuple-element.66), channel_id=1, source_target_pairs={{0,8},{1,9},{2,10},{3,11},{4,12},{5,13},{6,14},{7,15},{8,16},{9,17... | collective-permute-start | bytes 2064392 | tf_op jit(solution)/shard_map/ppermute | solution.py:312
  174.6 58.9 %collective-permute-start.10 = (bf16[48,8,896]{2,1,0:T(8,128)(2,1)}, bf16[48,8,896]{2,1,0:T(8,128)(2,1)S(1)}, u32[]{:S(2)}, u32[]{:S(2)}) collective-permute-start(bf16[48,8,896]{2,1,0:T(8,128)(2,1)} %get-tuple-element.67), channel_id=1, source_target_pairs={{0,16},{1,17},{2,18},{3,19},{4,20},{5,21},{6,22},{7,23},{8,24},{9,... | collective-permute-start | bytes 2064392 | tf_op jit(solution)/shard_map/ppermute | solution.py:312
  174.6 60.4 %collective-permute-start.11 = (bf16[48,8,896]{2,1,0:T(8,128)(2,1)}, bf16[48,8,896]{2,1,0:T(8,128)(2,1)}, u32[]{:S(2)}, u32[]{:S(2)}) collective-permute-start(bf16[48,8,896]{2,1,0:T(8,128)(2,1)} %get-tuple-element.68), channel_id=1, source_target_pairs={{0,24},{1,25},{2,26},{3,27},{4,28},{5,29},{6,30},{7,31},{8,0},{9,1... | collective-permute-start | bytes 2064392 | tf_op jit(solution)/shard_map/ppermute | solution.py:312
  191.1 43.8 %copy-start.7 = (bf16[48,8,896]{2,1,0:T(8,128)(2,1)}, bf16[48,8,896]{2,1,0:T(8,128)(2,1)S(1)}, u32[]{:S(2)}) copy-start(bf16[48,8,896]{2,1,0:T(8,128)(2,1)S(1)} %collective-permute-done.9.refs_1_) | copy-start | bytes 2064388
  233.5 1.4 copy-start.8
  245.5 110.3 %all-to-all-start.7 = ((bf16[256,8,896]{2,1,0:T(8,128)(2,1)}), bf16[256,8,896]{2,1,0:T(8,128)(2,1)}, u32[]{:S(2)}, u32[]{:S(2)}) async-start(bf16[256,8,896]{2,1,0:T(8,128)(2,1)} %gather_rows.6), calls=%async_computation.7 | async-start | bytes 7340032 | tf_op jit(solution)/shard_map/all_to_all | solution.py:298
  355.7 61.3 %all-to-all-start.8 = ((f32[16,8,1152]{2,1,0:T(8,128)}), f32[16,8,1152]{2,1,0:T(8,128)S(1)}, u32[]{:S(2)}, u32[]{:S(2)}) async-start(f32[16,8,1152]{2,1,0:T(8,128)} %bitcast.57), calls=%async_computation.8 | async-start | bytes 1179648 | tf_op jit(solution)/shard_map/all_to_all | solution.py:419
  417.1 0.9 copy-start
Sparse Core Ops, SparseCore 0:
  75.7 81.8 all-gather.1

commit v2 on v1

--- a/solution.py
+++ b/solution.py
@@ -156,39 +156,51 @@
     )(slots, out.reshape(shape), odd).reshape(out.shape)
 
 
-def gather_body(index_ref, *refs, copies):
-    sources, out_ref = refs[:-1], refs[-1]
+def gather_body(index_ref, *refs, count):
+    sources, out_ref, stage_ref, sem_ref = refs[:count], refs[count], refs[count + 1], refs[count + 2]
     size = sources[0].shape[0]
-    wanted = out_ref.shape[0]
-    base = pl.program_id(0) // copies * wanted
+    copies, wanted = out_ref.shape[1:3]
+    base = pl.program_id(0) * wanted
+
+    @pl.when(pl.program_id(0) == 0)
+    def _():
+        moves = [
+            pltpu.make_async_copy(source, stage_ref.at[pl.ds(k * size, size)], sem_ref.at[k])
+            for k, source in enumerate(sources)
+        ]
+        for move in moves:
+            move.start()
+        for move in moves:
+            move.wait()
 
     def step(i, carry):
-        at = index_ref[base + i]
-        for k, source in enumerate(sources):
-            @pl.when((at >= k * size) & (at < (k + 1) * size))
-            def _():
-                out_ref[i] = source[at - k * size]
-
+        row = stage_ref[index_ref[base + i]]
+        for c in range(copies):
+            out_ref[0, c, i] = row
         return carry
 
-    lax.fori_loop(0, wanted, step, 0, unroll=4)
+    lax.fori_loop(0, wanted, step, 0, unroll=8)
 
 
 def gather_rows(index, sources, groups, copies):
     wanted = index.shape[0] // groups
-    shape = sources[0].shape
-    whole = pl.BlockSpec(shape, lambda i, s: (0, 0, 0))
-    return pl.pallas_call(
-        functools.partial(gather_body, copies=copies),
-        out_shape=jax.ShapeDtypeStruct((index.shape[0] * copies,) + shape[1:], sources[0].dtype),
+    size, piece, width = sources[0].shape
+    out = pl.pallas_call(
+        functools.partial(gather_body, count=len(sources)),
+        out_shape=jax.ShapeDtypeStruct((groups, copies, wanted, piece, width), sources[0].dtype),
         grid_spec=pltpu.PrefetchScalarGridSpec(
             num_scalar_prefetch=1,
-            grid=(groups * copies,),
-            in_specs=[whole for _ in sources],
-            out_specs=pl.BlockSpec((wanted,) + shape[1:], lambda i, s: (i, 0, 0)),
+            grid=(groups,),
+            in_specs=[pl.BlockSpec(memory_space=pl.ANY) for _ in sources],
+            out_specs=pl.BlockSpec((1, copies, wanted, piece, width), lambda i, s: (i, 0, 0, 0, 0)),
+            scratch_shapes=[
+                pltpu.VMEM((len(sources) * size, piece, width), sources[0].dtype),
+                pltpu.SemaphoreType.DMA((len(sources),)),
+            ],
         ),
         name="gather_rows",
     )(index, *sources)
+    return out.reshape(groups * copies * wanted, piece, width)
 
 
 def select_body(index_ref, source_ref, *out_refs):
@@ -330,7 +342,8 @@
         sending, _ = lax.optimization_barrier((pieces[chunk].reshape(lanes * held, piece, width), after))
         plane_pieces.append(swap(sending, plane_groups))
 
-    spread(0, table)
+    for chunk in range(CHUNKS):
+        spread(chunk, plane_pieces[-1] if chunk else table)
 
     odd_shard = table_shard[:, :, 1].reshape(shards, wanted)
     odd_row = table_row[:, :, 1].reshape(shards, wanted)
@@ -347,12 +360,9 @@
     sender = jnp.sum(jnp.where(chosen, (earlier // neighbours).astype(jnp.int32)[None, :], 0), axis=1)
     last_rows = queries.reshape(sequences, SEQ, columns)[:, SEQ - 1]
     odd_query = jnp.take(last_rows, sender, axis=0, mode="clip").reshape(shards, capacity, columns)
-    odd_query, _ = lax.optimization_barrier((odd_query, plane_pieces[0]))
+    odd_query, _ = lax.optimization_barrier((odd_query, plane_pieces[-1]))
     odd_query = lax.all_to_all(odd_query, "db", 0, 0, tiled=True)
     odd_query = odd_query.reshape(shards * capacity, columns)
-
-    for chunk in range(1, CHUNKS):
-        spread(chunk, odd_query if chunk == 1 else plane_pieces[-1])
 
     even_id = (table_shard[:, :, 0] * shard_rows + table_row[:, :, 0]).reshape(planes, group * wanted)
     ids = jnp.arange(planes * plane_rows, dtype=jnp.int32)
@@ -393,13 +403,12 @@
                 sending, _ = lax.optimization_barrier((sending, received[-1]))
             received.append(across(sending))
             outgoing = gather_rows(index, received[-1], group, parts)
-            if arrived:
-                outgoing, _ = lax.optimization_barrier((outgoing, arrived[-1]))
+            outgoing, _ = lax.optimization_barrier((outgoing, arrived[-1] if arrived else odd_query))
             arrived.append(swap(outgoing, plane_groups))
         return [a.reshape(lanes, wanted, piece, width) for a in arrived]
 
     part_index = lax.axis_index("mp")
-    sharing, _ = lax.optimization_barrier((encodings, plane_pieces[0]))
+    sharing, _ = lax.optimization_barrier((encodings, plane_pieces[-1]))
     shared = [encodings]
     for k in range(1, parts):
         shared.append(lax.ppermute(sharing, "mp", [(m, (m + k) % parts) for m in range(parts)]))

time: 431 us -> 409 us (0.949)
  Pallas kernels: 126 us -> 115 us
  waiting for transfers between devices: 217 us -> 207 us
    ppermute x6, waiting for transfers between devices: 132 us -> 102 us  [across(): moved.append(lax.ppermute(blocks[k], BOTH, pairs))]
    all_to_all x4, waiting for transfers between devices: 18.7 us -> 42.4 us  [swap(): return lax.all_to_all(x, BOTH, 0, 0, axis_index_groups=groups, tiled=True)]
    pallas_call x2, Pallas kernels: 21.1 us -> 9.51 us  [gather_rows(): pl.pallas_call(functools.partial(gather_body, count=len(sources)), out_sh...]
    all_to_all x1, waiting for transfers between devices: 7.94 us -> 0.01 us  [local(): odd_query = lax.all_to_all(odd_query, 'db', 0, 0, tiled=True)]
    ppermute x1, waiting for transfers between devices: 58.1 us -> 62.4 us  [local(): lax.ppermute(sharing, 'mp', [(m, (m + k) % parts) for m in range(parts)])]
  transfers between devices with their start and end apart: 15 -> 15, of which waited for: 9 -> 8; matrix products, arithmetic and copies ran while one was open for 5% -> 5% of each run, Pallas kernels for 28% -> 27%
where the time goes in v2:
time: 409 us; the launch traced here: 408 us
  waiting for transfers between devices  207 us (51%)
  Pallas kernels  115 us (28%)
  starting transfers between devices  46.8 us (11%)
  between operations  14.3 us (3%)
  local copies, waits for them, and re-layouts  13.8 us (3%)
  other arithmetic  10.7 us (3%)
    ppermute x6, waiting for transfers between devices, across(): moved.append(lax.ppermute(blocks[k], BOTH, pairs))  102 us
    ppermute x1, waiting for transfers between devices, local(): lax.ppermute(sharing, 'mp', [(m, (m + k) % parts) for m in range(parts)])  62.4 us
    all_to_all x4, waiting for transfers between devices, swap(): return lax.all_to_all(x, BOTH, 0, 0, axis_index_groups=groups, tiled=True)  42.4 us
    pallas_call x1, Pallas kernels, even_attention(): pl.pallas_call(functools.partial(even_body, per_step=per_step, neighbours...  42.4 us
    pallas_call x1, Pallas kernels, odd_attention(): pl.pallas_call(odd_body, out_shape=jax.ShapeDtypeStruct((slots, columns +...  38.7 us
    all_to_all x4, starting transfers between devices, swap(): return lax.all_to_all(x, BOTH, 0, 0, axis_index_groups=groups, tiled=True)  20.5 us
    pallas_call x1, Pallas kernels, project(): pl.pallas_call(project_body, out_shape=jax.ShapeDtypeStruct((count * toke...  13.1 us
    pallas_call x2, Pallas kernels, gather_rows(): pl.pallas_call(functools.partial(gather_body, count=len(sources)), out_sh...  9.51 us
  transfers between devices with their start and end apart: 15, of which 8 were waited for; matrix products, arithmetic and copies ran while one was open for 5% of the time, Pallas kernels for 27%

profile of v2, /device:TPU:11, one launch (start us, length us, event | category | flops | bytes accessed | tf_op | source)
XLA Modules:
  0.0 407.6 jit_solution(5214307214752018758)
XLA Ops:
  6.5 0.8 copy.58
  7.3 0.1 reshape.224
  7.4 0.8 copy.59
  8.2 0.1 reshape.225
  8.3 0.1 pad_add_fusion
  8.3 0.6 broadcast_in_dim.107
  9.0 6.5 %all-to-all-start.2 = ((s32[16,1,128]{2,1,0:T(1,128)}), s32[16,1,128]{2,1,0:T(1,128)S(1)}, u32[]{:S(2)}, u32[]{:S(2)}) async-start(s32[16,1,128]{2,1,0:T(1,128)} %broadcast_in_dim.107), calls=%async_computation.2 | async-start | bytes 16384 | tf_op jit(solution)/shard_map/all_to_all | solution.py:329
  15.5 2.6 copy.80
  18.1 2.2 fusion.16
  20.3 0.1 copy.60
  20.4 4.3 %all-to-all-start.3 = ((bf16[128,8,896]{2,1,0:T(8,128)(2,1)}), bf16[128,8,896]{2,1,0:T(8,128)(2,1)S(1)}, u32[]{:S(2)}, u32[]{:S(2)}) async-start(bf16[128,8,896]{2,1,0:T(8,128)(2,1)} %bitcast.63), calls=%async_computation.3 | async-start | bytes 3670016 | tf_op jit(solution)/shard_map/all_to_all | solution.py:310
  24.7 0.7 pad_maximum_fusion.1
  25.4 1.0 slice.45
  26.6 21.7 %all-to-all-done.3.source_ref = bf16[128,8,896]{2,1,0:T(8,128)(2,1)S(1)} async-done(((bf16[128,8,896]{2,1,0:T(8,128)(2,1)}), bf16[128,8,896]{2,1,0:T(8,128)(2,1)S(1)}, u32[]{:S(2)}, u32[]{:S(2)}) %all-to-all-start.3) | async-done | bytes 1835040 | tf_op jit(solution)/shard_map/all_to_all | solution.py:310
  48.3 6.0 %all-to-all-start.4 = ((bf16[128,8,896]{2,1,0:T(8,128)(2,1)}), bf16[128,8,896]{2,1,0:T(8,128)(2,1)}, u32[]{:S(2)}, u32[]{:S(2)}) async-start(bf16[128,8,896]{2,1,0:T(8,128)(2,1)} %bitcast.62), calls=%async_computation.4 | async-start | bytes 3670016 | tf_op jit(solution)/shard_map/all_to_all | solution.py:310
  54.3 0.1 copy.76
  54.4 0.1 copy.75
  54.5 0.1 copy.62
  54.6 0.2 copy.67
  54.8 0.1 add.128
  55.0 0.2 fusion.2
  55.2 0.1 convolution_convert_fusion
  55.4 0.1 select_reduce_fusion.1
  55.5 0.1 select_reduce_fusion.4
  55.6 0.7 reshape.229.index_ref
  56.3 0.5 convert_reduce_fusion
  56.8 2.5 select_rows.3
  59.4 1.2 collective-permute-start.6
  60.5 2.1 collective-permute-start.7
  62.6 0.3 collective-permute-start.8
  62.9 0.1 select_reduce_fusion.3
  63.0 1.5 gather_fusion
  64.5 20.7 %all-to-all-done.4.source_ref = bf16[128,8,896]{2,1,0:T(8,128)(2,1)} async-done(((bf16[128,8,896]{2,1,0:T(8,128)(2,1)}), bf16[128,8,896]{2,1,0:T(8,128)(2,1)}, u32[]{:S(2)}, u32[]{:S(2)}) %all-to-all-start.4) | async-done | bytes 1835040 | tf_op jit(solution)/shard_map/all_to_all | solution.py:310
  85.3 6.4 %all-to-all-start.5 = ((bf16[16,8,1024]{2,1,0:T(8,128)(2,1)}), bf16[16,8,1024]{2,1,0:T(8,128)(2,1)S(1)}, u32[]{:S(2)}, u32[]{:S(2)}) async-start(bf16[16,8,1024]{2,1,0:T(8,128)(2,1)} %bitcast.26), calls=%async_computation.5 | async-start | bytes 524288 | tf_op jit(solution)/shard_map/all_to_all | solution.py:364
  91.7 0.2 select_reduce_fusion
  91.9 0.6 minimum_add_fusion
  92.5 41.2 %collective-permute-done.7.refs_2_ = bf16[48,8,896]{2,1,0:T(8,128)(2,1)S(1)} collective-permute-done((bf16[48,8,896]{2,1,0:T(8,128)(2,1)}, bf16[48,8,896]{2,1,0:T(8,128)(2,1)S(1)}, u32[]{:S(2)}, u32[]{:S(2)}) %collective-permute-start.7) | collective-permute-done | bytes 688160 | tf_op jit(solution)/shard_map/ppermute | solution.py:324
  133.7 2.1 collective-permute-done.8.refs_3_
  135.8 4.8 %gather_rows.7 = bf16[4,2,32,8,896]{4,3,2,1,0:T(8,128)(2,1)} custom-call(s32[128]{0:T(128)} %get-tuple-element.77.index_ref, bf16[48,8,896]{2,1,0:T(8,128)(2,1)} %get-tuple-element.62.refs_0_, bf16[48,8,896]{2,1,0:T(8,128)(2,1)} %copy-done.5, bf16[48,8,896]{2,1,0:T(8,128)(2,1)} %copy-done.6, bf16[48,8,896]{2,1,0:T(8,128)(2,1)} %collective-permute-done.8.refs_3_), custom_call_target="tpu_custom_call" | custom-call | tf_op jit(solution)/shard_map/gather_rows/pallas_call | solution.py:188
  140.6 0.7 copy-done.4
  141.3 5.2 %all-to-all-start.6 = ((bf16[256,8,896]{2,1,0:T(8,128)(2,1)}), bf16[256,8,896]{2,1,0:T(8,128)(2,1)}, u32[]{:S(2)}, u32[]{:S(2)}) async-start(bf16[256,8,896]{2,1,0:T(8,128)(2,1)} %bitcast.58), calls=%async_computation.6 | async-start | bytes 7340032 | tf_op jit(solution)/shard_map/all_to_all | solution.py:310
  146.5 1.2 collective-permute-start.12
  147.7 4.1 %select_rows.2 = (bf16[48,8,896]{2,1,0:T(8,128)(2,1)}, bf16[48,8,896]{2,1,0:T(8,128)(2,1)}, bf16[48,8,896]{2,1,0:T(8,128)(2,1)}, bf16[48,8,896]{2,1,0:T(8,128)(2,1)}) custom-call(s32[192]{0:T(256)} %reshape.229.index_ref, bf16[128,8,896]{2,1,0:T(8,128)(2,1)} %all-to-all-done.4.source_ref), custom_call_target="tpu_custom_call" | custom-call | tf_op jit(solution)/shard_map/select_rows/pallas_call | solution.py:220
  151.8 1.6 collective-permute-start.10
  153.3 1.5 collective-permute-start.11
  154.8 13.6 %collective-permute-done.9.refs_1_ = bf16[48,8,896]{2,1,0:T(8,128)(2,1)S(1)} collective-permute-done((bf16[48,8,896]{2,1,0:T(8,128)(2,1)}, bf16[48,8,896]{2,1,0:T(8,128)(2,1)S(1)}, u32[]{:S(2)}, u32[]{:S(2)}) %collective-permute-start.9) | collective-permute-done | bytes 688160 | tf_op jit(solution)/shard_map/ppermute | solution.py:324
  168.4 42.3 %collective-permute-done.10.refs_2_ = bf16[48,8,896]{2,1,0:T(8,128)(2,1)S(1)} collective-permute-done((bf16[48,8,896]{2,1,0:T(8,128)(2,1)}, bf16[48,8,896]{2,1,0:T(8,128)(2,1)S(1)}, u32[]{:S(2)}, u32[]{:S(2)}) %collective-permute-start.10) | collective-permute-done | bytes 688160 | tf_op jit(solution)/shard_map/ppermute | solution.py:324
  210.7 3.1 collective-permute-done.11.refs_3_
  213.8 4.7 %gather_rows.6 = bf16[4,2,32,8,896]{4,3,2,1,0:T(8,128)(2,1)} custom-call(s32[128]{0:T(128)} %get-tuple-element.77.index_ref, bf16[48,8,896]{2,1,0:T(8,128)(2,1)} %get-tuple-element.66.refs_0_, bf16[48,8,896]{2,1,0:T(8,128)(2,1)} %copy-done.7, bf16[48,8,896]{2,1,0:T(8,128)(2,1)} %copy-done.8, bf16[48,8,896]{2,1,0:T(8,128)(2,1)} %collective-permute-done.11.refs_3_), custom_call_target="tpu_custom_call" | custom-call | tf_op jit(solution)/shard_map/gather_rows/pallas_call | solution.py:188
  218.6 5.0 %all-to-all-start.7 = ((bf16[256,8,896]{2,1,0:T(8,128)(2,1)}), bf16[256,8,896]{2,1,0:T(8,128)(2,1)}, u32[]{:S(2)}, u32[]{:S(2)}) async-start(bf16[256,8,896]{2,1,0:T(8,128)(2,1)} %bitcast.57), calls=%async_computation.7 | async-start | bytes 7340032 | tf_op jit(solution)/shard_map/all_to_all | solution.py:310
  223.8 0.1 copy.72
  223.9 0.4 select_reduce_fusion.2
  224.2 0.1 sub.50
  224.3 62.4 %collective-permute-done.12 = bf16[16,128,896]{2,1,0:T(8,128)(2,1)} collective-permute-done((bf16[16,128,896]{2,1,0:T(8,128)(2,1)}, bf16[16,128,896]{2,1,0:T(8,128)(2,1)}, u32[]{:S(2)}, u32[]{:S(2)}) %collective-permute-start.12) | collective-permute-done | bytes 3670048 | tf_op jit(solution)/shard_map/ppermute | solution.py:414
  286.8 6.8 %pad_maximum_fusion.rows_ref = bf16[32,128,896]{2,1,0:T(8,128)(2,1)} fusion(bf16[16,128,896]{2,1,0:T(8,128)(2,1)} %collective-permute-done.12, bf16[16,128,896]{2,1,0:T(8,128)(2,1)} %param.9), kind=kLoop, calls=%fused_computation.6 | loop fusion | flops 3670016 | bytes 14680064 | tf_op jit(solution)/shard_map/concatenate | solution.py:415
  293.6 0.7 broadcast_in_dim.121.want_ref
  294.3 38.7 %odd_attention.1 = f32[128,1152]{1,0:T(8,128)} custom-call(bf16[128,1024]{1,0:T(8,128)(2,1)} %bitcast.66, s32[128,128]{1,0:T(8,128)} %broadcast_in_dim.121.want_ref, bf16[32,128,896]{2,1,0:T(8,128)(2,1)} %pad_maximum_fusion.rows_ref, bf16[896,2048]{1,0:T(8,128)(2,1)} %all-gather.2.cloned.1.call-done.weight_ref), custom_call_target="tpu_custom_call" | custom-call | tf_op jit(solution)/shard_map/odd_attention/pallas_call | solution.py:272
  333.0 5.6 %all-to-all-start.8 = ((f32[16,8,1152]{2,1,0:T(8,128)}), f32[16,8,1152]{2,1,0:T(8,128)S(1)}, u32[]{:S(2)}, u32[]{:S(2)}) async-start(f32[16,8,1152]{2,1,0:T(8,128)} %bitcast.65), calls=%async_computation.8 | async-start | bytes 1179648 | tf_op jit(solution)/shard_map/all_to_all | solution.py:428
  338.5 0.1 convert_reduce_fusion.1
  338.7 0.6 reduce_max.9
  340.0 13.1 %project.3.refs_0_ = bf16[2048,2048]{1,0:T(8,128)(2,1)} custom-call(bf16[8,32,8,896]{3,2,1,0:T(8,128)(2,1)} %bitcast.29.rows_ref, bf16[896,2048]{1,0:T(8,128)(2,1)} %all-gather.2.cloned.1.call-done.weight_ref), custom_call_target="tpu_custom_call" | custom-call | tf_op jit(solution)/shard_map/project/pallas_call | solution.py:38
  353.1 42.4 %even_attention.3 = bf16[2048,1024]{1,0:T(8,128)(2,1)} custom-call(bf16[2048,1024]{1,0:T(8,128)(2,1)} %query_ref.1, bf16[8,32,8,896]{3,2,1,0:T(8,128)(2,1)} %bitcast.28.rows_ref, bf16[896,2048]{1,0:T(8,128)(2,1)} %all-gather.2.cloned.1.call-done.weight_ref, bf16[2048,2048]{1,0:T(8,128)(2,1)} %project.3.refs_0_), custom_call_target="tpu_custom_call" | custom-call | tf_op jit(solution)/shard_map/even_attention/pallas_call | solution.py:92
  395.6 0.9 copy-done
  396.4 4.4 %patch.1 = bf16[16,8,16,1024]{3,2,1,0:T(8,128)(2,1)} custom-call(s32[32]{0:T(128)} %copy-done.11, bf16[16,8,16,1024]{3,2,1,0:T(8,128)(2,1)} %get-tuple-element.86.out_in_ref, f32[128,1152]{1,0:T(8,128)} %bitcast.64), custom_call_target="tpu_custom_call", output_to_operand_aliasing={{}: (1, {})} | custom-call | tf_op jit(solution)/shard_map/patch/pallas_call | solution.py:143
  (47 shorter events, 0.5 us)
Async XLA Ops:
  9.0 11.3 %all-to-all-start.2 = ((s32[16,1,128]{2,1,0:T(1,128)}), s32[16,1,128]{2,1,0:T(1,128)S(1)}, u32[]{:S(2)}, u32[]{:S(2)}) async-start(s32[16,1,128]{2,1,0:T(1,128)} %broadcast_in_dim.107), calls=%async_computation.2 | async-start | bytes 16384 | tf_op jit(solution)/shard_map/all_to_all | solution.py:329
  20.3 4.4 %copy-start.9 = (bf16[56,1024]{1,0:T(8,128)(2,1)S(1)}, bf16[56,1024]{1,0:T(8,128)(2,1)}, u32[]{:S(2)}) copy-start(bf16[56,1024]{1,0:T(8,128)(2,1)} %param.11) | copy-start | bytes 344068
  20.3 4.4 %copy-start.10 = (bf16[56,1024]{1,0:T(8,128)(2,1)S(1)}, bf16[56,1024]{1,0:T(8,128)(2,1)}, u32[]{:S(2)}) copy-start(bf16[56,1024]{1,0:T(8,128)(2,1)} %param.10) | copy-start | bytes 344068
  20.4 27.9 %all-to-all-start.3 = ((bf16[128,8,896]{2,1,0:T(8,128)(2,1)}), bf16[128,8,896]{2,1,0:T(8,128)(2,1)S(1)}, u32[]{:S(2)}, u32[]{:S(2)}) async-start(bf16[128,8,896]{2,1,0:T(8,128)(2,1)} %bitcast.63), calls=%async_computation.3 | async-start | bytes 3670016 | tf_op jit(solution)/shard_map/all_to_all | solution.py:310
  24.7 268.9 %all-gather.2.cloned.1.call-start = ((), (), s32[]{:S(2)}) async-start(), calls=%async_computation.9 | async-start | bytes 3899392 | tf_op jit(solution)/shard_map/all_gather | solution.py:334
  48.3 37.0 %all-to-all-start.4 = ((bf16[128,8,896]{2,1,0:T(8,128)(2,1)}), bf16[128,8,896]{2,1,0:T(8,128)(2,1)}, u32[]{:S(2)}, u32[]{:S(2)}) async-start(bf16[128,8,896]{2,1,0:T(8,128)(2,1)} %bitcast.62), calls=%async_computation.4 | async-start | bytes 3670016 | tf_op jit(solution)/shard_map/all_to_all | solution.py:310
  56.8 83.8 %copy-start.11 = (s32[32]{0:T(128)}, s32[32]{0:T(128)S(1)}, u32[]{:S(2)}) copy-start(s32[32]{0:T(128)S(1)} %fusion.9.slot_ref) | copy-start | bytes 388
  59.4 33.2 %collective-permute-start.6 = (bf16[48,8,896]{2,1,0:T(8,128)(2,1)}, bf16[48,8,896]{2,1,0:T(8,128)(2,1)S(1)}, u32[]{:S(2)}, u32[]{:S(2)}) collective-permute-start(bf16[48,8,896]{2,1,0:T(8,128)(2,1)} %get-tuple-element.63), channel_id=1, source_target_pairs={{0,8},{1,9},{2,10},{3,11},{4,12},{5,13},{6,14},{7,15},{8,16},{9,17... | collective-permute-start | bytes 2064392 | tf_op jit(solution)/shard_map/ppermute | solution.py:324
  60.5 73.2 %collective-permute-start.7 = (bf16[48,8,896]{2,1,0:T(8,128)(2,1)}, bf16[48,8,896]{2,1,0:T(8,128)(2,1)S(1)}, u32[]{:S(2)}, u32[]{:S(2)}) collective-permute-start(bf16[48,8,896]{2,1,0:T(8,128)(2,1)} %get-tuple-element.64), channel_id=1, source_target_pairs={{0,16},{1,17},{2,18},{3,19},{4,20},{5,21},{6,22},{7,23},{8,24},{9,... | collective-permute-start | bytes 2064392 | tf_op jit(solution)/shard_map/ppermute | solution.py:324
  62.6 73.2 %collective-permute-start.8 = (bf16[48,8,896]{2,1,0:T(8,128)(2,1)}, bf16[48,8,896]{2,1,0:T(8,128)(2,1)}, u32[]{:S(2)}, u32[]{:S(2)}) collective-permute-start(bf16[48,8,896]{2,1,0:T(8,128)(2,1)} %get-tuple-element.65), channel_id=1, source_target_pairs={{0,24},{1,25},{2,26},{3,27},{4,28},{5,29},{6,30},{7,31},{8,0},{9,1... | collective-permute-start | bytes 2064392 | tf_op jit(solution)/shard_map/ppermute | solution.py:324
  85.3 55.3 %all-to-all-start.5 = ((bf16[16,8,1024]{2,1,0:T(8,128)(2,1)}), bf16[16,8,1024]{2,1,0:T(8,128)(2,1)S(1)}, u32[]{:S(2)}, u32[]{:S(2)}) async-start(bf16[16,8,1024]{2,1,0:T(8,128)(2,1)} %bitcast.26), calls=%async_computation.5 | async-start | bytes 524288 | tf_op jit(solution)/shard_map/all_to_all | solution.py:364
  92.5 43.3 %copy-start.5 = (bf16[48,8,896]{2,1,0:T(8,128)(2,1)}, bf16[48,8,896]{2,1,0:T(8,128)(2,1)S(1)}, u32[]{:S(2)}) copy-start(bf16[48,8,896]{2,1,0:T(8,128)(2,1)S(1)} %collective-permute-done.6.refs_1_) | copy-start | bytes 2064388
  133.7 2.1 copy-start.6
  140.6 0.7 copy-start.4
  141.3 77.3 %all-to-all-start.6 = ((bf16[256,8,896]{2,1,0:T(8,128)(2,1)}), bf16[256,8,896]{2,1,0:T(8,128)(2,1)}, u32[]{:S(2)}, u32[]{:S(2)}) async-start(bf16[256,8,896]{2,1,0:T(8,128)(2,1)} %bitcast.58), calls=%async_computation.6 | async-start | bytes 7340032 | tf_op jit(solution)/shard_map/all_to_all | solution.py:310
  146.5 140.3 %collective-permute-start.12 = (bf16[16,128,896]{2,1,0:T(8,128)(2,1)}, bf16[16,128,896]{2,1,0:T(8,128)(2,1)}, u32[]{:S(2)}, u32[]{:S(2)}) collective-permute-start(bf16[16,128,896]{2,1,0:T(8,128)(2,1)} %param.9), channel_id=1, source_target_pairs={{0,1},{1,0},{2,3},{3,2},{4,5},{5,4},{6,7},{7,6},{8,9},{9,8},{10,11... | collective-permute-start | bytes 11010056 | tf_op jit(solution)/shard_map/ppermute | solution.py:414
  151.8 16.6 %collective-permute-start.9 = (bf16[48,8,896]{2,1,0:T(8,128)(2,1)}, bf16[48,8,896]{2,1,0:T(8,128)(2,1)S(1)}, u32[]{:S(2)}, u32[]{:S(2)}) collective-permute-start(bf16[48,8,896]{2,1,0:T(8,128)(2,1)} %get-tuple-element.67), channel_id=1, source_target_pairs={{0,8},{1,9},{2,10},{3,11},{4,12},{5,13},{6,14},{7,15},{8,16},{9,17... | collective-permute-start | bytes 2064392 | tf_op jit(solution)/shard_map/ppermute | solution.py:324
  151.8 59.0 %collective-permute-start.10 = (bf16[48,8,896]{2,1,0:T(8,128)(2,1)}, bf16[48,8,896]{2,1,0:T(8,128)(2,1)S(1)}, u32[]{:S(2)}, u32[]{:S(2)}) collective-permute-start(bf16[48,8,896]{2,1,0:T(8,128)(2,1)} %get-tuple-element.68), channel_id=1, source_target_pairs={{0,16},{1,17},{2,18},{3,19},{4,20},{5,21},{6,22},{7,23},{8,24},{9,... | collective-permute-start | bytes 2064392 | tf_op jit(solution)/shard_map/ppermute | solution.py:324
  153.3 60.5 %collective-permute-start.11 = (bf16[48,8,896]{2,1,0:T(8,128)(2,1)}, bf16[48,8,896]{2,1,0:T(8,128)(2,1)}, u32[]{:S(2)}, u32[]{:S(2)}) collective-permute-start(bf16[48,8,896]{2,1,0:T(8,128)(2,1)} %get-tuple-element.69), channel_id=1, source_target_pairs={{0,24},{1,25},{2,26},{3,27},{4,28},{5,29},{6,30},{7,31},{8,0},{9,1... | collective-permute-start | bytes 2064392 | tf_op jit(solution)/shard_map/ppermute | solution.py:324
  168.4 45.4 %copy-start.7 = (bf16[48,8,896]{2,1,0:T(8,128)(2,1)}, bf16[48,8,896]{2,1,0:T(8,128)(2,1)S(1)}, u32[]{:S(2)}) copy-start(bf16[48,8,896]{2,1,0:T(8,128)(2,1)S(1)} %collective-permute-done.9.refs_1_) | copy-start | bytes 2064388
  210.7 3.1 copy-start.8
  218.6 114.4 %all-to-all-start.7 = ((bf16[256,8,896]{2,1,0:T(8,128)(2,1)}), bf16[256,8,896]{2,1,0:T(8,128)(2,1)}, u32[]{:S(2)}, u32[]{:S(2)}) async-start(bf16[256,8,896]{2,1,0:T(8,128)(2,1)} %bitcast.57), calls=%async_computation.7 | async-start | bytes 7340032 | tf_op jit(solution)/shard_map/all_to_all | solution.py:310
  333.0 62.6 %all-to-all-start.8 = ((f32[16,8,1152]{2,1,0:T(8,128)}), f32[16,8,1152]{2,1,0:T(8,128)S(1)}, u32[]{:S(2)}, u32[]{:S(2)}) async-start(f32[16,8,1152]{2,1,0:T(8,128)} %bitcast.65), calls=%async_computation.8 | async-start | bytes 1179648 | tf_op jit(solution)/shard_map/all_to_all | solution.py:428
  395.6 0.9 copy-start
Sparse Core Ops, SparseCore 0:
  27.8 67.4 all-gather.1

commit v3 on v2

--- a/solution.py
+++ b/solution.py
@@ -230,15 +230,24 @@
     )(index.reshape(-1), source)
 
 
-def odd_body(query_ref, want_ref, rows_ref, weight_ref, out_ref):
+def odd_body(query_ref, want_ref, *refs):
+    rows_refs, (weight_ref, prior_ref, out_ref) = refs[:-3], refs[-3:]
     columns = query_ref.shape[1]
     heads = columns // DH
-    per_step, tokens, width = rows_ref.shape
-    base = pl.program_id(0) * per_step
-    projected = jnp.dot(
-        rows_ref[...].reshape(per_step * tokens, width), weight_ref[...], preferred_element_type=F32
-    ).astype(BF16)
-    want = want_ref[...] - base
+    lanes, per_step, piece, width = rows_refs[0].shape
+    tokens = len(rows_refs) * lanes * piece
+    step = pl.program_id(0)
+
+    @pl.when(step == 0)
+    def _():
+        out_ref[...] = prior_ref[...]
+
+    pieces = [ref[...] for ref in rows_refs]
+    stacked = jnp.concatenate(
+        [p[:, r].reshape(lanes * piece, width) for r in range(per_step) for p in pieces], axis=0
+    )
+    projected = jnp.dot(stacked, weight_ref[...], preferred_element_type=F32).astype(BF16)
+    want = want_ref[...] - step * per_step
     here = [want == r for r in range(per_step)]
     inside = (want >= 0) & (want < per_step)
     lane = lax.broadcasted_iota(jnp.int32, (want.shape[0], DH), 1)
@@ -265,23 +274,25 @@
     out_ref[:, columns:] = stats
 
 
-def odd_attention(queries, want, rows, weights):
+def odd_attention(queries, want, rows, weights, prior):
     slots, columns = queries.shape
-    count, tokens, width = rows.shape
+    lanes, count, piece, width = rows[0].shape
     per_step = math.gcd(count, 4)
+    row_spec = pl.BlockSpec((lanes, per_step, piece, width), lambda i: (0, i, 0, 0))
     return pl.pallas_call(
         odd_body,
-        out_shape=jax.ShapeDtypeStruct((slots, columns + DH), F32),
+        out_shape=jax.ShapeDtypeStruct(prior.shape, F32),
         grid=(count // per_step,),
         in_specs=[
             pl.BlockSpec((slots, columns), lambda i: (0, 0)),
             pl.BlockSpec((slots, DH), lambda i: (0, 0)),
-            pl.BlockSpec((per_step, tokens, width), lambda i: (i, 0, 0)),
+            *[row_spec for _ in rows],
             pl.BlockSpec(weights.shape, lambda i: (0, 0)),
+            pl.BlockSpec(prior.shape, lambda i: (0, 0)),
         ],
-        out_specs=pl.BlockSpec((slots, columns + DH), lambda i: (0, 0)),
+        out_specs=pl.BlockSpec(prior.shape, lambda i: (0, 0)),
         name="odd_attention",
-    )(queries, want, rows, weights)
+    )(queries, want, *rows, weights, prior)
 
 
 def local(queries, encodings, key_weight, value_weight, nbr_shard, nbr_row):
@@ -335,15 +346,39 @@
         jnp.concatenate([key_weight, value_weight], axis=1), "db", axis=0, tiled=True
     )
 
-    pieces = jnp.transpose(encodings.reshape(held, lanes, CHUNKS, piece, width), (2, 1, 0, 3, 4))
-    plane_pieces = []
-
-    def spread(chunk, after):
-        sending, _ = lax.optimization_barrier((pieces[chunk].reshape(lanes * held, piece, width), after))
-        plane_pieces.append(swap(sending, plane_groups))
-
-    for chunk in range(CHUNKS):
-        spread(chunk, plane_pieces[-1] if chunk else table)
+    early_half, late_half = jnp.transpose(encodings.reshape(held, lanes, CHUNKS, piece, width), (2, 1, 0, 3, 4))
+    first, _ = lax.optimization_barrier((early_half.reshape(lanes * held, piece, width), table))
+    first = swap(first, plane_groups)
+
+    part_index = lax.axis_index("mp")
+
+    def share(half, after):
+        half, _ = lax.optimization_barrier((half, after))
+        shared = [half]
+        for k in range(1, parts):
+            shared.append(lax.ppermute(half, "mp", [(m, (m + k) % parts) for m in range(parts)]))
+        return shared
+
+    late_shared = share(late_half, first)
+    second = [
+        lax.dynamic_index_in_dim(
+            half.reshape(group, parts, held, piece, width), part_index, 1, keepdims=False
+        )
+        for half in late_shared
+    ]
+    second = jnp.concatenate(second, axis=1).reshape(group * shard_rows, piece, width)
+    part_groups = [
+        [a * lanes + g * parts + m for g in range(group)] for a in range(planes) for m in range(parts)
+    ]
+    second, _ = lax.optimization_barrier((second, first))
+    if group > 1:
+        second = swap(second, part_groups)
+    early_shared = share(early_half, late_shared)
+    plane_pieces = [first, second]
+
+    def stepped(row):
+        step = (part_index + parts - row % shard_rows // held) % parts
+        return row // shard_rows * shard_rows + step * held + row % held
 
     odd_shard = table_shard[:, :, 1].reshape(shards, wanted)
     odd_row = table_row[:, :, 1].reshape(shards, wanted)
@@ -387,43 +422,42 @@
     place = jnp.sum(jnp.where(my_ids[:, None] == ids[None, :], my_rank[None, :], 0), axis=1)
     my_step = (plane_index + planes - my_ids // plane_rows) % planes
 
-    def exact(source):
+    def exact(source, chunk):
+        rows = stepped(send_rows) if chunk else send_rows
         if planes > MOST_SHIFTS:
-            return [jnp.take(source, send_rows[k], axis=0, mode="clip") for k in range(planes)]
-        return select_rows(send_rows, source)
-
-    def whole(source):
+            return [jnp.take(source, rows[k], axis=0, mode="clip") for k in range(planes)]
+        return select_rows(rows, source)
+
+    def whole(source, chunk):
         return [source] * planes
 
     def exchange(sources, select, index):
         received, arrived = [], []
-        for source in sources:
-            sending = select(source)
+        for chunk, source in enumerate(sources):
+            sending = select(source, chunk)
             if received:
                 sending, _ = lax.optimization_barrier((sending, received[-1]))
             received.append(across(sending))
-            outgoing = gather_rows(index, received[-1], group, parts)
+            outgoing = gather_rows(index[chunk], received[-1], group, parts)
             outgoing, _ = lax.optimization_barrier((outgoing, arrived[-1] if arrived else odd_query))
             arrived.append(swap(outgoing, plane_groups))
         return [a.reshape(lanes, wanted, piece, width) for a in arrived]
 
-    part_index = lax.axis_index("mp")
-    sharing, _ = lax.optimization_barrier((encodings, plane_pieces[-1]))
-    shared = [encodings]
-    for k in range(1, parts):
-        shared.append(lax.ppermute(sharing, "mp", [(m, (m + k) % parts) for m in range(parts)]))
-    shard_enc = jnp.concatenate(shared, axis=0)
-    slot_step = (part_index + parts - slot_row // held) % parts
-    slot_row = jnp.where(slot_row >= 0, slot_step * held + slot_row % held, -1)
-    slot_lanes = jnp.broadcast_to(slot_row.reshape(-1, 1), (shards * capacity, DH))
-    odd_part = odd_attention(odd_query, slot_lanes, shard_enc, weights)
+    odd_part = jnp.zeros((shards * capacity, columns + DH), F32)
+    for k in range(parts):
+        slot_want = slot_row - (part_index + parts - k) % parts * held
+        slot_want = jnp.broadcast_to(slot_want.reshape(-1, 1), (shards * capacity, DH))
+        odd_part = odd_attention(
+            odd_query, slot_want, (early_shared[k], late_shared[k]), weights, odd_part
+        )
 
     def attend(select, index):
         *early, late = exchange(plane_pieces, select, index)
         early = [project(e, weights) for e in early]
         return even_attention(queries, late, weights, early), late
 
-    result, last = attend(exact, my_step * fast + jnp.minimum(place, fast - 1))
+    fast_index = my_step * fast + jnp.minimum(place, fast - 1)
+    result, last = attend(exact, [fast_index] * CHUNKS)
     odd_part, _ = lax.optimization_barrier((odd_part, last))
     odd_part = lax.all_to_all(odd_part.reshape(shards, capacity, columns + DH), "db", 0, 0, tiled=True)
     odd_part = odd_part.reshape(shards * capacity, columns + DH)
@@ -432,7 +466,9 @@
         result = lax.cond(
             fits,
             lambda done: done,
-            lambda done: attend(whole, my_step * plane_rows + my_ids % plane_rows)[0],
+            lambda done: attend(
+                whole, [my_step * plane_rows + row for row in (my_ids % plane_rows, stepped(my_ids % plane_rows))]
+            )[0],
             result,
         )
     return patch(my_slot, result, odd_part)

time: 409 us -> 436 us (1.066)
  blocking collectives: 0 us -> 26.5 us
  local copies, waits for them, and re-layouts: 13.8 us -> 18.8 us
  other arithmetic: 10.7 us -> 5.92 us
    ppermute x1 -> x2, waiting for transfers between devices: 62.4 us -> 94.4 us  [share(): lax.ppermute(half, 'mp', [(m, (m + k) % parts) for m in range(parts)])]
    all_to_all x4 -> x3, waiting for transfers between devices: 42.4 us -> 10.9 us  [swap(): return lax.all_to_all(x, BOTH, 0, 0, axis_index_groups=groups, tiled=True)]
    all_to_all x0 -> x1, blocking collectives: none -> 26.5 us  [swap(): return lax.all_to_all(x, BOTH, 0, 0, axis_index_groups=groups, tiled=True)]
    concatenate x1, other arithmetic: 6.81 us -> 1.41 us  [local(): jnp.concatenate(second, axis=1).reshape(group * shard_rows, piece, width)]
    all_to_all x4 -> x3, starting transfers between devices: 20.5 us -> 16.1 us  [swap(): return lax.all_to_all(x, BOTH, 0, 0, axis_index_groups=groups, tiled=True)]
    pallas_call x1 -> x2, Pallas kernels: 38.7 us -> 42.4 us  [odd_attention(): pl.pallas_call(odd_body, out_shape=jax.ShapeDtypeStruct(prior.shape, F32)...]
  transfers between devices with their start and end apart: 15 -> 15, of which waited for: 8 -> 8; matrix products, arithmetic and copies ran while one was open for 5% -> 5% of each run, Pallas kernels for 27% -> 26%
where the time goes in v3:
time: 436 us; the launch traced here: 434 us
  waiting for transfers between devices  207 us (47%)
  Pallas kernels  119 us (27%)
  starting transfers between devices  42.7 us (10%)
  blocking collectives  26.5 us (6%)
  local copies, waits for them, and re-layouts  18.8 us (4%)
  between operations  14.3 us (3%)
  other arithmetic  5.92 us (1%)
    ppermute x6, waiting for transfers between devices, across(): moved.append(lax.ppermute(blocks[k], BOTH, pairs))  101 us
    ppermute x2, waiting for transfers between devices, share(): lax.ppermute(half, 'mp', [(m, (m + k) % parts) for m in range(parts)])  94.4 us
    pallas_call x1, Pallas kernels, even_attention(): pl.pallas_call(functools.partial(even_body, per_step=per_step, neighbours...  42.4 us
    pallas_call x2, Pallas kernels, odd_attention(): pl.pallas_call(odd_body, out_shape=jax.ShapeDtypeStruct(prior.shape, F32)...  42.4 us
    all_to_all x1, blocking collectives, swap(): return lax.all_to_all(x, BOTH, 0, 0, axis_index_groups=groups, tiled=True)  26.5 us
    all_to_all x3, starting transfers between devices, swap(): return lax.all_to_all(x, BOTH, 0, 0, axis_index_groups=groups, tiled=True)  16.1 us
    pallas_call x1, Pallas kernels, project(): pl.pallas_call(project_body, out_shape=jax.ShapeDtypeStruct((count * toke...  13.2 us
    all_to_all x3, waiting for transfers between devices, swap(): return lax.all_to_all(x, BOTH, 0, 0, axis_index_groups=groups, tiled=True)  10.9 us
  transfers between devices with their start and end apart: 15, of which 8 were waited for; matrix products, arithmetic and copies ran while one was open for 5% of the time, Pallas kernels for 26%

profile of v3, /device:TPU:11, one launch (start us, length us, event | category | flops | bytes accessed | tf_op | source)
XLA Modules:
  0.0 433.6 jit_solution(16281189064802403360)
XLA Ops:
  6.5 0.8 copy.57
  7.3 0.1 reshape.200
  7.4 0.8 copy.58
  8.2 0.1 reshape.201
  8.3 0.6 broadcast_in_dim.113
  9.0 6.5 %all-to-all-start.2 = ((s32[16,1,128]{2,1,0:T(1,128)}), s32[16,1,128]{2,1,0:T(1,128)S(1)}, u32[]{:S(2)}, u32[]{:S(2)}) async-start(s32[16,1,128]{2,1,0:T(1,128)} %broadcast_in_dim.113), calls=%async_computation.2 | async-start | bytes 16384 | tf_op jit(solution)/shard_map/all_to_all | solution.py:340
  15.5 2.6 copy.79
  18.1 3.0 slice_bitcast_fusion.1
  21.1 0.1 copy.59
  21.2 26.5 %all_to_all.43.source_ref = bf16[128,8,896]{2,1,0:T(8,128)(2,1)S(1)} all-to-all(bf16[128,8,896]{2,1,0:T(8,128)(2,1)} %bitcast.72), channel_id=1, replica_groups={{0,1,2,3,4,5,6,7},{8,9,10,11,12,13,14,15},{16,17,18,19,20,21,22,23},{24..., dimensions={0} | all-to-all | bytes 3670016 | tf_op jit(solution)/shard_map/all_to_all | solution.py:321
  47.7 0.2 collective-permute-start.6
  47.9 0.7 pad_maximum_fusion.1
  48.7 1.0 slice.35
  50.0 1.3 dynamic-slice_bitcast_fusion.1
  51.3 37.9 %collective-permute-done.6.refs_1_ = bf16[8,16,8,896]{3,2,1,0:T(8,128)(2,1)} collective-permute-done((bf16[8,16,8,896]{3,2,1,0:T(8,128)(2,1)}, bf16[8,16,8,896]{3,2,1,0:T(8,128)(2,1)}, u32[]{:S(2)}, u32[]{:S(2)}) %collective-permute-start.6) | collective-permute-done | bytes 1835040 | tf_op jit(solution)/shard_map/ppermute | solution.py:359
  89.2 1.3 dynamic-slice_bitcast_fusion
  90.4 1.4 pad_maximum_fusion
  91.9 6.3 %all-to-all-start.4 = ((bf16[128,8,896]{2,1,0:T(8,128)(2,1)}), bf16[128,8,896]{2,1,0:T(8,128)(2,1)}, u32[]{:S(2)}, u32[]{:S(2)}) async-start(bf16[128,8,896]{2,1,0:T(8,128)(2,1)} %bitcast.71), calls=%async_computation.4 | async-start | bytes 3670016 | tf_op jit(solution)/shard_map/all_to_all | solution.py:321
  98.3 0.2 copy.66
  98.4 0.1 add.173
  98.6 0.2 fusion.6
  98.9 0.1 convolution_convert_fusion
  99.0 0.1 select_reduce_fusion.1
  99.2 0.1 select_reduce_fusion.4
  99.3 0.7 reduce_sum.70.index_ref
  99.9 0.5 convert_reduce_fusion
  100.4 2.6 select_rows.3
  103.0 1.2 collective-permute-start.7
  104.2 1.3 collective-permute-start.8
  105.5 1.1 collective-permute-start.9
  106.7 1.6 gather_fusion
  108.3 10.9 %all-to-all-done.4.source_ref = bf16[128,8,896]{2,1,0:T(8,128)(2,1)} async-done(((bf16[128,8,896]{2,1,0:T(8,128)(2,1)}), bf16[128,8,896]{2,1,0:T(8,128)(2,1)}, u32[]{:S(2)}, u32[]{:S(2)}) %all-to-all-start.4) | async-done | bytes 1835040 | tf_op jit(solution)/shard_map/all_to_all | solution.py:321
  119.2 6.5 %all-to-all-start.5 = ((bf16[16,8,1024]{2,1,0:T(8,128)(2,1)}), bf16[16,8,1024]{2,1,0:T(8,128)(2,1)S(1)}, u32[]{:S(2)}, u32[]{:S(2)}) async-start(bf16[16,8,1024]{2,1,0:T(8,128)(2,1)} %bitcast.31), calls=%async_computation.5 | async-start | bytes 524288 | tf_op jit(solution)/shard_map/all_to_all | solution.py:399
  125.7 0.2 select_reduce_fusion
  125.9 0.6 minimum_add_fusion
  126.5 39.4 %collective-permute-done.8.refs_2_ = bf16[48,8,896]{2,1,0:T(8,128)(2,1)S(1)} collective-permute-done((bf16[48,8,896]{2,1,0:T(8,128)(2,1)}, bf16[48,8,896]{2,1,0:T(8,128)(2,1)S(1)}, u32[]{:S(2)}, u32[]{:S(2)}) %collective-permute-start.8) | collective-permute-done | bytes 688160 | tf_op jit(solution)/shard_map/ppermute | solution.py:335
  166.0 2.9 collective-permute-done.9.refs_3_
  168.9 4.8 %gather_rows.7 = bf16[4,2,32,8,896]{4,3,2,1,0:T(8,128)(2,1)} custom-call(s32[128]{0:T(128)} %get-tuple-element.84.index_ref, bf16[48,8,896]{2,1,0:T(8,128)(2,1)} %get-tuple-element.67.refs_0_, bf16[48,8,896]{2,1,0:T(8,128)(2,1)} %copy-done.6, bf16[48,8,896]{2,1,0:T(8,128)(2,1)} %copy-done.7, bf16[48,8,896]{2,1,0:T(8,128)(2,1)} %collective-permute-done.9.refs_3_), custom_call_target="tpu_custom_call" | custom-call | tf_op jit(solution)/shard_map/gather_rows/pallas_call | solution.py:188
  173.7 0.7 copy-done.1
  174.4 5.0 %all-to-all-start.6 = ((bf16[256,8,896]{2,1,0:T(8,128)(2,1)}), bf16[256,8,896]{2,1,0:T(8,128)(2,1)}, u32[]{:S(2)}, u32[]{:S(2)}) async-start(bf16[256,8,896]{2,1,0:T(8,128)(2,1)} %bitcast.67), calls=%async_computation.6 | async-start | bytes 7340032 | tf_op jit(solution)/shard_map/all_to_all | solution.py:321
  179.4 0.6 fusion.12.index_ref
  180.0 4.1 select_rows.2
  184.1 2.2 collective-permute-start.11
  186.3 1.5 collective-permute-start.12
  187.8 13.3 %collective-permute-done.10.refs_1_ = bf16[48,8,896]{2,1,0:T(8,128)(2,1)S(1)} collective-permute-done((bf16[48,8,896]{2,1,0:T(8,128)(2,1)}, bf16[48,8,896]{2,1,0:T(8,128)(2,1)S(1)}, u32[]{:S(2)}, u32[]{:S(2)}) %collective-permute-start.10) | collective-permute-done | bytes 688160 | tf_op jit(solution)/shard_map/ppermute | solution.py:335
  201.1 42.3 %collective-permute-done.11.refs_2_ = bf16[48,8,896]{2,1,0:T(8,128)(2,1)S(1)} collective-permute-done((bf16[48,8,896]{2,1,0:T(8,128)(2,1)}, bf16[48,8,896]{2,1,0:T(8,128)(2,1)S(1)}, u32[]{:S(2)}, u32[]{:S(2)}) %collective-permute-start.11) | collective-permute-done | bytes 688160 | tf_op jit(solution)/shard_map/ppermute | solution.py:335
  243.4 3.4 collective-permute-done.12.refs_3_
  246.8 4.7 %gather_rows.6 = bf16[4,2,32,8,896]{4,3,2,1,0:T(8,128)(2,1)} custom-call(s32[128]{0:T(128)} %get-tuple-element.84.index_ref, bf16[48,8,896]{2,1,0:T(8,128)(2,1)} %get-tuple-element.71.refs_0_, bf16[48,8,896]{2,1,0:T(8,128)(2,1)} %copy-done.8, bf16[48,8,896]{2,1,0:T(8,128)(2,1)} %copy-done.9, bf16[48,8,896]{2,1,0:T(8,128)(2,1)} %collective-permute-done.12.refs_3_), custom_call_target="tpu_custom_call" | custom-call | tf_op jit(solution)/shard_map/gather_rows/pallas_call | solution.py:188
  251.6 4.9 %all-to-all-start.7 = ((bf16[256,8,896]{2,1,0:T(8,128)(2,1)}), bf16[256,8,896]{2,1,0:T(8,128)(2,1)}, u32[]{:S(2)}, u32[]{:S(2)}) async-start(bf16[256,8,896]{2,1,0:T(8,128)(2,1)} %bitcast.66), calls=%async_computation.7 | async-start | bytes 7340032 | tf_op jit(solution)/shard_map/all_to_all | solution.py:321
  256.5 1.2 collective-permute-start.13
  257.9 0.4 select_reduce_fusion.2
  258.5 0.7 broadcast_in_dim.128.want_ref
  259.2 0.9 broadcast_in_dim.129.refs_3_
  260.1 21.2 %odd_attention.2.refs_3_ = f32[128,1152]{1,0:T(8,128)} custom-call(bf16[128,1024]{1,0:T(8,128)(2,1)} %bitcast.76, s32[128,128]{1,0:T(8,128)} %broadcast_in_dim.128.want_ref, bf16[8,16,8,896]{3,2,1,0:T(8,128)(2,1)} %get-tuple-element.78.refs_0_, bf16[8,16,8,896]{3,2,1,0:T(8,128)(2,1)} %get-tuple-element.61.refs_1_, ...), custom_call_target="tpu_custom_call" | custom-call | tf_op jit(solution)/shard_map/odd_attention/pallas_call | solution.py:282
  281.3 56.5 %collective-permute-done.13.refs_0_ = bf16[8,16,8,896]{3,2,1,0:T(8,128)(2,1)} collective-permute-done((bf16[8,16,8,896]{3,2,1,0:T(8,128)(2,1)}, bf16[8,16,8,896]{3,2,1,0:T(8,128)(2,1)}, u32[]{:S(2)}, u32[]{:S(2)}) %collective-permute-start.13) | collective-permute-done | bytes 1835040 | tf_op jit(solution)/shard_map/ppermute | solution.py:359
  337.8 0.7 broadcast_in_dim.127.want_ref
  338.5 21.2 %odd_attention.3 = f32[128,1152]{1,0:T(8,128)} custom-call(bf16[128,1024]{1,0:T(8,128)(2,1)} %bitcast.77, s32[128,128]{1,0:T(8,128)} %broadcast_in_dim.127.want_ref, bf16[8,16,8,896]{3,2,1,0:T(8,128)(2,1)} %collective-permute-done.13.refs_0_, bf16[8,16,8,896]{3,2,1,0:T(8,128)(2,1)} %collective-permute-done.6.refs_1_, ...), custom_call_target="tpu_custom_call" | custom-call | tf_op jit(solution)/shard_map/odd_attention/pallas_call | solution.py:282
  359.7 4.9 %all-to-all-start.8 = ((f32[16,8,1152]{2,1,0:T(8,128)}), f32[16,8,1152]{2,1,0:T(8,128)S(1)}, u32[]{:S(2)}, u32[]{:S(2)}) async-start(f32[16,8,1152]{2,1,0:T(8,128)} %bitcast.75), calls=%async_computation.8 | async-start | bytes 1179648 | tf_op jit(solution)/shard_map/all_to_all | solution.py:462
  364.5 0.1 convert_reduce_fusion.1
  364.7 0.6 reduce_max.9
  366.0 13.2 %project.3.refs_0_ = bf16[2048,2048]{1,0:T(8,128)(2,1)} custom-call(bf16[8,32,8,896]{3,2,1,0:T(8,128)(2,1)} %bitcast.34.rows_ref, bf16[896,2048]{1,0:T(8,128)(2,1)} %all-gather.2.cloned.1.call-done.weight_ref.refs_2_), custom_call_target="tpu_custom_call" | custom-call | tf_op jit(solution)/shard_map/project/pallas_call | solution.py:38
  379.1 42.4 %even_attention.3 = bf16[2048,1024]{1,0:T(8,128)(2,1)} custom-call(bf16[2048,1024]{1,0:T(8,128)(2,1)} %query_ref.1, bf16[8,32,8,896]{3,2,1,0:T(8,128)(2,1)} %bitcast.33.rows_ref, bf16[896,2048]{1,0:T(8,128)(2,1)} %all-gather.2.cloned.1.call-done.weight_ref.refs_2_, bf16[2048,2048]{1,0:T(8,128)(2,1)} %project.3.refs_0_), custom_call_target="tpu_custom_call" | custom-call | tf_op jit(solution)/shard_map/even_attention/pallas_call | solution.py:92
  421.6 0.9 copy-done
  422.4 4.4 %patch.1 = bf16[16,8,16,1024]{3,2,1,0:T(8,128)(2,1)} custom-call(s32[32]{0:T(128)} %copy-done.13, bf16[16,8,16,1024]{3,2,1,0:T(8,128)(2,1)} %get-tuple-element.96.out_in_ref, f32[128,1152]{1,0:T(8,128)} %bitcast.74), custom_call_target="tpu_custom_call", output_to_operand_aliasing={{}: (1, {})} | custom-call | tf_op jit(solution)/shard_map/patch/pallas_call | solution.py:143
  (56 shorter events, 1.2 us)
Async XLA Ops:
  9.0 12.2 %all-to-all-start.2 = ((s32[16,1,128]{2,1,0:T(1,128)}), s32[16,1,128]{2,1,0:T(1,128)S(1)}, u32[]{:S(2)}, u32[]{:S(2)}) async-start(s32[16,1,128]{2,1,0:T(1,128)} %broadcast_in_dim.113), calls=%async_computation.2 | async-start | bytes 16384 | tf_op jit(solution)/shard_map/all_to_all | solution.py:340
  15.5 243.0 %all-gather.2.cloned.1.call-start = ((), (), s32[]{:S(2)}) async-start(), calls=%async_computation.9 | async-start | bytes 3899392 | tf_op jit(solution)/shard_map/all_gather | solution.py:345
  21.2 26.7 %copy-start.10 = (bf16[56,1024]{1,0:T(8,128)(2,1)S(1)}, bf16[56,1024]{1,0:T(8,128)(2,1)}, u32[]{:S(2)}) copy-start(bf16[56,1024]{1,0:T(8,128)(2,1)} %param.11) | copy-start | bytes 344068
  21.2 26.7 %copy-start.11 = (bf16[56,1024]{1,0:T(8,128)(2,1)S(1)}, bf16[56,1024]{1,0:T(8,128)(2,1)}, u32[]{:S(2)}) copy-start(bf16[56,1024]{1,0:T(8,128)(2,1)} %param.10) | copy-start | bytes 344068
  47.7 41.5 %collective-permute-start.6 = (bf16[8,16,8,896]{3,2,1,0:T(8,128)(2,1)}, bf16[8,16,8,896]{3,2,1,0:T(8,128)(2,1)}, u32[]{:S(2)}, u32[]{:S(2)}) collective-permute-start(bf16[8,16,8,896]{3,2,1,0:T(8,128)(2,1)} %get-tuple-element.61.refs_1_), channel_id=1, source_target_pairs={{0,1},{1,0},{2,3},{3,2},{4,5},{5,4},{6,7},{7,6},{8,9},{9,8},{10,11... | collective-permute-start | bytes 5505032 | tf_op jit(solution)/shard_map/ppermute | solution.py:359
  91.9 27.4 %all-to-all-start.4 = ((bf16[128,8,896]{2,1,0:T(8,128)(2,1)}), bf16[128,8,896]{2,1,0:T(8,128)(2,1)}, u32[]{:S(2)}, u32[]{:S(2)}) async-start(bf16[128,8,896]{2,1,0:T(8,128)(2,1)} %bitcast.71), calls=%async_computation.4 | async-start | bytes 3670016 | tf_op jit(solution)/shard_map/all_to_all | solution.py:321
  100.4 7.9 %copy-start.13 = (s32[32]{0:T(128)}, s32[32]{0:T(128)S(1)}, u32[]{:S(2)}) copy-start(s32[32]{0:T(128)S(1)} %fusion.17.slot_ref) | copy-start | bytes 388
  103.0 23.5 %collective-permute-start.7 = (bf16[48,8,896]{2,1,0:T(8,128)(2,1)}, bf16[48,8,896]{2,1,0:T(8,128)(2,1)S(1)}, u32[]{:S(2)}, u32[]{:S(2)}) collective-permute-start(bf16[48,8,896]{2,1,0:T(8,128)(2,1)} %get-tuple-element.68), channel_id=1, source_target_pairs={{0,8},{1,9},{2,10},{3,11},{4,12},{5,13},{6,14},{7,15},{8,16},{9,17... | collective-permute-start | bytes 2064392 | tf_op jit(solution)/shard_map/ppermute | solution.py:335
  104.2 61.8 %collective-permute-start.8 = (bf16[48,8,896]{2,1,0:T(8,128)(2,1)}, bf16[48,8,896]{2,1,0:T(8,128)(2,1)S(1)}, u32[]{:S(2)}, u32[]{:S(2)}) collective-permute-start(bf16[48,8,896]{2,1,0:T(8,128)(2,1)} %get-tuple-element.69), channel_id=1, source_target_pairs={{0,16},{1,17},{2,18},{3,19},{4,20},{5,21},{6,22},{7,23},{8,24},{9,... | collective-permute-start | bytes 2064392 | tf_op jit(solution)/shard_map/ppermute | solution.py:335
  105.5 63.3 %collective-permute-start.9 = (bf16[48,8,896]{2,1,0:T(8,128)(2,1)}, bf16[48,8,896]{2,1,0:T(8,128)(2,1)}, u32[]{:S(2)}, u32[]{:S(2)}) collective-permute-start(bf16[48,8,896]{2,1,0:T(8,128)(2,1)} %get-tuple-element.70), channel_id=1, source_target_pairs={{0,24},{1,25},{2,26},{3,27},{4,28},{5,29},{6,30},{7,31},{8,0},{9,1... | collective-permute-start | bytes 2064392 | tf_op jit(solution)/shard_map/ppermute | solution.py:335
  119.2 54.4 %all-to-all-start.5 = ((bf16[16,8,1024]{2,1,0:T(8,128)(2,1)}), bf16[16,8,1024]{2,1,0:T(8,128)(2,1)S(1)}, u32[]{:S(2)}, u32[]{:S(2)}) async-start(bf16[16,8,1024]{2,1,0:T(8,128)(2,1)} %bitcast.31), calls=%async_computation.5 | async-start | bytes 524288 | tf_op jit(solution)/shard_map/all_to_all | solution.py:399
  126.5 42.4 %copy-start.6 = (bf16[48,8,896]{2,1,0:T(8,128)(2,1)}, bf16[48,8,896]{2,1,0:T(8,128)(2,1)S(1)}, u32[]{:S(2)}) copy-start(bf16[48,8,896]{2,1,0:T(8,128)(2,1)S(1)} %collective-permute-done.7.refs_1_) | copy-start | bytes 2064388
  166.0 2.9 copy-start.7
  173.7 0.7 copy-start.1
  173.7 5.7 %copy-start.12 = (s32[192]{0:T(256)S(1)}, s32[192]{0:T(256)}, u32[]{:S(2)}) copy-start(s32[192]{0:T(256)} %reduce_sum.70.index_ref) | copy-start | bytes 2308
  174.4 77.1 %all-to-all-start.6 = ((bf16[256,8,896]{2,1,0:T(8,128)(2,1)}), bf16[256,8,896]{2,1,0:T(8,128)(2,1)}, u32[]{:S(2)}, u32[]{:S(2)}) async-start(bf16[256,8,896]{2,1,0:T(8,128)(2,1)} %bitcast.67), calls=%async_computation.6 | async-start | bytes 7340032 | tf_op jit(solution)/shard_map/all_to_all | solution.py:321
  184.1 16.9 %collective-permute-start.10 = (bf16[48,8,896]{2,1,0:T(8,128)(2,1)}, bf16[48,8,896]{2,1,0:T(8,128)(2,1)S(1)}, u32[]{:S(2)}, u32[]{:S(2)}) collective-permute-start(bf16[48,8,896]{2,1,0:T(8,128)(2,1)} %get-tuple-element.72), channel_id=1, source_target_pairs={{0,8},{1,9},{2,10},{3,11},{4,12},{5,13},{6,14},{7,15},{8,16},{9,17... | collective-permute-start | bytes 2064392 | tf_op jit(solution)/shard_map/ppermute | solution.py:335
  184.1 59.2 %collective-permute-start.11 = (bf16[48,8,896]{2,1,0:T(8,128)(2,1)}, bf16[48,8,896]{2,1,0:T(8,128)(2,1)S(1)}, u32[]{:S(2)}, u32[]{:S(2)}) collective-permute-start(bf16[48,8,896]{2,1,0:T(8,128)(2,1)} %get-tuple-element.73), channel_id=1, source_target_pairs={{0,16},{1,17},{2,18},{3,19},{4,20},{5,21},{6,22},{7,23},{8,24},{9,... | collective-permute-start | bytes 2064392 | tf_op jit(solution)/shard_map/ppermute | solution.py:335
  186.3 60.5 %collective-permute-start.12 = (bf16[48,8,896]{2,1,0:T(8,128)(2,1)}, bf16[48,8,896]{2,1,0:T(8,128)(2,1)}, u32[]{:S(2)}, u32[]{:S(2)}) collective-permute-start(bf16[48,8,896]{2,1,0:T(8,128)(2,1)} %get-tuple-element.74), channel_id=1, source_target_pairs={{0,24},{1,25},{2,26},{3,27},{4,28},{5,29},{6,30},{7,31},{8,0},{9,1... | collective-permute-start | bytes 2064392 | tf_op jit(solution)/shard_map/ppermute | solution.py:335
  201.1 45.8 %copy-start.8 = (bf16[48,8,896]{2,1,0:T(8,128)(2,1)}, bf16[48,8,896]{2,1,0:T(8,128)(2,1)S(1)}, u32[]{:S(2)}) copy-start(bf16[48,8,896]{2,1,0:T(8,128)(2,1)S(1)} %collective-permute-done.10.refs_1_) | copy-start | bytes 2064388
  243.4 3.4 copy-start.9
  251.6 108.1 %all-to-all-start.7 = ((bf16[256,8,896]{2,1,0:T(8,128)(2,1)}), bf16[256,8,896]{2,1,0:T(8,128)(2,1)}, u32[]{:S(2)}, u32[]{:S(2)}) async-start(bf16[256,8,896]{2,1,0:T(8,128)(2,1)} %bitcast.66), calls=%async_computation.7 | async-start | bytes 7340032 | tf_op jit(solution)/shard_map/all_to_all | solution.py:321
  256.5 81.3 %collective-permute-start.13 = (bf16[8,16,8,896]{3,2,1,0:T(8,128)(2,1)}, bf16[8,16,8,896]{3,2,1,0:T(8,128)(2,1)}, u32[]{:S(2)}, u32[]{:S(2)}) collective-permute-start(bf16[8,16,8,896]{3,2,1,0:T(8,128)(2,1)} %get-tuple-element.78.refs_0_), channel_id=1, source_target_pairs={{0,1},{1,0},{2,3},{3,2},{4,5},{5,4},{6,7},{7,6},{8,9},{9,8},{10,11... | collective-permute-start | bytes 5505032 | tf_op jit(solution)/shard_map/ppermute | solution.py:359
  359.7 61.9 %all-to-all-start.8 = ((f32[16,8,1152]{2,1,0:T(8,128)}), f32[16,8,1152]{2,1,0:T(8,128)S(1)}, u32[]{:S(2)}, u32[]{:S(2)}) async-start(f32[16,8,1152]{2,1,0:T(8,128)} %bitcast.75), calls=%async_computation.8 | async-start | bytes 1179648 | tf_op jit(solution)/shard_map/all_to_all | solution.py:462
  421.6 0.9 copy-start
Sparse Core Ops, SparseCore 0:
  48.8 48.3 all-gather.1

commit v4 on v3

--- a/solution.py
+++ b/solution.py
@@ -158,14 +158,14 @@
 
 def gather_body(index_ref, *refs, count):
     sources, out_ref, stage_ref, sem_ref = refs[:count], refs[count], refs[count + 1], refs[count + 2]
-    size = sources[0].shape[0]
     copies, wanted = out_ref.shape[1:3]
+    starts = [sum(s.shape[0] for s in sources[:k]) for k in range(count)]
     base = pl.program_id(0) * wanted
 
     @pl.when(pl.program_id(0) == 0)
     def _():
         moves = [
-            pltpu.make_async_copy(source, stage_ref.at[pl.ds(k * size, size)], sem_ref.at[k])
+            pltpu.make_async_copy(source, stage_ref.at[pl.ds(starts[k], source.shape[0])], sem_ref.at[k])
             for k, source in enumerate(sources)
         ]
         for move in moves:
@@ -184,7 +184,7 @@
 
 def gather_rows(index, sources, groups, copies):
     wanted = index.shape[0] // groups
-    size, piece, width = sources[0].shape
+    piece, width = sources[0].shape[1:]
     out = pl.pallas_call(
         functools.partial(gather_body, count=len(sources)),
         out_shape=jax.ShapeDtypeStruct((groups, copies, wanted, piece, width), sources[0].dtype),
@@ -194,7 +194,7 @@
             in_specs=[pl.BlockSpec(memory_space=pl.ANY) for _ in sources],
             out_specs=pl.BlockSpec((1, copies, wanted, piece, width), lambda i, s: (i, 0, 0, 0, 0)),
             scratch_shapes=[
-                pltpu.VMEM((len(sources) * size, piece, width), sources[0].dtype),
+                pltpu.VMEM((sum(s.shape[0] for s in sources), piece, width), sources[0].dtype),
                 pltpu.SemaphoreType.DMA((len(sources),)),
             ],
         ),
@@ -350,6 +350,25 @@
     first, _ = lax.optimization_barrier((early_half.reshape(lanes * held, piece, width), table))
     first = swap(first, plane_groups)
 
+    odd_shard = table_shard[:, :, 1].reshape(shards, wanted)
+    odd_row = table_row[:, :, 1].reshape(shards, wanted)
+    earlier = jnp.arange(wanted)
+    same = (odd_shard[:, :, None] == odd_shard[:, None, :]) & (earlier[None, None, :] < earlier[None, :, None])
+    odd_rank = jnp.sum(same.astype(jnp.int32), axis=2)
+    arriving = (odd_shard == db_index)[:, None, :] & (
+        odd_rank[:, None, :] == jnp.arange(capacity, dtype=jnp.int32)[None, :, None]
+    )
+    slot_row = jnp.sum(jnp.where(arriving, odd_row[:, None, :] + 1, 0), axis=2) - 1
+    my_slot = lax.dynamic_index_in_dim(odd_shard * capacity + odd_rank, db_index, 0, keepdims=False)
+    slots = jnp.arange(shards * capacity, dtype=jnp.int32)
+    chosen = my_slot[None, :] == slots[:, None]
+    sender = jnp.sum(jnp.where(chosen, (earlier // neighbours).astype(jnp.int32)[None, :], 0), axis=1)
+    last_rows = queries.reshape(sequences, SEQ, columns)[:, SEQ - 1]
+    odd_query = jnp.take(last_rows, sender, axis=0, mode="clip").reshape(shards, capacity, columns)
+    odd_query, _ = lax.optimization_barrier((odd_query, first))
+    odd_query = lax.all_to_all(odd_query, "db", 0, 0, tiled=True)
+    odd_query = odd_query.reshape(shards * capacity, columns)
+
     part_index = lax.axis_index("mp")
 
     def share(half, after):
@@ -359,7 +378,7 @@
             shared.append(lax.ppermute(half, "mp", [(m, (m + k) % parts) for m in range(parts)]))
         return shared
 
-    late_shared = share(late_half, first)
+    late_shared = share(late_half, table)
     second = [
         lax.dynamic_index_in_dim(
             half.reshape(group, parts, held, piece, width), part_index, 1, keepdims=False
@@ -370,7 +389,7 @@
     part_groups = [
         [a * lanes + g * parts + m for g in range(group)] for a in range(planes) for m in range(parts)
     ]
-    second, _ = lax.optimization_barrier((second, first))
+    second, _ = lax.optimization_barrier((second, odd_query))
     if group > 1:
         second = swap(second, part_groups)
     early_shared = share(early_half, late_shared)
@@ -379,25 +398,6 @@
     def stepped(row):
         step = (part_index + parts - row % shard_rows // held) % parts
         return row // shard_rows * shard_rows + step * held + row % held
-
-    odd_shard = table_shard[:, :, 1].reshape(shards, wanted)
-    odd_row = table_row[:, :, 1].reshape(shards, wanted)
-    earlier = jnp.arange(wanted)
-    same = (odd_shard[:, :, None] == odd_shard[:, None, :]) & (earlier[None, None, :] < earlier[None, :, None])
-    odd_rank = jnp.sum(same.astype(jnp.int32), axis=2)
-    arriving = (odd_shard == db_index)[:, None, :] & (
-        odd_rank[:, None, :] == jnp.arange(capacity, dtype=jnp.int32)[None, :, None]
-    )
-    slot_row = jnp.sum(jnp.where(arriving, odd_row[:, None, :] + 1, 0), axis=2) - 1
-    my_slot = lax.dynamic_index_in_dim(odd_shard * capacity + odd_rank, db_index, 0, keepdims=False)
-    slots = jnp.arange(shards * capacity, dtype=jnp.int32)
-    chosen = my_slot[None, :] == slots[:, None]
-    sender = jnp.sum(jnp.where(chosen, (earlier // neighbours).astype(jnp.int32)[None, :], 0), axis=1)
-    last_rows = queries.reshape(sequences, SEQ, columns)[:, SEQ - 1]
-    odd_query = jnp.take(last_rows, sender, axis=0, mode="clip").reshape(shards, capacity, columns)
-    odd_query, _ = lax.optimization_barrier((odd_query, plane_pieces[-1]))
-    odd_query = lax.all_to_all(odd_query, "db", 0, 0, tiled=True)
-    odd_query = odd_query.reshape(shards * capacity, columns)
 
     even_id = (table_shard[:, :, 0] * shard_rows + table_row[:, :, 0]).reshape(planes, group * wanted)
     ids = jnp.arange(planes * plane_rows, dtype=jnp.int32)
@@ -405,7 +405,10 @@
     below = jnp.arange(plane_rows)
     before = (below[:, None] < below[None, :]).astype(BF16)
     rank = jnp.dot(want.astype(BF16), before, preferred_element_type=F32).astype(jnp.int32)
-    fits = jnp.max(jnp.sum(want.astype(jnp.int32), axis=2)) <= fast
+    loads = jnp.sum(want.astype(jnp.int32), axis=2)
+    if planes <= MOST_SHIFTS:
+        loads = jnp.where(jnp.eye(planes, dtype=jnp.bool_), 0, loads)
+    fits = jnp.max(loads) <= fast
     mine_want = lax.dynamic_index_in_dim(want, plane_index, 1, keepdims=False)
     mine_rank = lax.dynamic_index_in_dim(rank, plane_index, 1, keepdims=False)
     picks = mine_want[:, None, :] & (
@@ -426,7 +429,7 @@
         rows = stepped(send_rows) if chunk else send_rows
         if planes > MOST_SHIFTS:
             return [jnp.take(source, rows[k], axis=0, mode="clip") for k in range(planes)]
-        return select_rows(rows, source)
+        return [source, *select_rows(rows[1:], source)]
 
     def whole(source, chunk):
         return [source] * planes
@@ -456,8 +459,14 @@
         early = [project(e, weights) for e in early]
         return even_attention(queries, late, weights, early), late
 
+    own_rows = [my_ids % plane_rows, stepped(my_ids % plane_rows)]
     fast_index = my_step * fast + jnp.minimum(place, fast - 1)
-    result, last = attend(exact, [fast_index] * CHUNKS)
+    fast_index = [fast_index] * CHUNKS
+    if planes <= MOST_SHIFTS:
+        fast_index = [
+            jnp.where(my_step == 0, row, index + plane_rows - fast) for row, index in zip(own_rows, fast_index)
+        ]
+    result, last = attend(exact, fast_index)
     odd_part, _ = lax.optimization_barrier((odd_part, last))
     odd_part = lax.all_to_all(odd_part.reshape(shards, capacity, columns + DH), "db", 0, 0, tiled=True)
     odd_part = odd_part.reshape(shards * capacity, columns + DH)
@@ -466,9 +475,7 @@
         result = lax.cond(
             fits,
             lambda done: done,
-            lambda done: attend(
-                whole, [my_step * plane_rows + row for row in (my_ids % plane_rows, stepped(my_ids % plane_rows))]
-            )[0],
+            lambda done: attend(whole, [my_step * plane_rows + row for row in own_rows])[0],
             result,
         )
     return patch(my_slot, result, odd_part)

time: 436 us -> 449 us (1.030)
  waiting for transfers between devices: 207 us -> 244 us
  blocking collectives: 26.5 us -> 0 us
    ppermute x6, waiting for transfers between devices: 101 us -> 138 us  [across(): moved.append(lax.ppermute(blocks[k], BOTH, pairs))]
    all_to_all x1 -> x0, blocking collectives: 26.5 us -> none  [swap(): return lax.all_to_all(x, BOTH, 0, 0, axis_index_groups=groups, tiled=True)]
    all_to_all x3 -> x4, waiting for transfers between devices: 10.9 us -> 17.1 us  [swap(): return lax.all_to_all(x, BOTH, 0, 0, axis_index_groups=groups, tiled=True)]
    ppermute x2, waiting for transfers between devices: 94.4 us -> 88.4 us  [share(): lax.ppermute(half, 'mp', [(m, (m + k) % parts) for m in range(parts)])]
    all_to_all x3 -> x4, starting transfers between devices: 16.1 us -> 19.1 us  [swap(): return lax.all_to_all(x, BOTH, 0, 0, axis_index_groups=groups, tiled=True)]
  transfers between devices with their start and end apart: 15 -> 16, of which waited for: 8 -> 9; matrix products, arithmetic and copies ran while one was open for 5% -> 5% of each run, Pallas kernels for 26% -> 25%
where the time goes in v4:
time: 449 us; the launch traced here: 447 us
  waiting for transfers between devices  244 us (54%)
  Pallas kernels  118 us (26%)
  starting transfers between devices  46.1 us (10%)
  local copies, waits for them, and re-layouts  19.4 us (4%)
  between operations  14.3 us (3%)
  other arithmetic  5.73 us (1%)
    ppermute x6, waiting for transfers between devices, across(): moved.append(lax.ppermute(blocks[k], BOTH, pairs))  138 us
    ppermute x2, waiting for transfers between devices, share(): lax.ppermute(half, 'mp', [(m, (m + k) % parts) for m in range(parts)])  88.4 us
    pallas_call x1, Pallas kernels, even_attention(): pl.pallas_call(functools.partial(even_body, per_step=per_step, neighbours...  42.4 us
    pallas_call x2, Pallas kernels, odd_attention(): pl.pallas_call(odd_body, out_shape=jax.ShapeDtypeStruct(prior.shape, F32)...  42.4 us
    all_to_all x4, starting transfers between devices, swap(): return lax.all_to_all(x, BOTH, 0, 0, axis_index_groups=groups, tiled=True)  19.1 us
    all_to_all x4, waiting for transfers between devices, swap(): return lax.all_to_all(x, BOTH, 0, 0, axis_index_groups=groups, tiled=True)  17.1 us
    pallas_call x1, Pallas kernels, project(): pl.pallas_call(project_body, out_shape=jax.ShapeDtypeStruct((count * toke...  13.1 us
    pallas_call x2, Pallas kernels, gather_rows(): pl.pallas_call(functools.partial(gather_body, count=len(sources)), out_sh...  9.78 us
  transfers between devices with their start and end apart: 16, of which 9 were waited for; matrix products, arithmetic and copies ran while one was open for 5% of the time, Pallas kernels for 25%

profile of v4, /device:TPU:11, one launch (start us, length us, event | category | flops | bytes accessed | tf_op | source)
XLA Modules:
  0.0 447.4 jit_solution(3958416519349160943)
XLA Ops:
  6.5 0.8 copy.57
  7.3 0.1 reshape.203
  7.4 0.8 copy.58
  8.2 0.1 reshape.204
  8.3 0.6 broadcast_in_dim.117
  9.0 6.5 %all-to-all-start.2 = ((s32[16,1,128]{2,1,0:T(1,128)}), s32[16,1,128]{2,1,0:T(1,128)S(1)}, u32[]{:S(2)}, u32[]{:S(2)}) async-start(s32[16,1,128]{2,1,0:T(1,128)} %broadcast_in_dim.117), calls=%async_computation.2 | async-start | bytes 16384 | tf_op jit(solution)/shard_map/all_to_all | solution.py:340
  15.5 2.6 copy.79
  18.1 3.0 slice_bitcast_fusion.1
  21.2 4.3 all-to-all-start.3
  25.4 1.2 collective-permute-start.6
  26.6 1.0 slice.43
  28.1 0.2 copy.66
  28.3 0.1 add.169
  28.4 0.5 convert_reduce_fusion
  29.0 1.6 gather_fusion
  30.6 17.1 %all-to-all-done.3.source_ref.refs_0_ = bf16[128,8,896]{2,1,0:T(8,128)(2,1)S(1)} async-done(((bf16[128,8,896]{2,1,0:T(8,128)(2,1)}), bf16[128,8,896]{2,1,0:T(8,128)(2,1)S(1)}, u32[]{:S(2)}, u32[]{:S(2)}) %all-to-all-start.3) | async-done | bytes 1835040 | tf_op jit(solution)/shard_map/all_to_all | solution.py:321
  47.7 6.0 %all-to-all-start.4 = ((bf16[16,8,1024]{2,1,0:T(8,128)(2,1)}), bf16[16,8,1024]{2,1,0:T(8,128)(2,1)S(1)}, u32[]{:S(2)}, u32[]{:S(2)}) async-start(bf16[16,8,1024]{2,1,0:T(8,128)(2,1)} %bitcast.24), calls=%async_computation.4 | async-start | bytes 524288 | tf_op jit(solution)/shard_map/all_to_all | solution.py:369
  53.7 0.2 fusion
  53.9 1.3 dynamic-slice_bitcast_fusion.1
  55.2 31.9 %collective-permute-done.6.refs_1_ = bf16[8,16,8,896]{3,2,1,0:T(8,128)(2,1)} collective-permute-done((bf16[8,16,8,896]{3,2,1,0:T(8,128)(2,1)}, bf16[8,16,8,896]{3,2,1,0:T(8,128)(2,1)}, u32[]{:S(2)}, u32[]{:S(2)}) %collective-permute-start.6) | collective-permute-done | bytes 1835040 | tf_op jit(solution)/shard_map/ppermute | solution.py:378
  87.1 1.3 dynamic-slice_bitcast_fusion
  88.3 1.4 pad_maximum_fusion
  89.8 0.7 copy-done.1
  90.5 5.0 %all-to-all-start.5 = ((bf16[128,8,896]{2,1,0:T(8,128)(2,1)}), bf16[128,8,896]{2,1,0:T(8,128)(2,1)}, u32[]{:S(2)}, u32[]{:S(2)}) async-start(bf16[128,8,896]{2,1,0:T(8,128)(2,1)} %bitcast.72), calls=%async_computation.5 | async-start | bytes 3670016 | tf_op jit(solution)/shard_map/all_to_all | solution.py:321
  95.5 0.1 convolution_convert_fusion
  95.7 0.1 select_reduce_fusion.1
  95.9 0.7 reshape.215.index_ref
  96.6 2.3 select_rows.3
  98.9 1.2 collective-permute-start.7
  100.1 1.4 collective-permute-start.8
  101.5 1.0 collective-permute-start.9
  102.5 0.7 pad_maximum_fusion.1
  103.3 0.2 select_reduce_fusion
  103.4 0.5 compare_select_fusion.12
  104.0 14.3 %collective-permute-done.7.refs_1_ = bf16[48,8,896]{2,1,0:T(8,128)(2,1)S(1)} collective-permute-done((bf16[48,8,896]{2,1,0:T(8,128)(2,1)}, bf16[48,8,896]{2,1,0:T(8,128)(2,1)S(1)}, u32[]{:S(2)}, u32[]{:S(2)}) %collective-permute-start.7) | collective-permute-done | bytes 688160 | tf_op jit(solution)/shard_map/ppermute | solution.py:335
  118.3 59.9 %collective-permute-done.8.refs_2_ = bf16[48,8,896]{2,1,0:T(8,128)(2,1)S(1)} collective-permute-done((bf16[48,8,896]{2,1,0:T(8,128)(2,1)}, bf16[48,8,896]{2,1,0:T(8,128)(2,1)S(1)}, u32[]{:S(2)}, u32[]{:S(2)}) %collective-permute-start.8) | collective-permute-done | bytes 688160 | tf_op jit(solution)/shard_map/ppermute | solution.py:335
  178.2 5.2 %collective-permute-done.9.refs_3_ = bf16[48,8,896]{2,1,0:T(8,128)(2,1)} collective-permute-done((bf16[48,8,896]{2,1,0:T(8,128)(2,1)}, bf16[48,8,896]{2,1,0:T(8,128)(2,1)}, u32[]{:S(2)}, u32[]{:S(2)}) %collective-permute-start.9) | collective-permute-done | bytes 688160 | tf_op jit(solution)/shard_map/ppermute | solution.py:335
  183.4 4.7 %gather_rows.7 = bf16[4,2,32,8,896]{4,3,2,1,0:T(8,128)(2,1)} custom-call(s32[128]{0:T(128)} %get-tuple-element.78.index_ref, bf16[128,8,896]{2,1,0:T(8,128)(2,1)S(1)} %all-to-all-done.3.source_ref.refs_0_, bf16[48,8,896]{2,1,0:T(8,128)(2,1)} %copy-done.6, bf16[48,8,896]{2,1,0:T(8,128)(2,1)} %copy-done.7, bf16[48,8,896]{2,1,0:T(8,128)(2,1)} %collective-permute-done.9.refs_3_), custom_call_target="tpu_custom_call" | custom-call | tf_op jit(solution)/shard_map/gather_rows/pallas_call | solution.py:188
  188.1 4.9 %all-to-all-start.6 = ((bf16[256,8,896]{2,1,0:T(8,128)(2,1)}), bf16[256,8,896]{2,1,0:T(8,128)(2,1)}, u32[]{:S(2)}, u32[]{:S(2)}) async-start(bf16[256,8,896]{2,1,0:T(8,128)(2,1)} %bitcast.68), calls=%async_computation.6 | async-start | bytes 7340032 | tf_op jit(solution)/shard_map/all_to_all | solution.py:321
  193.1 0.6 reshape.214.index_ref
  193.7 3.8 select_rows.2
  197.5 2.2 collective-permute-start.11
  199.7 1.5 collective-permute-start.12
  201.1 0.5 compare_select_fusion.13
  201.6 12.8 %collective-permute-done.10.refs_1_ = bf16[48,8,896]{2,1,0:T(8,128)(2,1)S(1)} collective-permute-done((bf16[48,8,896]{2,1,0:T(8,128)(2,1)}, bf16[48,8,896]{2,1,0:T(8,128)(2,1)S(1)}, u32[]{:S(2)}, u32[]{:S(2)}) %collective-permute-start.10) | collective-permute-done | bytes 688160 | tf_op jit(solution)/shard_map/ppermute | solution.py:335
  214.4 42.3 %collective-permute-done.11.refs_2_ = bf16[48,8,896]{2,1,0:T(8,128)(2,1)S(1)} collective-permute-done((bf16[48,8,896]{2,1,0:T(8,128)(2,1)}, bf16[48,8,896]{2,1,0:T(8,128)(2,1)S(1)}, u32[]{:S(2)}, u32[]{:S(2)}) %collective-permute-start.11) | collective-permute-done | bytes 688160 | tf_op jit(solution)/shard_map/ppermute | solution.py:335
  256.7 3.4 collective-permute-done.12.refs_3_
  260.2 5.1 %gather_rows.6 = bf16[4,2,32,8,896]{4,3,2,1,0:T(8,128)(2,1)} custom-call(s32[128]{0:T(128)} %get-tuple-element.81.index_ref, bf16[128,8,896]{2,1,0:T(8,128)(2,1)} %all-to-all-done.5.source_ref.refs_0_, bf16[48,8,896]{2,1,0:T(8,128)(2,1)} %copy-done.8, bf16[48,8,896]{2,1,0:T(8,128)(2,1)} %copy-done.9, bf16[48,8,896]{2,1,0:T(8,128)(2,1)} %collective-permute-done.12.refs_3_), custom_call_target="tpu_custom_call" | custom-call | tf_op jit(solution)/shard_map/gather_rows/pallas_call | solution.py:188
  265.3 4.9 %all-to-all-start.7 = ((bf16[256,8,896]{2,1,0:T(8,128)(2,1)}), bf16[256,8,896]{2,1,0:T(8,128)(2,1)}, u32[]{:S(2)}, u32[]{:S(2)}) async-start(bf16[256,8,896]{2,1,0:T(8,128)(2,1)} %bitcast.67), calls=%async_computation.7 | async-start | bytes 7340032 | tf_op jit(solution)/shard_map/all_to_all | solution.py:321
  270.2 1.2 collective-permute-start.13
  271.6 0.4 select_reduce_fusion.2
  272.2 0.7 broadcast_in_dim.133.want_ref
  272.9 0.9 broadcast_in_dim.134.refs_3_
  273.8 21.2 %odd_attention.2.refs_3_ = f32[128,1152]{1,0:T(8,128)} custom-call(bf16[128,1024]{1,0:T(8,128)(2,1)} %bitcast.77, s32[128,128]{1,0:T(8,128)} %broadcast_in_dim.133.want_ref, bf16[8,16,8,896]{3,2,1,0:T(8,128)(2,1)} %get-tuple-element.74.refs_0_, bf16[8,16,8,896]{3,2,1,0:T(8,128)(2,1)} %get-tuple-element.59.refs_1_, ...), custom_call_target="tpu_custom_call" | custom-call | tf_op jit(solution)/shard_map/odd_attention/pallas_call | solution.py:282
  295.0 56.5 %collective-permute-done.13.refs_0_ = bf16[8,16,8,896]{3,2,1,0:T(8,128)(2,1)} collective-permute-done((bf16[8,16,8,896]{3,2,1,0:T(8,128)(2,1)}, bf16[8,16,8,896]{3,2,1,0:T(8,128)(2,1)}, u32[]{:S(2)}, u32[]{:S(2)}) %collective-permute-start.13) | collective-permute-done | bytes 1835040 | tf_op jit(solution)/shard_map/ppermute | solution.py:378
  351.5 0.7 broadcast_in_dim.132.want_ref
  352.2 21.2 %odd_attention.3 = f32[128,1152]{1,0:T(8,128)} custom-call(bf16[128,1024]{1,0:T(8,128)(2,1)} %bitcast.78, s32[128,128]{1,0:T(8,128)} %broadcast_in_dim.132.want_ref, bf16[8,16,8,896]{3,2,1,0:T(8,128)(2,1)} %collective-permute-done.13.refs_0_, bf16[8,16,8,896]{3,2,1,0:T(8,128)(2,1)} %collective-permute-done.6.refs_1_, ...), custom_call_target="tpu_custom_call" | custom-call | tf_op jit(solution)/shard_map/odd_attention/pallas_call | solution.py:282
  373.4 4.9 %all-to-all-start.8 = ((f32[16,8,1152]{2,1,0:T(8,128)}), f32[16,8,1152]{2,1,0:T(8,128)S(1)}, u32[]{:S(2)}, u32[]{:S(2)}) async-start(f32[16,8,1152]{2,1,0:T(8,128)} %bitcast.76), calls=%async_computation.8 | async-start | bytes 1179648 | tf_op jit(solution)/shard_map/all_to_all | solution.py:471
  378.2 0.1 convert_reduce_fusion.1
  378.4 0.6 select_reduce_fusion.5
  379.7 13.1 %project.3.refs_0_ = bf16[2048,2048]{1,0:T(8,128)(2,1)} custom-call(bf16[8,32,8,896]{3,2,1,0:T(8,128)(2,1)} %bitcast.34.rows_ref, bf16[896,2048]{1,0:T(8,128)(2,1)} %all-gather.2.cloned.1.call-done.weight_ref.refs_2_), custom_call_target="tpu_custom_call" | custom-call | tf_op jit(solution)/shard_map/project/pallas_call | solution.py:38
  392.8 42.4 %even_attention.3 = bf16[2048,1024]{1,0:T(8,128)(2,1)} custom-call(bf16[2048,1024]{1,0:T(8,128)(2,1)} %query_ref.1, bf16[8,32,8,896]{3,2,1,0:T(8,128)(2,1)} %bitcast.33.rows_ref, bf16[896,2048]{1,0:T(8,128)(2,1)} %all-gather.2.cloned.1.call-done.weight_ref.refs_2_, bf16[2048,2048]{1,0:T(8,128)(2,1)} %project.3.refs_0_), custom_call_target="tpu_custom_call" | custom-call | tf_op jit(solution)/shard_map/even_attention/pallas_call | solution.py:92
  435.3 0.9 copy-done
  436.1 4.4 patch.1
  (59 shorter events, 1.4 us)
Async XLA Ops:
  9.0 12.1 %all-to-all-start.2 = ((s32[16,1,128]{2,1,0:T(1,128)}), s32[16,1,128]{2,1,0:T(1,128)S(1)}, u32[]{:S(2)}, u32[]{:S(2)}) async-start(s32[16,1,128]{2,1,0:T(1,128)} %broadcast_in_dim.117), calls=%async_computation.2 | async-start | bytes 16384 | tf_op jit(solution)/shard_map/all_to_all | solution.py:340
  21.2 26.5 %all-to-all-start.3 = ((bf16[128,8,896]{2,1,0:T(8,128)(2,1)}), bf16[128,8,896]{2,1,0:T(8,128)(2,1)S(1)}, u32[]{:S(2)}, u32[]{:S(2)}) async-start(bf16[128,8,896]{2,1,0:T(8,128)(2,1)} %bitcast.73), calls=%async_computation.3 | async-start | bytes 3670016 | tf_op jit(solution)/shard_map/all_to_all | solution.py:321
  25.4 61.7 %collective-permute-start.6 = (bf16[8,16,8,896]{3,2,1,0:T(8,128)(2,1)}, bf16[8,16,8,896]{3,2,1,0:T(8,128)(2,1)}, u32[]{:S(2)}, u32[]{:S(2)}) collective-permute-start(bf16[8,16,8,896]{3,2,1,0:T(8,128)(2,1)} %get-tuple-element.59.refs_1_), channel_id=1, source_target_pairs={{0,1},{1,0},{2,3},{3,2},{4,5},{5,4},{6,7},{7,6},{8,9},{9,8},{10,11... | collective-permute-start | bytes 5505032 | tf_op jit(solution)/shard_map/ppermute | solution.py:378
  28.9 26.3 %copy-start.12 = (s32[32]{0:T(128)}, s32[32]{0:T(128)S(1)}, u32[]{:S(2)}) copy-start(s32[32]{0:T(128)S(1)} %fusion.20.slot_ref) | copy-start | bytes 388
  47.7 42.1 %all-to-all-start.4 = ((bf16[16,8,1024]{2,1,0:T(8,128)(2,1)}), bf16[16,8,1024]{2,1,0:T(8,128)(2,1)S(1)}, u32[]{:S(2)}, u32[]{:S(2)}) async-start(bf16[16,8,1024]{2,1,0:T(8,128)(2,1)} %bitcast.24), calls=%async_computation.4 | async-start | bytes 524288 | tf_op jit(solution)/shard_map/all_to_all | solution.py:369
  89.8 0.7 copy-start.1
  90.5 97.6 %all-to-all-start.5 = ((bf16[128,8,896]{2,1,0:T(8,128)(2,1)}), bf16[128,8,896]{2,1,0:T(8,128)(2,1)}, u32[]{:S(2)}, u32[]{:S(2)}) async-start(bf16[128,8,896]{2,1,0:T(8,128)(2,1)} %bitcast.72), calls=%async_computation.5 | async-start | bytes 3670016 | tf_op jit(solution)/shard_map/all_to_all | solution.py:321
  95.5 7.0 %copy-start.10 = (bf16[56,1024]{1,0:T(8,128)(2,1)S(1)}, bf16[56,1024]{1,0:T(8,128)(2,1)}, u32[]{:S(2)}) copy-start(bf16[56,1024]{1,0:T(8,128)(2,1)} %param.11) | copy-start | bytes 344068
  95.5 7.0 %copy-start.11 = (bf16[56,1024]{1,0:T(8,128)(2,1)S(1)}, bf16[56,1024]{1,0:T(8,128)(2,1)}, u32[]{:S(2)}) copy-start(bf16[56,1024]{1,0:T(8,128)(2,1)} %param.10) | copy-start | bytes 344068
  95.5 176.7 %all-gather.2.cloned.1.call-start = ((), (), s32[]{:S(2)}) async-start(), calls=%async_computation.9 | async-start | bytes 3899392 | tf_op jit(solution)/shard_map/all_gather | solution.py:345
  98.9 19.4 %collective-permute-start.7 = (bf16[48,8,896]{2,1,0:T(8,128)(2,1)}, bf16[48,8,896]{2,1,0:T(8,128)(2,1)S(1)}, u32[]{:S(2)}, u32[]{:S(2)}) collective-permute-start(bf16[48,8,896]{2,1,0:T(8,128)(2,1)} %get-tuple-element.65), channel_id=1, source_target_pairs={{0,8},{1,9},{2,10},{3,11},{4,12},{5,13},{6,14},{7,15},{8,16},{9,17... | collective-permute-start | bytes 2064392 | tf_op jit(solution)/shard_map/ppermute | solution.py:335
  100.1 78.0 %collective-permute-start.8 = (bf16[48,8,896]{2,1,0:T(8,128)(2,1)}, bf16[48,8,896]{2,1,0:T(8,128)(2,1)S(1)}, u32[]{:S(2)}, u32[]{:S(2)}) collective-permute-start(bf16[48,8,896]{2,1,0:T(8,128)(2,1)} %get-tuple-element.66), channel_id=1, source_target_pairs={{0,16},{1,17},{2,18},{3,19},{4,20},{5,21},{6,22},{7,23},{8,24},{9,... | collective-permute-start | bytes 2064392 | tf_op jit(solution)/shard_map/ppermute | solution.py:335
  101.5 81.9 %collective-permute-start.9 = (bf16[48,8,896]{2,1,0:T(8,128)(2,1)}, bf16[48,8,896]{2,1,0:T(8,128)(2,1)}, u32[]{:S(2)}, u32[]{:S(2)}) collective-permute-start(bf16[48,8,896]{2,1,0:T(8,128)(2,1)} %get-tuple-element.67), channel_id=1, source_target_pairs={{0,24},{1,25},{2,26},{3,27},{4,28},{5,29},{6,30},{7,31},{8,0},{9,1... | collective-permute-start | bytes 2064392 | tf_op jit(solution)/shard_map/ppermute | solution.py:335
  118.3 65.1 %copy-start.6 = (bf16[48,8,896]{2,1,0:T(8,128)(2,1)}, bf16[48,8,896]{2,1,0:T(8,128)(2,1)S(1)}, u32[]{:S(2)}) copy-start(bf16[48,8,896]{2,1,0:T(8,128)(2,1)S(1)} %collective-permute-done.7.refs_1_) | copy-start | bytes 2064388
  178.1 5.2 %copy-start.7 = (bf16[48,8,896]{2,1,0:T(8,128)(2,1)}, bf16[48,8,896]{2,1,0:T(8,128)(2,1)S(1)}, u32[]{:S(2)}) copy-start(bf16[48,8,896]{2,1,0:T(8,128)(2,1)S(1)} %collective-permute-done.8.refs_2_) | copy-start | bytes 2064388
  188.1 77.1 %all-to-all-start.6 = ((bf16[256,8,896]{2,1,0:T(8,128)(2,1)}), bf16[256,8,896]{2,1,0:T(8,128)(2,1)}, u32[]{:S(2)}, u32[]{:S(2)}) async-start(bf16[256,8,896]{2,1,0:T(8,128)(2,1)} %bitcast.68), calls=%async_computation.6 | async-start | bytes 7340032 | tf_op jit(solution)/shard_map/all_to_all | solution.py:321
  197.5 16.9 %collective-permute-start.10 = (bf16[48,8,896]{2,1,0:T(8,128)(2,1)}, bf16[48,8,896]{2,1,0:T(8,128)(2,1)S(1)}, u32[]{:S(2)}, u32[]{:S(2)}) collective-permute-start(bf16[48,8,896]{2,1,0:T(8,128)(2,1)} %get-tuple-element.69), channel_id=1, source_target_pairs={{0,8},{1,9},{2,10},{3,11},{4,12},{5,13},{6,14},{7,15},{8,16},{9,17... | collective-permute-start | bytes 2064392 | tf_op jit(solution)/shard_map/ppermute | solution.py:335
  197.5 59.2 %collective-permute-start.11 = (bf16[48,8,896]{2,1,0:T(8,128)(2,1)}, bf16[48,8,896]{2,1,0:T(8,128)(2,1)S(1)}, u32[]{:S(2)}, u32[]{:S(2)}) collective-permute-start(bf16[48,8,896]{2,1,0:T(8,128)(2,1)} %get-tuple-element.70), channel_id=1, source_target_pairs={{0,16},{1,17},{2,18},{3,19},{4,20},{5,21},{6,22},{7,23},{8,24},{9,... | collective-permute-start | bytes 2064392 | tf_op jit(solution)/shard_map/ppermute | solution.py:335
  199.7 60.5 %collective-permute-start.12 = (bf16[48,8,896]{2,1,0:T(8,128)(2,1)}, bf16[48,8,896]{2,1,0:T(8,128)(2,1)}, u32[]{:S(2)}, u32[]{:S(2)}) collective-permute-start(bf16[48,8,896]{2,1,0:T(8,128)(2,1)} %get-tuple-element.71), channel_id=1, source_target_pairs={{0,24},{1,25},{2,26},{3,27},{4,28},{5,29},{6,30},{7,31},{8,0},{9,1... | collective-permute-start | bytes 2064392 | tf_op jit(solution)/shard_map/ppermute | solution.py:335
  214.4 45.7 %copy-start.8 = (bf16[48,8,896]{2,1,0:T(8,128)(2,1)}, bf16[48,8,896]{2,1,0:T(8,128)(2,1)S(1)}, u32[]{:S(2)}) copy-start(bf16[48,8,896]{2,1,0:T(8,128)(2,1)S(1)} %collective-permute-done.10.refs_1_) | copy-start | bytes 2064388
  256.7 3.4 copy-start.9
  265.3 108.1 %all-to-all-start.7 = ((bf16[256,8,896]{2,1,0:T(8,128)(2,1)}), bf16[256,8,896]{2,1,0:T(8,128)(2,1)}, u32[]{:S(2)}, u32[]{:S(2)}) async-start(bf16[256,8,896]{2,1,0:T(8,128)(2,1)} %bitcast.67), calls=%async_computation.7 | async-start | bytes 7340032 | tf_op jit(solution)/shard_map/all_to_all | solution.py:321
  270.2 81.3 %collective-permute-start.13 = (bf16[8,16,8,896]{3,2,1,0:T(8,128)(2,1)}, bf16[8,16,8,896]{3,2,1,0:T(8,128)(2,1)}, u32[]{:S(2)}, u32[]{:S(2)}) collective-permute-start(bf16[8,16,8,896]{3,2,1,0:T(8,128)(2,1)} %get-tuple-element.74.refs_0_), channel_id=1, source_target_pairs={{0,1},{1,0},{2,3},{3,2},{4,5},{5,4},{6,7},{7,6},{8,9},{9,8},{10,11... | collective-permute-start | bytes 5505032 | tf_op jit(solution)/shard_map/ppermute | solution.py:378
  373.4 61.9 %all-to-all-start.8 = ((f32[16,8,1152]{2,1,0:T(8,128)}), f32[16,8,1152]{2,1,0:T(8,128)S(1)}, u32[]{:S(2)}, u32[]{:S(2)}) async-start(f32[16,8,1152]{2,1,0:T(8,128)} %bitcast.76), calls=%async_computation.8 | async-start | bytes 1179648 | tf_op jit(solution)/shard_map/all_to_all | solution.py:471
  435.3 0.9 copy-start
Sparse Core Ops, SparseCore 0:
  103.3 81.5 all-gather.1

commit v5 on v4

--- a/solution.py
+++ b/solution.py
@@ -15,8 +15,8 @@
 LANES = 8
 CHUNKS = 2
 MOST_SHIFTS = 8
-TAIL = 16
-FAST_SLOTS = 48
+LOW = (SPAN - 1) // 16 * 16
+FAST_SLOTS = 46
 BF16 = jnp.bfloat16
 F32 = jnp.float32
 SCALE = 1.0 / math.sqrt(DH)
@@ -24,136 +24,139 @@
 CONTRACT_LAST = (((1,), (1,)), ((), ()))
 
 
-def project_body(rows_ref, weight_ref, out_ref):
+def project_rows(rows_ref, weight_ref):
     lanes, count, piece, width = rows_ref.shape
     rows = rows_ref[...]
     stacked = jnp.concatenate([rows[:, j].reshape(lanes * piece, width) for j in range(count)], axis=0)
-    out_ref[...] = jnp.dot(stacked, weight_ref[...], preferred_element_type=F32).astype(BF16)
-
-
-def project(rows, weights):
+    return jnp.dot(stacked, weight_ref[...], preferred_element_type=F32).astype(BF16)
+
+
+def attend_head(query, keys, values):
+    scores = lax.dot_general(query, keys, CONTRACT_LAST, preferred_element_type=F32) * SCALE
+    largest = jnp.max(scores, axis=1, keepdims=True)
+    expscore = jnp.exp(scores - largest)
+    total = jnp.sum(expscore, axis=1, keepdims=True)
+    return jnp.dot(expscore.astype(BF16), values, preferred_element_type=F32), largest, total
+
+
+def early_body(query_ref, rows_ref, weight_ref, mixed_ref, stats_ref, *, per_step):
+    columns = query_ref.shape[1]
+    projected = project_rows(rows_ref, weight_ref)
+    span = projected.shape[0] // per_step
+    lane = lax.broadcasted_iota(jnp.int32, (SEQ - LOW, DH), 1)
+    for s in range(per_step):
+        own = projected[s * span : (s + 1) * span]
+        at = slice(s * (SEQ - LOW), (s + 1) * (SEQ - LOW))
+        stats = jnp.zeros((SEQ - LOW, DH), F32)
+        for h in range(columns // DH):
+            lo, hi = h * DH, (h + 1) * DH
+            query = query_ref[s * SEQ + LOW : (s + 1) * SEQ, lo:hi]
+            mixed, largest, total = attend_head(query, own[:, lo:hi], own[:, columns + lo : columns + hi])
+            mixed_ref[at, lo:hi] = mixed
+            stats = jnp.where(lane == h, largest, stats)
+            stats = jnp.where(lane == DH // 2 + h, total, stats)
+        stats_ref[at, :] = stats
+
+
+def late_body(query_ref, rows_ref, weight_ref, mixed_ref, stats_ref, odd_ref, out_ref, *, per_step):
+    columns = query_ref.shape[1]
+    projected = project_rows(rows_ref, weight_ref)
+    span = projected.shape[0] // per_step
+    first = SPAN - 1
+    position = LOW + lax.broadcasted_iota(jnp.int32, (SEQ - LOW, DH), 0)
+    for s in range(per_step):
+        own = projected[s * span : (s + 1) * span]
+        at = slice(s * (SEQ - LOW), (s + 1) * (SEQ - LOW))
+        stats = stats_ref[at, :]
+        odd = odd_ref[pl.ds(pl.program_id(0) * per_step + s, 1), :]
+        out_ref[s * SEQ : s * SEQ + LOW, :] = jnp.zeros((LOW, columns), BF16)
+        for h in range(columns // DH):
+            lo, hi = h * DH, (h + 1) * DH
+            query = query_ref[s * SEQ + LOW : (s + 1) * SEQ, lo:hi]
+            mixed, largest, total = attend_head(query, own[:, lo:hi], own[:, columns + lo : columns + hi])
+            before = stats[:, h : h + 1]
+            top = jnp.maximum(largest, before)
+            here, there = jnp.exp(largest - top), jnp.exp(before - top)
+            under = total * here + stats[:, DH // 2 + h : DH // 2 + h + 1] * there
+            attended = mixed * (here / under) + mixed_ref[at, lo:hi] * (there / under)
+            attended = jnp.where(position == SEQ - 1, odd[:, lo:hi], attended)
+            attended = jnp.where(position < first, 0.0, attended)
+            out_ref[s * SEQ + LOW : (s + 1) * SEQ, lo:hi] = attended.astype(BF16)
+
+
+def even_specs(queries, rows, weights):
+    columns = queries.shape[1]
+    sequences = queries.shape[0] // SEQ
     lanes, count, piece, width = rows.shape
-    per_step = math.gcd(count, 8)
-    tokens = lanes * piece
+    per_step = math.gcd(sequences, 2)
+    specs = [
+        pl.BlockSpec((per_step * SEQ, columns), lambda i: (i, 0)),
+        pl.BlockSpec((lanes, per_step * count // sequences, piece, width), lambda i: (0, i, 0, 0)),
+        pl.BlockSpec(weights.shape, lambda i: (0, 0)),
+    ]
+    halves = [
+        pl.BlockSpec((per_step * (SEQ - LOW), columns), lambda i: (i, 0)),
+        pl.BlockSpec((per_step * (SEQ - LOW), DH), lambda i: (i, 0)),
+    ]
+    return sequences, per_step, specs, halves
+
+
+def early_attention(queries, rows, weights):
+    sequences, per_step, specs, halves = even_specs(queries, rows, weights)
     return pl.pallas_call(
-        project_body,
-        out_shape=jax.ShapeDtypeStruct((count * tokens, weights.shape[1]), BF16),
-        grid=(count // per_step,),
-        in_specs=[
-            pl.BlockSpec((lanes, per_step, piece, width), lambda i: (0, i, 0, 0)),
-            pl.BlockSpec(weights.shape, lambda i: (0, 0)),
+        functools.partial(early_body, per_step=per_step),
+        out_shape=[
+            jax.ShapeDtypeStruct((sequences * (SEQ - LOW), width), F32) for width in (queries.shape[1], DH)
         ],
-        out_specs=pl.BlockSpec((per_step * tokens, weights.shape[1]), lambda i: (i, 0)),
-        name="project",
-    )(rows, weights)
-
-
-def even_body(query_ref, rows_ref, weight_ref, *refs, per_step, neighbours):
-    early_refs, out_ref = refs[:-1], refs[-1]
-    columns = query_ref.shape[1]
-    heads = columns // DH
-    lanes, _, piece, width = rows_ref.shape
-    tokens = lanes * piece
-    first = SPAN - 1
-    low = first // 16 * 16
-    rows = rows_ref[...]
-    stacked = jnp.concatenate(
-        [rows[:, j].reshape(tokens, width) for j in range(per_step * neighbours)], axis=0
-    )
-    late = jnp.dot(stacked, weight_ref[...], preferred_element_type=F32).astype(BF16)
-    position = low + lax.broadcasted_iota(jnp.int32, (SEQ - low, DH), 0)
-    span = neighbours * tokens
-    for s in range(per_step):
-        out_ref[s * SEQ : s * SEQ + low, :] = jnp.zeros((low, columns), BF16)
-        for h in range(heads):
-            lo, hi = h * DH, (h + 1) * DH
-            parts = [(r, s * span, span) for r in (*early_refs, late)]
-            keys = jnp.concatenate([r[b : b + n, lo:hi] for r, b, n in parts], axis=0)
-            values = jnp.concatenate([r[b : b + n, columns + lo : columns + hi] for r, b, n in parts], axis=0)
-            query = query_ref[s * SEQ + low : (s + 1) * SEQ, lo:hi]
-            scores = lax.dot_general(query, keys, CONTRACT_LAST, preferred_element_type=F32) * SCALE
-            largest = jnp.max(scores, axis=1, keepdims=True)
-            expscore = jnp.exp(scores - largest)
-            total = jnp.sum(expscore, axis=1, keepdims=True)
-            mixed = jnp.dot(expscore.astype(BF16), values, preferred_element_type=F32)
-            attended = mixed / total
-            attended = jnp.where(position < first, 0.0, attended)
-            out_ref[s * SEQ + low : (s + 1) * SEQ, lo:hi] = attended.astype(BF16)
-
-
-def even_attention(queries, rows, weights, early):
-    tokens, columns = queries.shape
-    sequences = tokens // SEQ
-    lanes, count, piece, width = rows.shape
-    neighbours = count // sequences
-    per_step = math.gcd(sequences, 2)
-    early_rows = lanes * piece * per_step * neighbours
-    early_spec = pl.BlockSpec((early_rows, weights.shape[1]), lambda i: (i, 0))
+        grid=(sequences // per_step,),
+        in_specs=specs,
+        out_specs=halves,
+        name="early_attention",
+    )(queries, rows, weights)
+
+
+def late_attention(queries, rows, weights, mixed, stats, odd):
+    sequences, per_step, specs, halves = even_specs(queries, rows, weights)
     return pl.pallas_call(
-        functools.partial(even_body, per_step=per_step, neighbours=neighbours),
+        functools.partial(late_body, per_step=per_step),
         out_shape=jax.ShapeDtypeStruct(queries.shape, BF16),
         grid=(sequences // per_step,),
-        in_specs=[
-            pl.BlockSpec((per_step * SEQ, columns), lambda i: (i, 0)),
-            pl.BlockSpec((lanes, per_step * neighbours, piece, width), lambda i: (0, i, 0, 0)),
-            pl.BlockSpec(weights.shape, lambda i: (0, 0)),
-            *[early_spec for _ in early],
-        ],
-        out_specs=pl.BlockSpec((per_step * SEQ, columns), lambda i: (i, 0)),
-        name="even_attention",
-    )(queries, rows, weights, *early)
-
-
-def patch_body(slot_ref, out_in_ref, odd_ref, out_ref, *rest, neighbours):
-    picked_refs, row_ref = rest[:-1], rest[-1]
-    per_step, _, tail, columns = out_ref.shape
-    heads = columns // DH
-    sequences = row_ref.shape[0]
-    step = pl.program_id(0)
-
-    @pl.when(step == 0)
-    def _():
-        for i in range(sequences):
-            for j, picked_ref in enumerate(picked_refs):
-                picked_ref[i : i + 1, :] = odd_ref[pl.ds(slot_ref[i * neighbours + j], 1), :]
-        for h in range(heads):
-            lo, hi = h * DH, (h + 1) * DH
-            maxima = [p[:, columns + h : columns + h + 1] for p in picked_refs]
-            sums = [p[:, columns + DH // 2 + h : columns + DH // 2 + h + 1] for p in picked_refs]
-            top = functools.reduce(jnp.maximum, maxima)
-            each = [jnp.exp(m - top) for m in maxima]
-            under = sum(e * t for e, t in zip(each, sums))
-            over = sum(e * p[:, lo:hi] for e, p in zip(each, picked_refs))
-            row_ref[:, lo:hi] = over / under
-
-    last = lax.broadcasted_iota(jnp.int32, (tail, columns), 0) == tail - 1
-    for i in range(per_step):
-        row = row_ref[pl.ds(step * per_step + i, 1), :]
-        out_ref[i, 0] = jnp.where(last, row, out_in_ref[i, 0].astype(F32)).astype(BF16)
-
-
-def patch(slots, out, odd):
-    tokens, columns = out.shape
-    sequences = tokens // SEQ
-    neighbours = slots.shape[0] // sequences
-    per_step = math.gcd(sequences, 4)
-    blocks = SEQ // TAIL
-    tail = pl.BlockSpec((per_step, 1, TAIL, columns), lambda i, s: (i, blocks - 1, 0, 0))
-    shape = (sequences, blocks, TAIL, columns)
+        in_specs=[*specs, *halves, pl.BlockSpec(odd.shape, lambda i: (0, 0))],
+        out_specs=specs[0],
+        name="late_attention",
+    )(queries, rows, weights, mixed, stats, odd)
+
+
+def combine_body(slot_ref, odd_ref, row_ref, *picked_refs):
+    sequences, columns = row_ref.shape
+    for i in range(sequences):
+        for j, picked_ref in enumerate(picked_refs):
+            picked_ref[i : i + 1, :] = odd_ref[pl.ds(slot_ref[i * len(picked_refs) + j], 1), :]
+    for h in range(columns // DH):
+        lo, hi = h * DH, (h + 1) * DH
+        maxima = [p[:, columns + h : columns + h + 1] for p in picked_refs]
+        sums = [p[:, columns + DH // 2 + h : columns + DH // 2 + h + 1] for p in picked_refs]
+        top = functools.reduce(jnp.maximum, maxima)
+        each = [jnp.exp(m - top) for m in maxima]
+        under = sum(e * t for e, t in zip(each, sums))
+        over = sum(e * p[:, lo:hi] for e, p in zip(each, picked_refs))
+        row_ref[:, lo:hi] = over / under
+
+
+def combine(slots, odd, sequences):
+    columns = odd.shape[1] - DH
     return pl.pallas_call(
-        functools.partial(patch_body, neighbours=neighbours),
-        out_shape=jax.ShapeDtypeStruct(shape, BF16),
+        combine_body,
+        out_shape=jax.ShapeDtypeStruct((sequences, columns), F32),
         grid_spec=pltpu.PrefetchScalarGridSpec(
             num_scalar_prefetch=1,
-            grid=(sequences // per_step,),
-            in_specs=[tail, pl.BlockSpec(odd.shape, lambda i, s: (0, 0))],
-            out_specs=tail,
-            scratch_shapes=[pltpu.VMEM((sequences, odd.shape[1]), F32)] * neighbours
-            + [pltpu.VMEM((sequences, columns), F32)],
+            grid=(1,),
+            in_specs=[pl.BlockSpec(odd.shape, lambda i, s: (0, 0))],
+            out_specs=pl.BlockSpec((sequences, columns), lambda i, s: (0, 0)),
+            scratch_shapes=[pltpu.VMEM((sequences, odd.shape[1]), F32)] * (slots.shape[0] // sequences),
         ),
-        input_output_aliases={1: 0},
-        name="patch",
-    )(slots, out.reshape(shape), odd).reshape(out.shape)
+        name="combine",
+    )(slots, odd)
 
 
 def gather_body(index_ref, *refs, count):
@@ -434,7 +437,7 @@
     def whole(source, chunk):
         return [source] * planes
 
-    def exchange(sources, select, index):
+    def exchange(sources, select, index, between):
         received, arrived = [], []
         for chunk, source in enumerate(sources):
             sending = select(source, chunk)
@@ -442,8 +445,9 @@
                 sending, _ = lax.optimization_barrier((sending, received[-1]))
             received.append(across(sending))
             outgoing = gather_rows(index[chunk], received[-1], group, parts)
-            outgoing, _ = lax.optimization_barrier((outgoing, arrived[-1] if arrived else odd_query))
+            outgoing, _ = lax.optimization_barrier((outgoing, after if arrived else odd_query))
             arrived.append(swap(outgoing, plane_groups))
+            after = arrived[-1] if chunk else between(arrived[-1])
         return [a.reshape(lanes, wanted, piece, width) for a in arrived]
 
     odd_part = jnp.zeros((shards * capacity, columns + DH), F32)
@@ -454,10 +458,21 @@
             odd_query, slot_want, (early_shared[k], late_shared[k]), weights, odd_part
         )
 
-    def attend(select, index):
-        *early, late = exchange(plane_pieces, select, index)
-        early = [project(e, weights) for e in early]
-        return even_attention(queries, late, weights, early), late
+    returned = []
+
+    def send_back(after):
+        part, _ = lax.optimization_barrier((odd_part, after))
+        part = lax.all_to_all(part.reshape(shards, capacity, columns + DH), "db", 0, 0, tiled=True)
+        returned.append(part)
+        return part
+
+    def attend(select, index, between, odd_rows):
+        early, late = exchange(plane_pieces, select, index, between)
+        early = early_attention(queries, early, weights)
+        return late_attention(queries, late, weights, *early, odd_rows())
+
+    def odd_rows():
+        return combine(my_slot, returned[0].reshape(shards * capacity, columns + DH), sequences)
 
     own_rows = [my_ids % plane_rows, stepped(my_ids % plane_rows)]
     fast_index = my_step * fast + jnp.minimum(place, fast - 1)
@@ -466,19 +481,17 @@
         fast_index = [
             jnp.where(my_step == 0, row, index + plane_rows - fast) for row, index in zip(own_rows, fast_index)
         ]
-    result, last = attend(exact, fast_index)
-    odd_part, _ = lax.optimization_barrier((odd_part, last))
-    odd_part = lax.all_to_all(odd_part.reshape(shards, capacity, columns + DH), "db", 0, 0, tiled=True)
-    odd_part = odd_part.reshape(shards * capacity, columns + DH)
+    result = attend(exact, fast_index, send_back, odd_rows)
     if fast < most:
-        result, odd_part = lax.optimization_barrier((result, odd_part))
         result = lax.cond(
             fits,
             lambda done: done,
-            lambda done: attend(whole, [my_step * plane_rows + row for row in own_rows])[0],
+            lambda done: attend(
+                whole, [my_step * plane_rows + row for row in own_rows], lambda arrived: arrived, odd_rows
+            ),
             result,
         )
-    return patch(my_slot, result, odd_part)
+    return result
 
 
 def solution(mesh):

time: 449 us -> 478 us (1.065)
  Pallas kernels: 118 us -> 156 us
  waiting for transfers between devices: 244 us -> 229 us
  starting transfers between devices: 46.1 us -> 51.7 us
    pallas_call x3, Pallas kernels: 59.9 us -> 97.6 us  [the longest x1 54.3 us: late_attention(): pl.pallas_call(functools.partial(late_body, per_step=per_step), out_shape...]
    ppermute x6, waiting for transfers between devices: 138 us -> 119 us  [across(): moved.append(lax.ppermute(blocks[k], BOTH, pairs))]
  transfers between devices with their start and end apart: 16 -> 16, of which waited for: 9 -> 10; matrix products, arithmetic and copies ran while one was open for 5% -> 5% of each run, Pallas kernels for 25% -> 21%
where the time goes in v5:
time: 478 us; the launch traced here: 477 us
  waiting for transfers between devices  229 us (48%)
  Pallas kernels  156 us (33%)
  starting transfers between devices  51.7 us (11%)
  local copies, waits for them, and re-layouts  18.5 us (4%)
  between operations  14.2 us (3%)
  other arithmetic  7.48 us (2%)
    ppermute x6, waiting for transfers between devices, across(): moved.append(lax.ppermute(blocks[k], BOTH, pairs))  119 us
    ppermute x2, waiting for transfers between devices, share(): lax.ppermute(half, 'mp', [(m, (m + k) % parts) for m in range(parts)])  88.7 us
    pallas_call x1, Pallas kernels, late_attention(): pl.pallas_call(functools.partial(late_body, per_step=per_step), out_shape...  54.3 us
    pallas_call x2, Pallas kernels, odd_attention(): pl.pallas_call(odd_body, out_shape=jax.ShapeDtypeStruct(prior.shape, F32)...  42.4 us
    pallas_call x1, Pallas kernels, early_attention(): pl.pallas_call(functools.partial(early_body, per_step=per_step), out_shap...  41.8 us
    all_to_all x4, starting transfers between devices, swap(): return lax.all_to_all(x, BOTH, 0, 0, axis_index_groups=groups, tiled=True)  21.6 us
    all_to_all x4, waiting for transfers between devices, swap(): return lax.all_to_all(x, BOTH, 0, 0, axis_index_groups=groups, tiled=True)  21.2 us
    pallas_call x2, Pallas kernels, gather_rows(): pl.pallas_call(functools.partial(gather_body, count=len(sources)), out_sh...  9.67 us
  transfers between devices with their start and end apart: 16, of which 10 were waited for; matrix products, arithmetic and copies ran while one was open for 5% of the time, Pallas kernels for 21%

profile of v5, /device:TPU:11, one launch (start us, length us, event | category | flops | bytes accessed | tf_op | source)
XLA Modules:
  0.0 476.8 jit_solution(11871043899164966750)
XLA Ops:
  6.5 0.8 copy.59
  7.3 0.1 reshape.198
  7.4 0.8 copy.60
  8.2 0.1 reshape.199
  8.3 0.6 broadcast_in_dim.118
  8.9 6.5 %all-to-all-start.2 = ((s32[16,1,128]{2,1,0:T(1,128)}), s32[16,1,128]{2,1,0:T(1,128)S(1)}, u32[]{:S(2)}, u32[]{:S(2)}) async-start(s32[16,1,128]{2,1,0:T(1,128)} %broadcast_in_dim.118), calls=%async_computation.2 | async-start | bytes 16384 | tf_op jit(solution)/shard_map/all_to_all | solution.py:343
  15.5 1.7 pad_maximum_fusion.1
  17.3 2.6 copy.82
  19.9 3.0 slice_bitcast_fusion.1
  23.0 1.0 slice.42
  24.1 4.3 all-to-all-start.3
  28.6 0.2 copy.64
  28.7 0.1 add.167
  28.9 0.2 fusion
  29.2 0.1 convolution_convert_fusion
  29.3 0.9 select_reduce_fusion.1
  30.5 0.6 reshape.209.index_ref
  31.2 0.5 convert_reduce_fusion
  31.7 1.5 gather_fusion
  33.3 21.2 %all-to-all-done.3.source_ref.refs_0_ = bf16[128,8,896]{2,1,0:T(8,128)(2,1)S(1)} async-done(((bf16[128,8,896]{2,1,0:T(8,128)(2,1)}), bf16[128,8,896]{2,1,0:T(8,128)(2,1)S(1)}, u32[]{:S(2)}, u32[]{:S(2)}) %all-to-all-start.3) | async-done | bytes 1835040 | tf_op jit(solution)/shard_map/all_to_all | solution.py:324
  54.5 2.2 select_rows.2
  56.8 1.4 collective-permute-start.8
  58.2 3.9 collective-permute-start.9
  62.1 5.3 %all-to-all-start.4 = ((bf16[16,8,1024]{2,1,0:T(8,128)(2,1)}), bf16[16,8,1024]{2,1,0:T(8,128)(2,1)S(1)}, u32[]{:S(2)}, u32[]{:S(2)}) async-start(bf16[16,8,1024]{2,1,0:T(8,128)(2,1)} %bitcast.23), calls=%async_computation.4 | async-start | bytes 524288 | tf_op jit(solution)/shard_map/all_to_all | solution.py:372
  67.4 0.2 select_reduce_fusion
  67.6 0.6 compare_select_fusion.12
  68.1 0.5 compare_select_fusion.13.index_ref
  68.7 11.8 %collective-permute-done.10.refs_3_ = bf16[46,8,896]{2,1,0:T(8,128)(2,1)S(1)} collective-permute-done((bf16[46,8,896]{2,1,0:T(8,128)(2,1)}, bf16[46,8,896]{2,1,0:T(8,128)(2,1)S(1)}, u32[]{:S(2)}, u32[]{:S(2)}) %collective-permute-start.10) | collective-permute-done | bytes 659488 | tf_op jit(solution)/shard_map/ppermute | solution.py:338
  80.5 13.5 %collective-permute-done.8.refs_1_ = bf16[46,8,896]{2,1,0:T(8,128)(2,1)S(1)} collective-permute-done((bf16[46,8,896]{2,1,0:T(8,128)(2,1)}, bf16[46,8,896]{2,1,0:T(8,128)(2,1)S(1)}, u32[]{:S(2)}, u32[]{:S(2)}) %collective-permute-start.8) | collective-permute-done | bytes 659488 | tf_op jit(solution)/shard_map/ppermute | solution.py:338
  94.0 29.9 %collective-permute-done.9.refs_2_ = bf16[46,8,896]{2,1,0:T(8,128)(2,1)} collective-permute-done((bf16[46,8,896]{2,1,0:T(8,128)(2,1)}, bf16[46,8,896]{2,1,0:T(8,128)(2,1)}, u32[]{:S(2)}, u32[]{:S(2)}) %collective-permute-start.9) | collective-permute-done | bytes 659488 | tf_op jit(solution)/shard_map/ppermute | solution.py:338
  123.9 4.6 gather_rows.6
  128.5 0.7 all-to-all-done.4
  129.2 0.7 copy-done
  129.9 6.5 %all-to-all-start.6 = ((bf16[256,8,896]{2,1,0:T(8,128)(2,1)}), bf16[256,8,896]{2,1,0:T(8,128)(2,1)}, u32[]{:S(2)}, u32[]{:S(2)}) async-start(bf16[256,8,896]{2,1,0:T(8,128)(2,1)} %bitcast.64), calls=%async_computation.6 | async-start | bytes 7340032 | tf_op jit(solution)/shard_map/all_to_all | solution.py:324
  136.4 1.2 collective-permute-start.6
  137.6 80.1 %collective-permute-done.6.refs_1_ = bf16[8,16,8,896]{3,2,1,0:T(8,128)(2,1)} collective-permute-done((bf16[8,16,8,896]{3,2,1,0:T(8,128)(2,1)}, bf16[8,16,8,896]{3,2,1,0:T(8,128)(2,1)}, u32[]{:S(2)}, u32[]{:S(2)}) %collective-permute-start.6) | collective-permute-done | bytes 1835040 | tf_op jit(solution)/shard_map/ppermute | solution.py:381
  217.7 0.1 collective-permute-start.7
  217.8 1.3 dynamic-slice_bitcast_fusion.1
  219.1 1.3 dynamic-slice_bitcast_fusion
  220.4 1.4 pad_maximum_fusion
  221.8 5.3 %all-to-all-start.5 = ((bf16[128,8,896]{2,1,0:T(8,128)(2,1)}), bf16[128,8,896]{2,1,0:T(8,128)(2,1)}, u32[]{:S(2)}, u32[]{:S(2)}) async-start(bf16[128,8,896]{2,1,0:T(8,128)(2,1)} %bitcast.68), calls=%async_computation.5 | async-start | bytes 3670016 | tf_op jit(solution)/shard_map/all_to_all | solution.py:324
  227.3 0.4 select_reduce_fusion.2
  227.8 0.7 broadcast_in_dim.125.want_ref
  228.5 0.9 broadcast_in_dim.126.refs_3_
  229.4 21.2 %odd_attention.2.refs_3_ = f32[128,1152]{1,0:T(8,128)} custom-call(bf16[128,1024]{1,0:T(8,128)(2,1)} %bitcast.74, s32[128,128]{1,0:T(8,128)} %broadcast_in_dim.125.want_ref, bf16[8,16,8,896]{3,2,1,0:T(8,128)(2,1)} %get-tuple-element.68.refs_0_, bf16[8,16,8,896]{3,2,1,0:T(8,128)(2,1)} %get-tuple-element.65.refs_1_, ...), custom_call_target="tpu_custom_call" | custom-call | tf_op jit(solution)/shard_map/odd_attention/pallas_call | solution.py:285
  250.6 8.6 %collective-permute-done.7.refs_0_ = bf16[8,16,8,896]{3,2,1,0:T(8,128)(2,1)} collective-permute-done((bf16[8,16,8,896]{3,2,1,0:T(8,128)(2,1)}, bf16[8,16,8,896]{3,2,1,0:T(8,128)(2,1)}, u32[]{:S(2)}, u32[]{:S(2)}) %collective-permute-start.7) | collective-permute-done | bytes 1835040 | tf_op jit(solution)/shard_map/ppermute | solution.py:381
  259.2 0.7 broadcast_in_dim.124.want_ref
  259.9 21.2 %odd_attention.3 = f32[128,1152]{1,0:T(8,128)} custom-call(bf16[128,1024]{1,0:T(8,128)(2,1)} %bitcast.75, s32[128,128]{1,0:T(8,128)} %broadcast_in_dim.124.want_ref, bf16[8,16,8,896]{3,2,1,0:T(8,128)(2,1)} %collective-permute-done.7.refs_0_, bf16[8,16,8,896]{3,2,1,0:T(8,128)(2,1)} %collective-permute-done.6.refs_1_, ...), custom_call_target="tpu_custom_call" | custom-call | tf_op jit(solution)/shard_map/odd_attention/pallas_call | solution.py:285
  281.1 7.9 %all-to-all-start.7 = ((f32[16,8,1152]{2,1,0:T(8,128)}), f32[16,8,1152]{2,1,0:T(8,128)S(1)}, u32[]{:S(2)}, u32[]{:S(2)}) async-start(f32[16,8,1152]{2,1,0:T(8,128)} %bitcast.73), calls=%async_computation.7 | async-start | bytes 1179648 | tf_op jit(solution)/shard_map/all_to_all | solution.py:465
  289.0 0.6 reshape.212.index_ref
  289.6 3.7 select_rows.3
  293.4 1.2 collective-permute-start.11
  294.6 1.2 collective-permute-start.12
  295.8 1.2 collective-permute-start.13
  296.9 47.4 %collective-permute-done.11.refs_1_ = bf16[46,8,896]{2,1,0:T(8,128)(2,1)S(1)} collective-permute-done((bf16[46,8,896]{2,1,0:T(8,128)(2,1)}, bf16[46,8,896]{2,1,0:T(8,128)(2,1)S(1)}, u32[]{:S(2)}, u32[]{:S(2)}) %collective-permute-start.11) | collective-permute-done | bytes 659488 | tf_op jit(solution)/shard_map/ppermute | solution.py:338
  344.4 14.1 %collective-permute-done.12.refs_2_ = bf16[46,8,896]{2,1,0:T(8,128)(2,1)} collective-permute-done((bf16[46,8,896]{2,1,0:T(8,128)(2,1)}, bf16[46,8,896]{2,1,0:T(8,128)(2,1)}, u32[]{:S(2)}, u32[]{:S(2)}) %collective-permute-start.12) | collective-permute-done | bytes 659488 | tf_op jit(solution)/shard_map/ppermute | solution.py:338
  358.5 1.9 collective-permute-done.13.refs_3_
  360.4 5.0 %gather_rows.7 = bf16[4,2,32,8,896]{4,3,2,1,0:T(8,128)(2,1)} custom-call(s32[128]{0:T(128)} %get-tuple-element.85.index_ref, bf16[128,8,896]{2,1,0:T(8,128)(2,1)} %all-to-all-done.5.source_ref.refs_0_, bf16[46,8,896]{2,1,0:T(8,128)(2,1)} %copy-done.7, bf16[46,8,896]{2,1,0:T(8,128)(2,1)} %collective-permute-done.12.refs_2_, ...), custom_call_target="tpu_custom_call" | custom-call | tf_op jit(solution)/shard_map/gather_rows/pallas_call | solution.py:191
  365.5 5.6 %all-to-all-start.8 = ((bf16[256,8,896]{2,1,0:T(8,128)(2,1)}), bf16[256,8,896]{2,1,0:T(8,128)(2,1)}, u32[]{:S(2)}, u32[]{:S(2)}) async-start(bf16[256,8,896]{2,1,0:T(8,128)(2,1)} %bitcast.65), calls=%async_computation.8 | async-start | bytes 7340032 | tf_op jit(solution)/shard_map/all_to_all | solution.py:324
  371.0 0.1 convert_reduce_fusion.1
  371.2 0.7 select_reduce_fusion.5
  372.4 41.8 %early_attention.3 = (f32[1280,1024]{1,0:T(8,128)}, f32[1280,128]{1,0:T(8,128)}) custom-call(bf16[2048,1024]{1,0:T(8,128)(2,1)} %query_ref.3, bf16[8,32,8,896]{3,2,1,0:T(8,128)(2,1)} %bitcast.36.rows_ref, bf16[896,2048]{1,0:T(8,128)(2,1)} %all-gather.2.cloned.1.call-done.refs_2_.weight_ref), custom_call_target="tpu_custom_call" | custom-call | tf_op jit(solution)/shard_map/early_attention/pallas_call | solution.py:106
  414.2 1.4 combine.3.odd_ref
  415.6 54.3 %late_attention.3 = bf16[2048,1024]{1,0:T(8,128)(2,1)} custom-call(bf16[2048,1024]{1,0:T(8,128)(2,1)} %query_ref.3, bf16[8,32,8,896]{3,2,1,0:T(8,128)(2,1)} %bitcast.35.rows_ref, bf16[896,2048]{1,0:T(8,128)(2,1)} %all-gather.2.cloned.1.call-done.refs_2_.weight_ref, f32[1280,1024]{1,0:T(8,128)} %get-tuple-element.82.mixed_ref, ...), custom_call_target="tpu_custom_call" | custom-call | tf_op jit(solution)/shard_map/late_attention/pallas_call | solution.py:120
  (50 shorter events, 1.5 us)
Async XLA Ops:
  8.9 15.1 %all-to-all-start.2 = ((s32[16,1,128]{2,1,0:T(1,128)}), s32[16,1,128]{2,1,0:T(1,128)S(1)}, u32[]{:S(2)}, u32[]{:S(2)}) async-start(s32[16,1,128]{2,1,0:T(1,128)} %broadcast_in_dim.118), calls=%async_computation.2 | async-start | bytes 16384 | tf_op jit(solution)/shard_map/all_to_all | solution.py:343
  15.5 212.4 %all-gather.2.cloned.1.call-start = ((), (), s32[]{:S(2)}) async-start(), calls=%async_computation.9 | async-start | bytes 3899392 | tf_op jit(solution)/shard_map/all_gather | solution.py:348
  24.1 30.3 %all-to-all-start.3 = ((bf16[128,8,896]{2,1,0:T(8,128)(2,1)}), bf16[128,8,896]{2,1,0:T(8,128)(2,1)S(1)}, u32[]{:S(2)}, u32[]{:S(2)}) async-start(bf16[128,8,896]{2,1,0:T(8,128)(2,1)} %bitcast.69), calls=%async_computation.3 | async-start | bytes 3670016 | tf_op jit(solution)/shard_map/all_to_all | solution.py:324
  56.7 23.8 %collective-permute-start.10 = (bf16[46,8,896]{2,1,0:T(8,128)(2,1)}, bf16[46,8,896]{2,1,0:T(8,128)(2,1)S(1)}, u32[]{:S(2)}, u32[]{:S(2)}) collective-permute-start(bf16[46,8,896]{2,1,0:T(8,128)(2,1)} %get-tuple-element.71), channel_id=1, source_target_pairs={{0,24},{1,25},{2,26},{3,27},{4,28},{5,29},{6,30},{7,31},{8,0},{9,1... | collective-permute-start | bytes 1978376 | tf_op jit(solution)/shard_map/ppermute | solution.py:338
  56.8 37.2 %collective-permute-start.8 = (bf16[46,8,896]{2,1,0:T(8,128)(2,1)}, bf16[46,8,896]{2,1,0:T(8,128)(2,1)S(1)}, u32[]{:S(2)}, u32[]{:S(2)}) collective-permute-start(bf16[46,8,896]{2,1,0:T(8,128)(2,1)} %get-tuple-element.69), channel_id=1, source_target_pairs={{0,8},{1,9},{2,10},{3,11},{4,12},{5,13},{6,14},{7,15},{8,16},{9,17... | collective-permute-start | bytes 1978376 | tf_op jit(solution)/shard_map/ppermute | solution.py:338
  58.2 65.7 %collective-permute-start.9 = (bf16[46,8,896]{2,1,0:T(8,128)(2,1)}, bf16[46,8,896]{2,1,0:T(8,128)(2,1)}, u32[]{:S(2)}, u32[]{:S(2)}) collective-permute-start(bf16[46,8,896]{2,1,0:T(8,128)(2,1)} %get-tuple-element.70), channel_id=1, source_target_pairs={{0,16},{1,17},{2,18},{3,19},{4,20},{5,21},{6,22},{7,23},{8,24},{9,... | collective-permute-start | bytes 1978376 | tf_op jit(solution)/shard_map/ppermute | solution.py:338
  62.1 67.1 %all-to-all-start.4 = ((bf16[16,8,1024]{2,1,0:T(8,128)(2,1)}), bf16[16,8,1024]{2,1,0:T(8,128)(2,1)S(1)}, u32[]{:S(2)}, u32[]{:S(2)}) async-start(bf16[16,8,1024]{2,1,0:T(8,128)(2,1)} %bitcast.23), calls=%async_computation.4 | async-start | bytes 524288 | tf_op jit(solution)/shard_map/all_to_all | solution.py:372
  80.5 43.4 %copy-start.5 = (bf16[46,8,896]{2,1,0:T(8,128)(2,1)}, bf16[46,8,896]{2,1,0:T(8,128)(2,1)S(1)}, u32[]{:S(2)}) copy-start(bf16[46,8,896]{2,1,0:T(8,128)(2,1)S(1)} %collective-permute-done.10.refs_3_) | copy-start | bytes 1978372
  94.0 29.9 %copy-start.6 = (bf16[46,8,896]{2,1,0:T(8,128)(2,1)}, bf16[46,8,896]{2,1,0:T(8,128)(2,1)S(1)}, u32[]{:S(2)}) copy-start(bf16[46,8,896]{2,1,0:T(8,128)(2,1)S(1)} %collective-permute-done.8.refs_1_) | copy-start | bytes 1978372
  129.2 0.7 copy-start
  129.9 91.9 %all-to-all-start.6 = ((bf16[256,8,896]{2,1,0:T(8,128)(2,1)}), bf16[256,8,896]{2,1,0:T(8,128)(2,1)}, u32[]{:S(2)}, u32[]{:S(2)}) async-start(bf16[256,8,896]{2,1,0:T(8,128)(2,1)} %bitcast.64), calls=%async_computation.6 | async-start | bytes 7340032 | tf_op jit(solution)/shard_map/all_to_all | solution.py:324
  136.4 81.3 %collective-permute-start.6 = (bf16[8,16,8,896]{3,2,1,0:T(8,128)(2,1)}, bf16[8,16,8,896]{3,2,1,0:T(8,128)(2,1)}, u32[]{:S(2)}, u32[]{:S(2)}) collective-permute-start(bf16[8,16,8,896]{3,2,1,0:T(8,128)(2,1)} %get-tuple-element.65.refs_1_), channel_id=1, source_target_pairs={{0,1},{1,0},{2,3},{3,2},{4,5},{5,4},{6,7},{7,6},{8,9},{9,8},{10,11... | collective-permute-start | bytes 5505032 | tf_op jit(solution)/shard_map/ppermute | solution.py:381
  217.7 41.4 %collective-permute-start.7 = (bf16[8,16,8,896]{3,2,1,0:T(8,128)(2,1)}, bf16[8,16,8,896]{3,2,1,0:T(8,128)(2,1)}, u32[]{:S(2)}, u32[]{:S(2)}) collective-permute-start(bf16[8,16,8,896]{3,2,1,0:T(8,128)(2,1)} %get-tuple-element.68.refs_0_), channel_id=1, source_target_pairs={{0,1},{1,0},{2,3},{3,2},{4,5},{5,4},{6,7},{7,6},{8,9},{9,8},{10,11... | collective-permute-start | bytes 5505032 | tf_op jit(solution)/shard_map/ppermute | solution.py:381
  221.8 59.3 %all-to-all-start.5 = ((bf16[128,8,896]{2,1,0:T(8,128)(2,1)}), bf16[128,8,896]{2,1,0:T(8,128)(2,1)}, u32[]{:S(2)}, u32[]{:S(2)}) async-start(bf16[128,8,896]{2,1,0:T(8,128)(2,1)} %bitcast.68), calls=%async_computation.5 | async-start | bytes 3670016 | tf_op jit(solution)/shard_map/all_to_all | solution.py:324
  281.1 84.4 %all-to-all-start.7 = ((f32[16,8,1152]{2,1,0:T(8,128)}), f32[16,8,1152]{2,1,0:T(8,128)S(1)}, u32[]{:S(2)}, u32[]{:S(2)}) async-start(f32[16,8,1152]{2,1,0:T(8,128)} %bitcast.73), calls=%async_computation.7 | async-start | bytes 1179648 | tf_op jit(solution)/shard_map/all_to_all | solution.py:465
  293.4 51.0 %collective-permute-start.11 = (bf16[46,8,896]{2,1,0:T(8,128)(2,1)}, bf16[46,8,896]{2,1,0:T(8,128)(2,1)S(1)}, u32[]{:S(2)}, u32[]{:S(2)}) collective-permute-start(bf16[46,8,896]{2,1,0:T(8,128)(2,1)} %get-tuple-element.78), channel_id=1, source_target_pairs={{0,8},{1,9},{2,10},{3,11},{4,12},{5,13},{6,14},{7,15},{8,16},{9,17... | collective-permute-start | bytes 1978376 | tf_op jit(solution)/shard_map/ppermute | solution.py:338
  294.6 63.9 %collective-permute-start.12 = (bf16[46,8,896]{2,1,0:T(8,128)(2,1)}, bf16[46,8,896]{2,1,0:T(8,128)(2,1)}, u32[]{:S(2)}, u32[]{:S(2)}) collective-permute-start(bf16[46,8,896]{2,1,0:T(8,128)(2,1)} %get-tuple-element.79), channel_id=1, source_target_pairs={{0,16},{1,17},{2,18},{3,19},{4,20},{5,21},{6,22},{7,23},{8,24},{9,... | collective-permute-start | bytes 1978376 | tf_op jit(solution)/shard_map/ppermute | solution.py:338
  295.8 64.6 %collective-permute-start.13 = (bf16[46,8,896]{2,1,0:T(8,128)(2,1)}, bf16[46,8,896]{2,1,0:T(8,128)(2,1)}, u32[]{:S(2)}, u32[]{:S(2)}) collective-permute-start(bf16[46,8,896]{2,1,0:T(8,128)(2,1)} %get-tuple-element.80), channel_id=1, source_target_pairs={{0,24},{1,25},{2,26},{3,27},{4,28},{5,29},{6,30},{7,31},{8,0},{9,1... | collective-permute-start | bytes 1978376 | tf_op jit(solution)/shard_map/ppermute | solution.py:338
  344.4 16.0 %copy-start.7 = (bf16[46,8,896]{2,1,0:T(8,128)(2,1)}, bf16[46,8,896]{2,1,0:T(8,128)(2,1)S(1)}, u32[]{:S(2)}) copy-start(bf16[46,8,896]{2,1,0:T(8,128)(2,1)S(1)} %collective-permute-done.11.refs_1_) | copy-start | bytes 1978372
  365.5 50.2 %all-to-all-start.8 = ((bf16[256,8,896]{2,1,0:T(8,128)(2,1)}), bf16[256,8,896]{2,1,0:T(8,128)(2,1)}, u32[]{:S(2)}, u32[]{:S(2)}) async-start(bf16[256,8,896]{2,1,0:T(8,128)(2,1)} %bitcast.65), calls=%async_computation.8 | async-start | bytes 7340032 | tf_op jit(solution)/shard_map/all_to_all | solution.py:324
Sparse Core Ops, SparseCore 0:
  18.6 64.2 all-gather.1

commit v6 on v5

--- a/solution.py
+++ b/solution.py
@@ -31,100 +31,87 @@
     return jnp.dot(stacked, weight_ref[...], preferred_element_type=F32).astype(BF16)
 
 
-def attend_head(query, keys, values):
-    scores = lax.dot_general(query, keys, CONTRACT_LAST, preferred_element_type=F32) * SCALE
-    largest = jnp.max(scores, axis=1, keepdims=True)
-    expscore = jnp.exp(scores - largest)
-    total = jnp.sum(expscore, axis=1, keepdims=True)
-    return jnp.dot(expscore.astype(BF16), values, preferred_element_type=F32), largest, total
-
-
-def early_body(query_ref, rows_ref, weight_ref, mixed_ref, stats_ref, *, per_step):
+def project_body(rows_ref, weight_ref, out_ref):
+    out_ref[...] = project_rows(rows_ref, weight_ref)
+
+
+def project(rows, weights):
+    lanes, count, piece, width = rows.shape
+    per_step = math.gcd(count, 8)
+    tokens = lanes * piece
+    return pl.pallas_call(
+        project_body,
+        out_shape=jax.ShapeDtypeStruct((count * tokens, weights.shape[1]), BF16),
+        grid=(count // per_step,),
+        in_specs=[
+            pl.BlockSpec((lanes, per_step, piece, width), lambda i: (0, i, 0, 0)),
+            pl.BlockSpec(weights.shape, lambda i: (0, 0)),
+        ],
+        out_specs=pl.BlockSpec((per_step * tokens, weights.shape[1]), lambda i: (i, 0)),
+        name="project",
+    )(rows, weights)
+
+
+def even_body(query_ref, rows_ref, weight_ref, early_ref, odd_ref, out_ref, *, per_step):
     columns = query_ref.shape[1]
-    projected = project_rows(rows_ref, weight_ref)
-    span = projected.shape[0] // per_step
-    lane = lax.broadcasted_iota(jnp.int32, (SEQ - LOW, DH), 1)
-    for s in range(per_step):
-        own = projected[s * span : (s + 1) * span]
-        at = slice(s * (SEQ - LOW), (s + 1) * (SEQ - LOW))
-        stats = jnp.zeros((SEQ - LOW, DH), F32)
-        for h in range(columns // DH):
-            lo, hi = h * DH, (h + 1) * DH
-            query = query_ref[s * SEQ + LOW : (s + 1) * SEQ, lo:hi]
-            mixed, largest, total = attend_head(query, own[:, lo:hi], own[:, columns + lo : columns + hi])
-            mixed_ref[at, lo:hi] = mixed
-            stats = jnp.where(lane == h, largest, stats)
-            stats = jnp.where(lane == DH // 2 + h, total, stats)
-        stats_ref[at, :] = stats
-
-
-def late_body(query_ref, rows_ref, weight_ref, mixed_ref, stats_ref, odd_ref, out_ref, *, per_step):
-    columns = query_ref.shape[1]
-    projected = project_rows(rows_ref, weight_ref)
-    span = projected.shape[0] // per_step
+    late = project_rows(rows_ref, weight_ref)
+    span = late.shape[0] // per_step
     first = SPAN - 1
     position = LOW + lax.broadcasted_iota(jnp.int32, (SEQ - LOW, DH), 0)
+    odd = [odd_ref[pl.ds(pl.program_id(0) * per_step + s, 1), :] for s in range(per_step)]
+    blocks = [(s, h * DH) for s in range(per_step) for h in range(columns // DH)]
+
+    def both(s, lo):
+        at = slice(s * span, (s + 1) * span)
+        return jnp.concatenate([early_ref[at, lo : lo + DH], late[at, lo : lo + DH]], axis=0)
+
+    scores = [
+        lax.dot_general(
+            query_ref[s * SEQ + LOW : (s + 1) * SEQ, lo : lo + DH],
+            both(s, lo),
+            CONTRACT_LAST,
+            preferred_element_type=F32,
+        )
+        * SCALE
+        for s, lo in blocks
+    ]
+    largest = [jnp.max(x, axis=1, keepdims=True) for x in scores]
+    expscore = [jnp.exp(x - m) for x, m in zip(scores, largest)]
+    total = [jnp.sum(e, axis=1, keepdims=True) for e in expscore]
+    mixed = [
+        jnp.dot(e.astype(BF16), both(s, columns + lo), preferred_element_type=F32)
+        for e, (s, lo) in zip(expscore, blocks)
+    ]
     for s in range(per_step):
-        own = projected[s * span : (s + 1) * span]
-        at = slice(s * (SEQ - LOW), (s + 1) * (SEQ - LOW))
-        stats = stats_ref[at, :]
-        odd = odd_ref[pl.ds(pl.program_id(0) * per_step + s, 1), :]
         out_ref[s * SEQ : s * SEQ + LOW, :] = jnp.zeros((LOW, columns), BF16)
-        for h in range(columns // DH):
-            lo, hi = h * DH, (h + 1) * DH
-            query = query_ref[s * SEQ + LOW : (s + 1) * SEQ, lo:hi]
-            mixed, largest, total = attend_head(query, own[:, lo:hi], own[:, columns + lo : columns + hi])
-            before = stats[:, h : h + 1]
-            top = jnp.maximum(largest, before)
-            here, there = jnp.exp(largest - top), jnp.exp(before - top)
-            under = total * here + stats[:, DH // 2 + h : DH // 2 + h + 1] * there
-            attended = mixed * (here / under) + mixed_ref[at, lo:hi] * (there / under)
-            attended = jnp.where(position == SEQ - 1, odd[:, lo:hi], attended)
-            attended = jnp.where(position < first, 0.0, attended)
-            out_ref[s * SEQ + LOW : (s + 1) * SEQ, lo:hi] = attended.astype(BF16)
-
-
-def even_specs(queries, rows, weights):
+    for (s, lo), over, under in zip(blocks, mixed, total):
+        attended = over * (1.0 / under)
+        attended = jnp.where(position == SEQ - 1, odd[s][:, lo : lo + DH], attended)
+        attended = jnp.where(position < first, 0.0, attended)
+        out_ref[s * SEQ + LOW : (s + 1) * SEQ, lo : lo + DH] = attended.astype(BF16)
+
+
+def even_attention(queries, rows, weights, early, odd):
     columns = queries.shape[1]
     sequences = queries.shape[0] // SEQ
     lanes, count, piece, width = rows.shape
     per_step = math.gcd(sequences, 2)
-    specs = [
-        pl.BlockSpec((per_step * SEQ, columns), lambda i: (i, 0)),
-        pl.BlockSpec((lanes, per_step * count // sequences, piece, width), lambda i: (0, i, 0, 0)),
-        pl.BlockSpec(weights.shape, lambda i: (0, 0)),
-    ]
-    halves = [
-        pl.BlockSpec((per_step * (SEQ - LOW), columns), lambda i: (i, 0)),
-        pl.BlockSpec((per_step * (SEQ - LOW), DH), lambda i: (i, 0)),
-    ]
-    return sequences, per_step, specs, halves
-
-
-def early_attention(queries, rows, weights):
-    sequences, per_step, specs, halves = even_specs(queries, rows, weights)
+    rows_step = per_step * count // sequences
+    query_spec = pl.BlockSpec((per_step * SEQ, columns), lambda i: (i, 0))
     return pl.pallas_call(
-        functools.partial(early_body, per_step=per_step),
-        out_shape=[
-            jax.ShapeDtypeStruct((sequences * (SEQ - LOW), width), F32) for width in (queries.shape[1], DH)
-        ],
-        grid=(sequences // per_step,),
-        in_specs=specs,
-        out_specs=halves,
-        name="early_attention",
-    )(queries, rows, weights)
-
-
-def late_attention(queries, rows, weights, mixed, stats, odd):
-    sequences, per_step, specs, halves = even_specs(queries, rows, weights)
-    return pl.pallas_call(
-        functools.partial(late_body, per_step=per_step),
+        functools.partial(even_body, per_step=per_step),
         out_shape=jax.ShapeDtypeStruct(queries.shape, BF16),
         grid=(sequences // per_step,),
-        in_specs=[*specs, *halves, pl.BlockSpec(odd.shape, lambda i: (0, 0))],
-        out_specs=specs[0],
-        name="late_attention",
-    )(queries, rows, weights, mixed, stats, odd)
+        in_specs=[
+            query_spec,
+            pl.BlockSpec((lanes, rows_step, piece, width), lambda i: (0, i, 0, 0)),
+            pl.BlockSpec(weights.shape, lambda i: (0, 0)),
+            pl.BlockSpec((rows_step * lanes * piece, weights.shape[1]), lambda i: (i, 0)),
+            pl.BlockSpec(odd.shape, lambda i: (0, 0)),
+        ],
+        out_specs=query_spec,
+        name="even_attention",
+    )(queries, rows, weights, early, odd)
 
 
 def combine_body(slot_ref, odd_ref, row_ref, *picked_refs):
@@ -254,26 +241,36 @@
     here = [want == r for r in range(per_step)]
     inside = (want >= 0) & (want < per_step)
     lane = lax.broadcasted_iota(jnp.int32, (want.shape[0], DH), 1)
+    spans = [(h * DH, (h + 1) * DH) for h in range(heads)]
+    scores = [
+        lax.dot_general(
+            query_ref[:, lo:hi], projected[:, lo:hi], CONTRACT_LAST, preferred_element_type=F32
+        )
+        * SCALE
+        for lo, hi in spans
+    ]
+    mine = []
+    for x in scores:
+        chosen = jnp.zeros((want.shape[0], tokens), F32)
+        for r in range(per_step):
+            chosen = jnp.where(here[r], x[:, r * tokens : (r + 1) * tokens], chosen)
+        mine.append(chosen)
+    largest = [jnp.max(x, axis=1, keepdims=True) for x in mine]
+    expscore = [jnp.exp(x - m) for x, m in zip(mine, largest)]
+    total = [jnp.sum(e, axis=1, keepdims=True) for e in expscore]
+    spread = [
+        jnp.concatenate([jnp.where(here[r], e, 0.0) for r in range(per_step)], axis=1).astype(BF16)
+        for e in expscore
+    ]
+    mixed = [
+        jnp.dot(p, projected[:, columns + lo : columns + hi], preferred_element_type=F32)
+        for p, (lo, hi) in zip(spread, spans)
+    ]
     stats = out_ref[:, columns:]
-    for h in range(heads):
-        lo, hi = h * DH, (h + 1) * DH
-        scores = (
-            lax.dot_general(
-                query_ref[:, lo:hi], projected[:, lo:hi], CONTRACT_LAST, preferred_element_type=F32
-            )
-            * SCALE
-        )
-        mine = jnp.zeros((want.shape[0], tokens), F32)
-        for r in range(per_step):
-            mine = jnp.where(here[r], scores[:, r * tokens : (r + 1) * tokens], mine)
-        largest = jnp.max(mine, axis=1, keepdims=True)
-        expscore = jnp.exp(mine - largest)
-        total = jnp.sum(expscore, axis=1, keepdims=True)
-        spread = jnp.concatenate([jnp.where(here[r], expscore, 0.0) for r in range(per_step)], axis=1)
-        mixed = jnp.dot(spread.astype(BF16), projected[:, columns + lo : columns + hi], preferred_element_type=F32)
-        out_ref[:, lo:hi] = jnp.where(inside, mixed, out_ref[:, lo:hi])
-        stats = jnp.where(inside & (lane == h), largest, stats)
-        stats = jnp.where(inside & (lane == DH // 2 + h), total, stats)
+    for h, (lo, hi) in enumerate(spans):
+        out_ref[:, lo:hi] = jnp.where(inside, mixed[h], out_ref[:, lo:hi])
+        stats = jnp.where(inside & (lane == h), largest[h], stats)
+        stats = jnp.where(inside & (lane == DH // 2 + h), total[h], stats)
     out_ref[:, columns:] = stats
 
 
@@ -468,8 +465,8 @@
 
     def attend(select, index, between, odd_rows):
         early, late = exchange(plane_pieces, select, index, between)
-        early = early_attention(queries, early, weights)
-        return late_attention(queries, late, weights, *early, odd_rows())
+        early = project(early, weights)
+        return even_attention(queries, late, weights, early, odd_rows())
 
     def odd_rows():
         return combine(my_slot, returned[0].reshape(shards * capacity, columns + DH), sequences)

time: 478 us -> 436 us (0.912)
  Pallas kernels: 156 us -> 80.8 us
  waiting for transfers between devices: 229 us -> 263 us
    pallas_call x2, Pallas kernels: 96.1 us -> 32.7 us  [the longest x1 19.5 us: even_attention(): pl.pallas_call(functools.partial(even_body, per_step=per_step), out_shape...]
    all_to_all x4, waiting for transfers between devices: 21.2 us -> 47.2 us  [swap(): return lax.all_to_all(x, BOTH, 0, 0, axis_index_groups=groups, tiled=True)]
    pallas_call x2, Pallas kernels: 42.4 us -> 30.9 us  [odd_attention(): pl.pallas_call(odd_body, out_shape=jax.ShapeDtypeStruct(prior.shape, F32)...]
    ppermute x2, waiting for transfers between devices: 88.7 us -> 94.4 us  [share(): lax.ppermute(half, 'mp', [(m, (m + k) % parts) for m in range(parts)])]
  transfers between devices with their start and end apart: 16 -> 16, of which waited for: 10 -> 10; matrix products, arithmetic and copies ran while one was open for 5% -> 5% of each run, Pallas kernels for 21% -> 14%
where the time goes in v6:
time: 436 us; the launch traced here: 434 us
  waiting for transfers between devices  263 us (60%)
  Pallas kernels  80.8 us (19%)
  starting transfers between devices  50.4 us (12%)
  local copies, waits for them, and re-layouts  18.6 us (4%)
  between operations  14.2 us (3%)
  other arithmetic  7.48 us (2%)
    ppermute x6, waiting for transfers between devices, across(): moved.append(lax.ppermute(blocks[k], BOTH, pairs))  121 us
    ppermute x2, waiting for transfers between devices, share(): lax.ppermute(half, 'mp', [(m, (m + k) % parts) for m in range(parts)])  94.4 us
    all_to_all x4, waiting for transfers between devices, swap(): return lax.all_to_all(x, BOTH, 0, 0, axis_index_groups=groups, tiled=True)  47.2 us
    pallas_call x2, Pallas kernels, odd_attention(): pl.pallas_call(odd_body, out_shape=jax.ShapeDtypeStruct(prior.shape, F32)...  30.9 us
    all_to_all x4, starting transfers between devices, swap(): return lax.all_to_all(x, BOTH, 0, 0, axis_index_groups=groups, tiled=True)  21.3 us
    pallas_call x1, Pallas kernels, even_attention(): pl.pallas_call(functools.partial(even_body, per_step=per_step), out_shape...  19.5 us
    pallas_call x1, Pallas kernels, project(): pl.pallas_call(project_body, out_shape=jax.ShapeDtypeStruct((count * toke...  13.2 us
    pallas_call x2, Pallas kernels, gather_rows(): pl.pallas_call(functools.partial(gather_body, count=len(sources)), out_sh...  9.67 us
  transfers between devices with their start and end apart: 16, of which 10 were waited for; matrix products, arithmetic and copies ran while one was open for 5% of the time, Pallas kernels for 14%

profile of v6, /device:TPU:11, one launch (start us, length us, event | category | flops | bytes accessed | tf_op | source)
XLA Modules:
  0.0 434.4 jit_solution(1789781107062195796)
XLA Ops:
  6.5 0.8 copy.59
  7.3 0.1 reshape.198
  7.4 0.8 copy.60
  8.3 0.6 broadcast_in_dim.118
  9.0 6.5 %all-to-all-start.2 = ((s32[16,1,128]{2,1,0:T(1,128)}), s32[16,1,128]{2,1,0:T(1,128)S(1)}, u32[]{:S(2)}, u32[]{:S(2)}) async-start(s32[16,1,128]{2,1,0:T(1,128)} %broadcast_in_dim.118), calls=%async_computation.2 | async-start | bytes 16384 | tf_op jit(solution)/shard_map/all_to_all | solution.py:340
  15.5 1.7 pad_maximum_fusion.1
  17.3 2.6 copy.82
  19.9 3.0 slice_bitcast_fusion.1
  22.9 1.0 slice.42
  24.1 4.3 all-to-all-start.3
  28.7 0.2 copy.64
  28.8 0.1 add.167
  29.0 0.2 fusion
  29.3 0.1 convolution_convert_fusion
  29.4 0.9 select_reduce_fusion.1
  30.5 0.6 reshape.209.index_ref
  31.1 0.5 convert_reduce_fusion
  31.7 1.6 gather_fusion
  33.3 21.2 %all-to-all-done.3.source_ref.refs_0_ = bf16[128,8,896]{2,1,0:T(8,128)(2,1)S(1)} async-done(((bf16[128,8,896]{2,1,0:T(8,128)(2,1)}), bf16[128,8,896]{2,1,0:T(8,128)(2,1)S(1)}, u32[]{:S(2)}, u32[]{:S(2)}) %all-to-all-start.3) | async-done | bytes 1835040 | tf_op jit(solution)/shard_map/all_to_all | solution.py:321
  54.4 2.3 select_rows.2
  56.7 1.2 collective-permute-start.8
  57.9 1.0 collective-permute-start.9
  58.8 1.4 collective-permute-start.10
  60.3 6.8 %all-to-all-start.4 = ((bf16[16,8,1024]{2,1,0:T(8,128)(2,1)}), bf16[16,8,1024]{2,1,0:T(8,128)(2,1)S(1)}, u32[]{:S(2)}, u32[]{:S(2)}) async-start(bf16[16,8,1024]{2,1,0:T(8,128)(2,1)} %bitcast.23), calls=%async_computation.4 | async-start | bytes 524288 | tf_op jit(solution)/shard_map/all_to_all | solution.py:369
  67.1 0.2 select_reduce_fusion
  67.2 0.6 compare_select_fusion.12
  67.8 0.5 compare_select_fusion.13.index_ref
  68.3 10.7 %collective-permute-done.8.refs_1_ = bf16[46,8,896]{2,1,0:T(8,128)(2,1)S(1)} collective-permute-done((bf16[46,8,896]{2,1,0:T(8,128)(2,1)}, bf16[46,8,896]{2,1,0:T(8,128)(2,1)S(1)}, u32[]{:S(2)}, u32[]{:S(2)}) %collective-permute-start.8) | collective-permute-done | bytes 659488 | tf_op jit(solution)/shard_map/ppermute | solution.py:335
  79.1 44.3 %collective-permute-done.9.refs_2_ = bf16[46,8,896]{2,1,0:T(8,128)(2,1)S(1)} collective-permute-done((bf16[46,8,896]{2,1,0:T(8,128)(2,1)}, bf16[46,8,896]{2,1,0:T(8,128)(2,1)S(1)}, u32[]{:S(2)}, u32[]{:S(2)}) %collective-permute-start.9) | collective-permute-done | bytes 659488 | tf_op jit(solution)/shard_map/ppermute | solution.py:335
  123.3 2.9 collective-permute-done.10.refs_3_
  126.2 4.6 %gather_rows.6 = bf16[4,2,32,8,896]{4,3,2,1,0:T(8,128)(2,1)} custom-call(s32[128]{0:T(128)} %compare_select_fusion.13.index_ref, bf16[128,8,896]{2,1,0:T(8,128)(2,1)S(1)} %all-to-all-done.3.source_ref.refs_0_, bf16[46,8,896]{2,1,0:T(8,128)(2,1)} %copy-done.5, bf16[46,8,896]{2,1,0:T(8,128)(2,1)} %copy-done.6, bf16[46,8,896]{2,1,0:T(8,128)(2,1)} %collective-permute-done.10.refs_3_), custom_call_target="tpu_custom_call" | custom-call | tf_op jit(solution)/shard_map/gather_rows/pallas_call | solution.py:178
  130.9 0.7 copy-done
  131.6 6.2 %all-to-all-start.6 = ((bf16[256,8,896]{2,1,0:T(8,128)(2,1)}), bf16[256,8,896]{2,1,0:T(8,128)(2,1)}, u32[]{:S(2)}, u32[]{:S(2)}) async-start(bf16[256,8,896]{2,1,0:T(8,128)(2,1)} %bitcast.64), calls=%async_computation.6 | async-start | bytes 7340032 | tf_op jit(solution)/shard_map/all_to_all | solution.py:321
  137.8 1.2 collective-permute-start.6
  139.0 80.1 %collective-permute-done.6.refs_1_ = bf16[8,16,8,896]{3,2,1,0:T(8,128)(2,1)} collective-permute-done((bf16[8,16,8,896]{3,2,1,0:T(8,128)(2,1)}, bf16[8,16,8,896]{3,2,1,0:T(8,128)(2,1)}, u32[]{:S(2)}, u32[]{:S(2)}) %collective-permute-start.6) | collective-permute-done | bytes 1835040 | tf_op jit(solution)/shard_map/ppermute | solution.py:378
  219.2 0.1 collective-permute-start.7
  219.3 1.3 dynamic-slice_bitcast_fusion.1
  220.5 1.3 dynamic-slice_bitcast_fusion
  221.8 1.4 pad_maximum_fusion
  223.2 5.3 %all-to-all-start.5 = ((bf16[128,8,896]{2,1,0:T(8,128)(2,1)}), bf16[128,8,896]{2,1,0:T(8,128)(2,1)}, u32[]{:S(2)}, u32[]{:S(2)}) async-start(bf16[128,8,896]{2,1,0:T(8,128)(2,1)} %bitcast.68), calls=%async_computation.5 | async-start | bytes 3670016 | tf_op jit(solution)/shard_map/all_to_all | solution.py:321
  228.7 0.4 select_reduce_fusion.2
  229.3 0.7 broadcast_in_dim.125.want_ref
  230.0 0.9 broadcast_in_dim.126.refs_3_
  230.9 15.5 %odd_attention.2.refs_3_ = f32[128,1152]{1,0:T(8,128)} custom-call(bf16[128,1024]{1,0:T(8,128)(2,1)} %bitcast.74, s32[128,128]{1,0:T(8,128)} %broadcast_in_dim.125.want_ref, bf16[8,16,8,896]{3,2,1,0:T(8,128)(2,1)} %get-tuple-element.64.refs_0_, bf16[8,16,8,896]{3,2,1,0:T(8,128)(2,1)} %get-tuple-element.61.refs_1_, ...), custom_call_target="tpu_custom_call" | custom-call | tf_op jit(solution)/shard_map/odd_attention/pallas_call | solution.py:282
  246.3 14.2 %collective-permute-done.7.refs_0_ = bf16[8,16,8,896]{3,2,1,0:T(8,128)(2,1)} collective-permute-done((bf16[8,16,8,896]{3,2,1,0:T(8,128)(2,1)}, bf16[8,16,8,896]{3,2,1,0:T(8,128)(2,1)}, u32[]{:S(2)}, u32[]{:S(2)}) %collective-permute-start.7) | collective-permute-done | bytes 1835040 | tf_op jit(solution)/shard_map/ppermute | solution.py:378
  260.6 0.7 broadcast_in_dim.124.want_ref
  261.3 15.5 %odd_attention.3 = f32[128,1152]{1,0:T(8,128)} custom-call(bf16[128,1024]{1,0:T(8,128)(2,1)} %bitcast.75, s32[128,128]{1,0:T(8,128)} %broadcast_in_dim.124.want_ref, bf16[8,16,8,896]{3,2,1,0:T(8,128)(2,1)} %collective-permute-done.7.refs_0_, bf16[8,16,8,896]{3,2,1,0:T(8,128)(2,1)} %collective-permute-done.6.refs_1_, ...), custom_call_target="tpu_custom_call" | custom-call | tf_op jit(solution)/shard_map/odd_attention/pallas_call | solution.py:282
  276.8 7.3 %all-to-all-start.7 = ((f32[16,8,1152]{2,1,0:T(8,128)}), f32[16,8,1152]{2,1,0:T(8,128)S(1)}, u32[]{:S(2)}, u32[]{:S(2)}) async-start(f32[16,8,1152]{2,1,0:T(8,128)} %bitcast.73), calls=%async_computation.7 | async-start | bytes 1179648 | tf_op jit(solution)/shard_map/all_to_all | solution.py:462
  284.1 0.7 reshape.212.index_ref
  284.8 3.7 select_rows.3
  288.5 1.2 collective-permute-start.11
  289.7 1.2 collective-permute-start.12
  290.9 1.2 collective-permute-start.13
  292.0 47.4 %collective-permute-done.11.refs_1_ = bf16[46,8,896]{2,1,0:T(8,128)(2,1)S(1)} collective-permute-done((bf16[46,8,896]{2,1,0:T(8,128)(2,1)}, bf16[46,8,896]{2,1,0:T(8,128)(2,1)S(1)}, u32[]{:S(2)}, u32[]{:S(2)}) %collective-permute-start.11) | collective-permute-done | bytes 659488 | tf_op jit(solution)/shard_map/ppermute | solution.py:335
  339.4 14.1 %collective-permute-done.12.refs_2_ = bf16[46,8,896]{2,1,0:T(8,128)(2,1)} collective-permute-done((bf16[46,8,896]{2,1,0:T(8,128)(2,1)}, bf16[46,8,896]{2,1,0:T(8,128)(2,1)}, u32[]{:S(2)}, u32[]{:S(2)}) %collective-permute-start.12) | collective-permute-done | bytes 659488 | tf_op jit(solution)/shard_map/ppermute | solution.py:335
  353.6 1.9 collective-permute-done.13.refs_3_
  355.4 5.0 %gather_rows.7 = bf16[4,2,32,8,896]{4,3,2,1,0:T(8,128)(2,1)} custom-call(s32[128]{0:T(128)} %get-tuple-element.79.index_ref, bf16[128,8,896]{2,1,0:T(8,128)(2,1)} %all-to-all-done.5.source_ref.refs_0_, bf16[46,8,896]{2,1,0:T(8,128)(2,1)} %copy-done.7, bf16[46,8,896]{2,1,0:T(8,128)(2,1)} %collective-permute-done.12.refs_2_, ...), custom_call_target="tpu_custom_call" | custom-call | tf_op jit(solution)/shard_map/gather_rows/pallas_call | solution.py:178
  360.5 5.6 %all-to-all-start.8 = ((bf16[256,8,896]{2,1,0:T(8,128)(2,1)}), bf16[256,8,896]{2,1,0:T(8,128)(2,1)}, u32[]{:S(2)}, u32[]{:S(2)}) async-start(bf16[256,8,896]{2,1,0:T(8,128)(2,1)} %bitcast.65), calls=%async_computation.8 | async-start | bytes 7340032 | tf_op jit(solution)/shard_map/all_to_all | solution.py:321
  366.1 0.1 convert_reduce_fusion.1
  366.2 0.6 select_reduce_fusion.5
  367.4 13.2 %project.3.early_ref = bf16[2048,2048]{1,0:T(8,128)(2,1)} custom-call(bf16[8,32,8,896]{3,2,1,0:T(8,128)(2,1)} %bitcast.36.rows_ref, bf16[896,2048]{1,0:T(8,128)(2,1)} %all-gather.2.cloned.1.call-done.refs_2_.weight_ref), custom_call_target="tpu_custom_call" | custom-call | tf_op jit(solution)/shard_map/project/pallas_call | solution.py:42
  380.6 1.5 combine.3.odd_ref
  382.0 26.0 %all-to-all-done.8 = bf16[256,8,896]{2,1,0:T(8,128)(2,1)} async-done(((bf16[256,8,896]{2,1,0:T(8,128)(2,1)}), bf16[256,8,896]{2,1,0:T(8,128)(2,1)}, u32[]{:S(2)}, u32[]{:S(2)}) %all-to-all-start.8) | async-done | bytes 3670048 | tf_op jit(solution)/shard_map/all_to_all | solution.py:321
  408.0 19.5 %even_attention.3 = bf16[2048,1024]{1,0:T(8,128)(2,1)} custom-call(bf16[2048,1024]{1,0:T(8,128)(2,1)} %query_ref.1, bf16[8,32,8,896]{3,2,1,0:T(8,128)(2,1)} %bitcast.35.rows_ref, bf16[896,2048]{1,0:T(8,128)(2,1)} %all-gather.2.cloned.1.call-done.refs_2_.weight_ref, bf16[2048,2048]{1,0:T(8,128)(2,1)} %project.3.early_ref, f32[16,1024]{1,0:T(8,128)} %combine.3.odd_ref), custom_call_target="tpu_custom_call" | custom-call | tf_op jit(solution)/shard_map/even_attention/pallas_call | solution.py:101
  (50 shorter events, 1.6 us)
Async XLA Ops:
  9.0 15.0 %all-to-all-start.2 = ((s32[16,1,128]{2,1,0:T(1,128)}), s32[16,1,128]{2,1,0:T(1,128)S(1)}, u32[]{:S(2)}, u32[]{:S(2)}) async-start(s32[16,1,128]{2,1,0:T(1,128)} %broadcast_in_dim.118), calls=%async_computation.2 | async-start | bytes 16384 | tf_op jit(solution)/shard_map/all_to_all | solution.py:340
  15.5 213.8 %all-gather.2.cloned.1.call-start = ((), (), s32[]{:S(2)}) async-start(), calls=%async_computation.9 | async-start | bytes 3899392 | tf_op jit(solution)/shard_map/all_gather | solution.py:345
  24.1 30.3 %all-to-all-start.3 = ((bf16[128,8,896]{2,1,0:T(8,128)(2,1)}), bf16[128,8,896]{2,1,0:T(8,128)(2,1)S(1)}, u32[]{:S(2)}, u32[]{:S(2)}) async-start(bf16[128,8,896]{2,1,0:T(8,128)(2,1)} %bitcast.69), calls=%async_computation.3 | async-start | bytes 3670016 | tf_op jit(solution)/shard_map/all_to_all | solution.py:321
  56.7 22.4 %collective-permute-start.8 = (bf16[46,8,896]{2,1,0:T(8,128)(2,1)}, bf16[46,8,896]{2,1,0:T(8,128)(2,1)S(1)}, u32[]{:S(2)}, u32[]{:S(2)}) collective-permute-start(bf16[46,8,896]{2,1,0:T(8,128)(2,1)} %get-tuple-element.65), channel_id=1, source_target_pairs={{0,8},{1,9},{2,10},{3,11},{4,12},{5,13},{6,14},{7,15},{8,16},{9,17... | collective-permute-start | bytes 1978376 | tf_op jit(solution)/shard_map/ppermute | solution.py:335
  57.9 65.5 %collective-permute-start.9 = (bf16[46,8,896]{2,1,0:T(8,128)(2,1)}, bf16[46,8,896]{2,1,0:T(8,128)(2,1)S(1)}, u32[]{:S(2)}, u32[]{:S(2)}) collective-permute-start(bf16[46,8,896]{2,1,0:T(8,128)(2,1)} %get-tuple-element.66), channel_id=1, source_target_pairs={{0,16},{1,17},{2,18},{3,19},{4,20},{5,21},{6,22},{7,23},{8,24},{9,... | collective-permute-start | bytes 1978376 | tf_op jit(solution)/shard_map/ppermute | solution.py:335
  58.8 67.4 %collective-permute-start.10 = (bf16[46,8,896]{2,1,0:T(8,128)(2,1)}, bf16[46,8,896]{2,1,0:T(8,128)(2,1)}, u32[]{:S(2)}, u32[]{:S(2)}) collective-permute-start(bf16[46,8,896]{2,1,0:T(8,128)(2,1)} %get-tuple-element.67), channel_id=1, source_target_pairs={{0,24},{1,25},{2,26},{3,27},{4,28},{5,29},{6,30},{7,31},{8,0},{9,1... | collective-permute-start | bytes 1978376 | tf_op jit(solution)/shard_map/ppermute | solution.py:335
  60.3 70.6 %all-to-all-start.4 = ((bf16[16,8,1024]{2,1,0:T(8,128)(2,1)}), bf16[16,8,1024]{2,1,0:T(8,128)(2,1)S(1)}, u32[]{:S(2)}, u32[]{:S(2)}) async-start(bf16[16,8,1024]{2,1,0:T(8,128)(2,1)} %bitcast.23), calls=%async_computation.4 | async-start | bytes 524288 | tf_op jit(solution)/shard_map/all_to_all | solution.py:369
  79.1 47.1 %copy-start.5 = (bf16[46,8,896]{2,1,0:T(8,128)(2,1)}, bf16[46,8,896]{2,1,0:T(8,128)(2,1)S(1)}, u32[]{:S(2)}) copy-start(bf16[46,8,896]{2,1,0:T(8,128)(2,1)S(1)} %collective-permute-done.8.refs_1_) | copy-start | bytes 1978372
  123.3 2.9 copy-start.6
  130.9 0.7 copy-start
  131.6 91.6 %all-to-all-start.6 = ((bf16[256,8,896]{2,1,0:T(8,128)(2,1)}), bf16[256,8,896]{2,1,0:T(8,128)(2,1)}, u32[]{:S(2)}, u32[]{:S(2)}) async-start(bf16[256,8,896]{2,1,0:T(8,128)(2,1)} %bitcast.64), calls=%async_computation.6 | async-start | bytes 7340032 | tf_op jit(solution)/shard_map/all_to_all | solution.py:321
  137.8 81.3 %collective-permute-start.6 = (bf16[8,16,8,896]{3,2,1,0:T(8,128)(2,1)}, bf16[8,16,8,896]{3,2,1,0:T(8,128)(2,1)}, u32[]{:S(2)}, u32[]{:S(2)}) collective-permute-start(bf16[8,16,8,896]{3,2,1,0:T(8,128)(2,1)} %get-tuple-element.61.refs_1_), channel_id=1, source_target_pairs={{0,1},{1,0},{2,3},{3,2},{4,5},{5,4},{6,7},{7,6},{8,9},{9,8},{10,11... | collective-permute-start | bytes 5505032 | tf_op jit(solution)/shard_map/ppermute | solution.py:378
  219.2 41.4 %collective-permute-start.7 = (bf16[8,16,8,896]{3,2,1,0:T(8,128)(2,1)}, bf16[8,16,8,896]{3,2,1,0:T(8,128)(2,1)}, u32[]{:S(2)}, u32[]{:S(2)}) collective-permute-start(bf16[8,16,8,896]{3,2,1,0:T(8,128)(2,1)} %get-tuple-element.64.refs_0_), channel_id=1, source_target_pairs={{0,1},{1,0},{2,3},{3,2},{4,5},{5,4},{6,7},{7,6},{8,9},{9,8},{10,11... | collective-permute-start | bytes 5505032 | tf_op jit(solution)/shard_map/ppermute | solution.py:378
  223.2 53.6 %all-to-all-start.5 = ((bf16[128,8,896]{2,1,0:T(8,128)(2,1)}), bf16[128,8,896]{2,1,0:T(8,128)(2,1)}, u32[]{:S(2)}, u32[]{:S(2)}) async-start(bf16[128,8,896]{2,1,0:T(8,128)(2,1)} %bitcast.68), calls=%async_computation.5 | async-start | bytes 3670016 | tf_op jit(solution)/shard_map/all_to_all | solution.py:321
  276.8 83.7 %all-to-all-start.7 = ((f32[16,8,1152]{2,1,0:T(8,128)}), f32[16,8,1152]{2,1,0:T(8,128)S(1)}, u32[]{:S(2)}, u32[]{:S(2)}) async-start(f32[16,8,1152]{2,1,0:T(8,128)} %bitcast.73), calls=%async_computation.7 | async-start | bytes 1179648 | tf_op jit(solution)/shard_map/all_to_all | solution.py:462
  288.5 50.9 %collective-permute-start.11 = (bf16[46,8,896]{2,1,0:T(8,128)(2,1)}, bf16[46,8,896]{2,1,0:T(8,128)(2,1)S(1)}, u32[]{:S(2)}, u32[]{:S(2)}) collective-permute-start(bf16[46,8,896]{2,1,0:T(8,128)(2,1)} %get-tuple-element.74), channel_id=1, source_target_pairs={{0,8},{1,9},{2,10},{3,11},{4,12},{5,13},{6,14},{7,15},{8,16},{9,17... | collective-permute-start | bytes 1978376 | tf_op jit(solution)/shard_map/ppermute | solution.py:335
  289.7 63.9 %collective-permute-start.12 = (bf16[46,8,896]{2,1,0:T(8,128)(2,1)}, bf16[46,8,896]{2,1,0:T(8,128)(2,1)}, u32[]{:S(2)}, u32[]{:S(2)}) collective-permute-start(bf16[46,8,896]{2,1,0:T(8,128)(2,1)} %get-tuple-element.75), channel_id=1, source_target_pairs={{0,16},{1,17},{2,18},{3,19},{4,20},{5,21},{6,22},{7,23},{8,24},{9,... | collective-permute-start | bytes 1978376 | tf_op jit(solution)/shard_map/ppermute | solution.py:335
  290.9 64.6 %collective-permute-start.13 = (bf16[46,8,896]{2,1,0:T(8,128)(2,1)}, bf16[46,8,896]{2,1,0:T(8,128)(2,1)}, u32[]{:S(2)}, u32[]{:S(2)}) collective-permute-start(bf16[46,8,896]{2,1,0:T(8,128)(2,1)} %get-tuple-element.76), channel_id=1, source_target_pairs={{0,24},{1,25},{2,26},{3,27},{4,28},{5,29},{6,30},{7,31},{8,0},{9,1... | collective-permute-start | bytes 1978376 | tf_op jit(solution)/shard_map/ppermute | solution.py:335
  339.4 16.0 %copy-start.7 = (bf16[46,8,896]{2,1,0:T(8,128)(2,1)}, bf16[46,8,896]{2,1,0:T(8,128)(2,1)S(1)}, u32[]{:S(2)}) copy-start(bf16[46,8,896]{2,1,0:T(8,128)(2,1)S(1)} %collective-permute-done.11.refs_1_) | copy-start | bytes 1978372
  360.5 47.5 %all-to-all-start.8 = ((bf16[256,8,896]{2,1,0:T(8,128)(2,1)}), bf16[256,8,896]{2,1,0:T(8,128)(2,1)}, u32[]{:S(2)}, u32[]{:S(2)}) async-start(bf16[256,8,896]{2,1,0:T(8,128)(2,1)} %bitcast.65), calls=%async_computation.8 | async-start | bytes 7340032 | tf_op jit(solution)/shard_map/all_to_all | solution.py:321
Sparse Core Ops, SparseCore 0:
  18.6 63.9 all-gather.1

commit v7 on v6

--- a/solution.py
+++ b/solution.py
@@ -24,15 +24,21 @@
 CONTRACT_LAST = (((1,), (1,)), ((), ()))
 
 
-def project_rows(rows_ref, weight_ref):
-    lanes, count, piece, width = rows_ref.shape
-    rows = rows_ref[...]
-    stacked = jnp.concatenate([rows[:, j].reshape(lanes * piece, width) for j in range(count)], axis=0)
+def project_rows(rows_refs, weight_ref):
+    lanes, count, piece, _ = rows_refs[0].shape
+    rows = [ref[...] for ref in rows_refs]
+    stacked = jnp.concatenate(
+        [
+            jnp.concatenate([r[:, j].reshape(lanes * piece, r.shape[3]) for r in rows], axis=1)
+            for j in range(count)
+        ],
+        axis=0,
+    )
     return jnp.dot(stacked, weight_ref[...], preferred_element_type=F32).astype(BF16)
 
 
 def project_body(rows_ref, weight_ref, out_ref):
-    out_ref[...] = project_rows(rows_ref, weight_ref)
+    out_ref[...] = project_rows([rows_ref], weight_ref)
 
 
 def project(rows, weights):
@@ -52,9 +58,10 @@
     )(rows, weights)
 
 
-def even_body(query_ref, rows_ref, weight_ref, early_ref, odd_ref, out_ref, *, per_step):
+def even_body(query_ref, *refs, per_step):
+    rows_refs, (weight_ref, early_ref, odd_ref, out_ref) = refs[:-4], refs[-4:]
     columns = query_ref.shape[1]
-    late = project_rows(rows_ref, weight_ref)
+    late = project_rows(rows_refs, weight_ref)
     span = late.shape[0] // per_step
     first = SPAN - 1
     position = LOW + lax.broadcasted_iota(jnp.int32, (SEQ - LOW, DH), 0)
@@ -94,7 +101,7 @@
 def even_attention(queries, rows, weights, early, odd):
     columns = queries.shape[1]
     sequences = queries.shape[0] // SEQ
-    lanes, count, piece, width = rows.shape
+    lanes, count, piece, _ = rows[0].shape
     per_step = math.gcd(sequences, 2)
     rows_step = per_step * count // sequences
     query_spec = pl.BlockSpec((per_step * SEQ, columns), lambda i: (i, 0))
@@ -104,14 +111,14 @@
         grid=(sequences // per_step,),
         in_specs=[
             query_spec,
-            pl.BlockSpec((lanes, rows_step, piece, width), lambda i: (0, i, 0, 0)),
+            *[pl.BlockSpec((lanes, rows_step, piece, r.shape[3]), lambda i: (0, i, 0, 0)) for r in rows],
             pl.BlockSpec(weights.shape, lambda i: (0, 0)),
             pl.BlockSpec((rows_step * lanes * piece, weights.shape[1]), lambda i: (i, 0)),
             pl.BlockSpec(odd.shape, lambda i: (0, 0)),
         ],
         out_specs=query_spec,
         name="even_attention",
-    )(queries, rows, weights, early, odd)
+    )(queries, *rows, weights, early, odd)
 
 
 def combine_body(slot_ref, odd_ref, row_ref, *picked_refs):
@@ -337,9 +344,8 @@
 
     table = jnp.concatenate([nbr_shard.reshape(-1), nbr_row.reshape(-1)])
     table = jnp.broadcast_to(table[None, None], (shards, 1, table.shape[0]))
-    table = lax.all_to_all(table, "db", 0, 0, tiled=True).reshape(
-        shards, 2, sequences, SEQ // SPAN, neighbours
-    )
+    table = lax.all_to_all(table, "db", 0, 0, tiled=True)
+    table = table.reshape(shards, 2, sequences, SEQ // SPAN, neighbours)
     table_shard, table_row = table[:, 0], table[:, 1]
 
     weights = lax.all_gather(
@@ -365,9 +371,6 @@
     sender = jnp.sum(jnp.where(chosen, (earlier // neighbours).astype(jnp.int32)[None, :], 0), axis=1)
     last_rows = queries.reshape(sequences, SEQ, columns)[:, SEQ - 1]
     odd_query = jnp.take(last_rows, sender, axis=0, mode="clip").reshape(shards, capacity, columns)
-    odd_query, _ = lax.optimization_barrier((odd_query, first))
-    odd_query = lax.all_to_all(odd_query, "db", 0, 0, tiled=True)
-    odd_query = odd_query.reshape(shards * capacity, columns)
 
     part_index = lax.axis_index("mp")
 
@@ -389,11 +392,15 @@
     part_groups = [
         [a * lanes + g * parts + m for g in range(group)] for a in range(planes) for m in range(parts)
     ]
-    second, _ = lax.optimization_barrier((second, odd_query))
+    second, _ = lax.optimization_barrier((second, first))
     if group > 1:
         second = swap(second, part_groups)
     early_shared = share(early_half, late_shared)
-    plane_pieces = [first, second]
+    odd_query, _ = lax.optimization_barrier((odd_query, second))
+    odd_query = lax.all_to_all(odd_query, "db", 0, 0, tiled=True)
+    odd_query = odd_query.reshape(shards * capacity, columns)
+    cut = (width // DH + 1) // 2 * DH
+    plane_pieces = [first, second[:, :, :cut], second[:, :, cut:]]
 
     def stepped(row):
         step = (part_index + parts - row % shard_rows // held) % parts
@@ -441,11 +448,11 @@
             if received:
                 sending, _ = lax.optimization_barrier((sending, received[-1]))
             received.append(across(sending))
-            outgoing = gather_rows(index[chunk], received[-1], group, parts)
+            outgoing = gather_rows(index[min(chunk, 1)], received[-1], group, parts)
             outgoing, _ = lax.optimization_barrier((outgoing, after if arrived else odd_query))
             arrived.append(swap(outgoing, plane_groups))
             after = arrived[-1] if chunk else between(arrived[-1])
-        return [a.reshape(lanes, wanted, piece, width) for a in arrived]
+        return [a.reshape(lanes, wanted, piece, a.shape[2]) for a in arrived]
 
     odd_part = jnp.zeros((shards * capacity, columns + DH), F32)
     for k in range(parts):
@@ -464,7 +471,7 @@
         return part
 
     def attend(select, index, between, odd_rows):
-        early, late = exchange(plane_pieces, select, index, between)
+        early, *late = exchange(plane_pieces, select, index, between)
         early = project(early, weights)
         return even_attention(queries, late, weights, early, odd_rows())
 

time: 436 us -> 416 us (0.954)
  waiting for transfers between devices: 263 us -> 231 us
  starting transfers between devices: 50.4 us -> 55.7 us
    all_to_all x4 -> x5, waiting for transfers between devices: 47.2 us -> 22.3 us  [swap(): return lax.all_to_all(x, BOTH, 0, 0, axis_index_groups=groups, tiled=True)]
    ppermute x6 -> x9, waiting for transfers between devices: 121 us -> 105 us  [across(): moved.append(lax.ppermute(blocks[k], BOTH, pairs))]
    ppermute x2, waiting for transfers between devices: 94.4 us -> 104 us  [share(): lax.ppermute(half, 'mp', [(m, (m + k) % parts) for m in range(parts)])]
    all_to_all x4 -> x5, starting transfers between devices: 21.3 us -> 24.1 us  [swap(): return lax.all_to_all(x, BOTH, 0, 0, axis_index_groups=groups, tiled=True)]
    ppermute x6 -> x9, starting transfers between devices: 7.15 us -> 9.78 us  [across(): moved.append(lax.ppermute(blocks[k], BOTH, pairs))]
    pallas_call x2 -> x3, Pallas kernels: 9.67 us -> 12.3 us  [gather_rows(): pl.pallas_call(functools.partial(gather_body, count=len(sources)), out_sh...]
  transfers between devices with their start and end apart: 16 -> 20, of which waited for: 10 -> 13; matrix products, arithmetic and copies ran while one was open for 5% -> 6% of each run, Pallas kernels for 14% -> 16%
where the time goes in v7:
time: 416 us; the launch traced here: 415 us
  waiting for transfers between devices  231 us (56%)
  Pallas kernels  84.9 us (20%)
  starting transfers between devices  55.7 us (13%)
  local copies, waits for them, and re-layouts  22 us (5%)
  between operations  14.3 us (3%)
  other arithmetic  6.58 us (2%)
    ppermute x9, waiting for transfers between devices, across(): moved.append(lax.ppermute(blocks[k], BOTH, pairs))  105 us
    ppermute x2, waiting for transfers between devices, share(): lax.ppermute(half, 'mp', [(m, (m + k) % parts) for m in range(parts)])  104 us
    pallas_call x2, Pallas kernels, odd_attention(): pl.pallas_call(odd_body, out_shape=jax.ShapeDtypeStruct(prior.shape, F32)...  31 us
    all_to_all x5, starting transfers between devices, swap(): return lax.all_to_all(x, BOTH, 0, 0, axis_index_groups=groups, tiled=True)  24.1 us
    all_to_all x5, waiting for transfers between devices, swap(): return lax.all_to_all(x, BOTH, 0, 0, axis_index_groups=groups, tiled=True)  22.3 us
    pallas_call x1, Pallas kernels, even_attention(): pl.pallas_call(functools.partial(even_body, per_step=per_step), out_shape...  19.7 us
    pallas_call x1, Pallas kernels, project(): pl.pallas_call(project_body, out_shape=jax.ShapeDtypeStruct((count * toke...  13.2 us
    pallas_call x3, Pallas kernels, gather_rows(): pl.pallas_call(functools.partial(gather_body, count=len(sources)), out_sh...  12.3 us
  transfers between devices with their start and end apart: 20, of which 13 were waited for; matrix products, arithmetic and copies ran while one was open for 6% of the time, Pallas kernels for 16%

profile of v7, /device:TPU:11, one launch (start us, length us, event | category | flops | bytes accessed | tf_op | source)
XLA Modules:
  0.0 415.1 jit_solution(5446351394544794254)
XLA Ops:
  6.5 0.8 copy.59
  7.4 0.8 copy.60
  8.3 0.6 broadcast_in_dim.118
  9.0 6.5 %all-to-all-start.3 = ((s32[16,1,128]{2,1,0:T(1,128)}), s32[16,1,128]{2,1,0:T(1,128)S(1)}, u32[]{:S(2)}, u32[]{:S(2)}) async-start(s32[16,1,128]{2,1,0:T(1,128)} %broadcast_in_dim.118), calls=%async_computation.3 | async-start | bytes 16384 | tf_op jit(solution)/shard_map/all_to_all | solution.py:347
  15.5 2.6 copy.82
  18.1 3.0 slice_bitcast_fusion.1
  21.2 1.3 collective-permute-start.9
  22.5 0.7 pad_maximum_fusion.1
  23.2 4.4 %all-to-all-start.4 = ((bf16[128,8,896]{2,1,0:T(8,128)(2,1)}), bf16[128,8,896]{2,1,0:T(8,128)(2,1)S(1)}, u32[]{:S(2)}, u32[]{:S(2)}) async-start(bf16[128,8,896]{2,1,0:T(8,128)(2,1)} %bitcast.72), calls=%async_computation.4 | async-start | bytes 3670016 | tf_op jit(solution)/shard_map/all_to_all | solution.py:328
  27.6 1.0 slice.53
  29.3 1.3 dynamic-slice_bitcast_fusion.1
  30.6 42.0 %collective-permute-done.9.refs_1_ = bf16[8,16,8,896]{3,2,1,0:T(8,128)(2,1)} collective-permute-done((bf16[8,16,8,896]{3,2,1,0:T(8,128)(2,1)}, bf16[8,16,8,896]{3,2,1,0:T(8,128)(2,1)}, u32[]{:S(2)}, u32[]{:S(2)}) %collective-permute-start.9) | collective-permute-done | bytes 1835040 | tf_op jit(solution)/shard_map/ppermute | solution.py:381
  72.6 1.3 dynamic-slice_bitcast_fusion
  73.8 1.4 pad_maximum_fusion
  75.3 7.6 %all-to-all-done.4.source_ref.refs_0_ = bf16[128,8,896]{2,1,0:T(8,128)(2,1)S(1)} async-done(((bf16[128,8,896]{2,1,0:T(8,128)(2,1)}), bf16[128,8,896]{2,1,0:T(8,128)(2,1)S(1)}, u32[]{:S(2)}, u32[]{:S(2)}) %all-to-all-start.4) | async-done | bytes 1835040 | tf_op jit(solution)/shard_map/all_to_all | solution.py:328
  82.9 4.4 %all-to-all-start.5 = ((bf16[128,8,896]{2,1,0:T(8,128)(2,1)}), bf16[128,8,896]{2,1,0:T(8,128)(2,1)}, u32[]{:S(2)}, u32[]{:S(2)}) async-start(bf16[128,8,896]{2,1,0:T(8,128)(2,1)} %bitcast.71), calls=%async_computation.5 | async-start | bytes 3670016 | tf_op jit(solution)/shard_map/all_to_all | solution.py:328
  87.8 0.9 select_reduce_fusion.1
  88.9 0.6 reshape.222.index_ref
  90.1 1.6 gather_fusion
  91.6 2.3 select_rows.3
  93.9 1.2 collective-permute-start.11
  95.1 1.2 collective-permute-start.12
  96.3 1.2 collective-permute-start.13
  97.5 11.2 %all-to-all-done.5 = bf16[128,8,896]{2,1,0:T(8,128)(2,1)} async-done(((bf16[128,8,896]{2,1,0:T(8,128)(2,1)}), bf16[128,8,896]{2,1,0:T(8,128)(2,1)}, u32[]{:S(2)}, u32[]{:S(2)}) %all-to-all-start.5) | async-done | bytes 1835040 | tf_op jit(solution)/shard_map/all_to_all | solution.py:328
  108.7 6.0 %all-to-all-start.6 = ((bf16[16,8,1024]{2,1,0:T(8,128)(2,1)}), bf16[16,8,1024]{2,1,0:T(8,128)(2,1)S(1)}, u32[]{:S(2)}, u32[]{:S(2)}) async-start(bf16[16,8,1024]{2,1,0:T(8,128)(2,1)} %bitcast.25), calls=%async_computation.6 | async-start | bytes 524288 | tf_op jit(solution)/shard_map/all_to_all | solution.py:400
  115.0 0.6 compare_select_fusion.12
  116.1 38.4 %collective-permute-done.12.refs_2_ = bf16[46,8,896]{2,1,0:T(8,128)(2,1)S(1)} collective-permute-done((bf16[46,8,896]{2,1,0:T(8,128)(2,1)}, bf16[46,8,896]{2,1,0:T(8,128)(2,1)S(1)}, u32[]{:S(2)}, u32[]{:S(2)}) %collective-permute-start.12) | collective-permute-done | bytes 659488 | tf_op jit(solution)/shard_map/ppermute | solution.py:342
  154.5 2.7 collective-permute-done.13.refs_3_
  157.2 4.6 %gather_rows.9 = bf16[4,2,32,8,896]{4,3,2,1,0:T(8,128)(2,1)} custom-call(s32[128]{0:T(128)} %compare_select_fusion.13.index_ref, bf16[128,8,896]{2,1,0:T(8,128)(2,1)S(1)} %all-to-all-done.4.source_ref.refs_0_, bf16[46,8,896]{2,1,0:T(8,128)(2,1)} %copy-done.11, bf16[46,8,896]{2,1,0:T(8,128)(2,1)} %copy-done.12, ...), custom_call_target="tpu_custom_call" | custom-call | tf_op jit(solution)/shard_map/gather_rows/pallas_call | solution.py:185
  161.8 0.7 copy-done.2
  162.5 5.3 %all-to-all-start.7 = ((bf16[256,8,896]{2,1,0:T(8,128)(2,1)}), bf16[256,8,896]{2,1,0:T(8,128)(2,1)}, u32[]{:S(2)}, u32[]{:S(2)}) async-start(bf16[256,8,896]{2,1,0:T(8,128)(2,1)} %bitcast.67), calls=%async_computation.7 | async-start | bytes 7340032 | tf_op jit(solution)/shard_map/all_to_all | solution.py:328
  167.8 1.4 collective-permute-start.10
  170.0 0.7 broadcast_in_dim.125.want_ref
  170.7 0.9 broadcast_in_dim.126.refs_3_
  171.6 15.5 %odd_attention.2.refs_3_ = f32[128,1152]{1,0:T(8,128)} custom-call(bf16[128,1024]{1,0:T(8,128)(2,1)} %bitcast.80, s32[128,128]{1,0:T(8,128)} %broadcast_in_dim.125.want_ref, bf16[8,16,8,896]{3,2,1,0:T(8,128)(2,1)} %get-tuple-element.80.refs_0_, bf16[8,16,8,896]{3,2,1,0:T(8,128)(2,1)} %get-tuple-element.77.refs_1_, ...), custom_call_target="tpu_custom_call" | custom-call | tf_op jit(solution)/shard_map/odd_attention/pallas_call | solution.py:289
  187.2 62.0 %collective-permute-done.10.refs_0_ = bf16[8,16,8,896]{3,2,1,0:T(8,128)(2,1)} collective-permute-done((bf16[8,16,8,896]{3,2,1,0:T(8,128)(2,1)}, bf16[8,16,8,896]{3,2,1,0:T(8,128)(2,1)}, u32[]{:S(2)}, u32[]{:S(2)}) %collective-permute-start.10) | collective-permute-done | bytes 1835040 | tf_op jit(solution)/shard_map/ppermute | solution.py:381
  249.1 0.7 broadcast_in_dim.124.want_ref
  249.9 15.5 %odd_attention.3 = f32[128,1152]{1,0:T(8,128)} custom-call(bf16[128,1024]{1,0:T(8,128)(2,1)} %bitcast.81, s32[128,128]{1,0:T(8,128)} %broadcast_in_dim.124.want_ref, bf16[8,16,8,896]{3,2,1,0:T(8,128)(2,1)} %collective-permute-done.10.refs_0_, bf16[8,16,8,896]{3,2,1,0:T(8,128)(2,1)} %collective-permute-done.9.refs_1_, ...), custom_call_target="tpu_custom_call" | custom-call | tf_op jit(solution)/shard_map/odd_attention/pallas_call | solution.py:289
  265.3 6.6 %all-to-all-start.8 = ((f32[16,8,1152]{2,1,0:T(8,128)}), f32[16,8,1152]{2,1,0:T(8,128)S(1)}, u32[]{:S(2)}, u32[]{:S(2)}) async-start(f32[16,8,1152]{2,1,0:T(8,128)} %bitcast.79), calls=%async_computation.8 | async-start | bytes 1179648 | tf_op jit(solution)/shard_map/all_to_all | solution.py:469
  272.0 0.6 reshape.225.index_ref
  272.6 1.3 slice.51.source_ref.refs_0_
  273.9 2.0 select_rows.4
  275.9 1.2 collective-permute-start.14
  277.1 1.2 collective-permute-start.15
  278.2 1.2 collective-permute-start.16
  279.4 29.7 %collective-permute-done.14.refs_1_ = bf16[46,8,512]{2,1,0:T(8,128)(2,1)} collective-permute-done((bf16[46,8,512]{2,1,0:T(8,128)(2,1)}, bf16[46,8,512]{2,1,0:T(8,128)(2,1)}, u32[]{:S(2)}, u32[]{:S(2)}) %collective-permute-start.14) | collective-permute-done | bytes 376864 | tf_op jit(solution)/shard_map/ppermute | solution.py:342
  309.1 8.1 %collective-permute-done.15.refs_2_ = bf16[46,8,512]{2,1,0:T(8,128)(2,1)} collective-permute-done((bf16[46,8,512]{2,1,0:T(8,128)(2,1)}, bf16[46,8,512]{2,1,0:T(8,128)(2,1)}, u32[]{:S(2)}, u32[]{:S(2)}) %collective-permute-start.15) | collective-permute-done | bytes 376864 | tf_op jit(solution)/shard_map/ppermute | solution.py:342
  317.2 1.9 collective-permute-done.16.refs_3_
  319.1 3.9 gather_rows.10
  322.9 5.4 %all-to-all-start.9 = ((bf16[256,8,512]{2,1,0:T(8,128)(2,1)}), bf16[256,8,512]{2,1,0:T(8,128)(2,1)}, u32[]{:S(2)}, u32[]{:S(2)}) async-start(bf16[256,8,512]{2,1,0:T(8,128)(2,1)} %bitcast.70), calls=%async_computation.9 | async-start | bytes 4194304 | tf_op jit(solution)/shard_map/all_to_all | solution.py:328
  328.4 2.1 slice.52.source_ref.refs_0_
  330.5 3.1 select_rows.5
  333.6 1.2 collective-permute-start.18
  334.8 1.5 collective-permute-start.19
  336.2 5.6 %collective-permute-done.17.refs_1_ = bf16[46,8,384]{2,1,0:T(8,128)(2,1)} collective-permute-done((bf16[46,8,384]{2,1,0:T(8,128)(2,1)}, bf16[46,8,384]{2,1,0:T(8,128)(2,1)}, u32[]{:S(2)}, u32[]{:S(2)}) %collective-permute-start.17) | collective-permute-done | bytes 282656 | tf_op jit(solution)/shard_map/ppermute | solution.py:342
  341.8 16.3 %collective-permute-done.18.refs_2_ = bf16[46,8,384]{2,1,0:T(8,128)(2,1)} collective-permute-done((bf16[46,8,384]{2,1,0:T(8,128)(2,1)}, bf16[46,8,384]{2,1,0:T(8,128)(2,1)}, u32[]{:S(2)}, u32[]{:S(2)}) %collective-permute-start.18) | collective-permute-done | bytes 282656 | tf_op jit(solution)/shard_map/ppermute | solution.py:342
  358.0 2.5 collective-permute-done.19.refs_3_
  360.5 3.8 gather_rows.11
  364.3 4.7 %all-to-all-start.10 = ((bf16[256,8,384]{2,1,0:T(8,128)(2,1)}), bf16[256,8,384]{2,1,0:T(8,128)(2,1)}, u32[]{:S(2)}, u32[]{:S(2)}) async-start(bf16[256,8,384]{2,1,0:T(8,128)(2,1)} %bitcast.75), calls=%async_computation.10 | async-start | bytes 3145728 | tf_op jit(solution)/shard_map/all_to_all | solution.py:328
  369.2 0.6 select_reduce_fusion.5
  370.5 13.2 %project.3.refs_3_ = bf16[2048,2048]{1,0:T(8,128)(2,1)} custom-call(bf16[8,32,8,896]{3,2,1,0:T(8,128)(2,1)} %bitcast.40.rows_ref, bf16[896,2048]{1,0:T(8,128)(2,1)} %all-gather.2.cloned.1.call-done.refs_2_.weight_ref), custom_call_target="tpu_custom_call" | custom-call | tf_op jit(solution)/shard_map/project/pallas_call | solution.py:48
  383.6 1.4 combine.3.refs_4_
  385.1 3.5 all-to-all-done.10
  388.5 19.7 %even_attention.3 = bf16[2048,1024]{1,0:T(8,128)(2,1)} custom-call(bf16[2048,1024]{1,0:T(8,128)(2,1)} %query_ref.1, bf16[8,32,8,512]{3,2,1,0:T(8,128)(2,1)} %bitcast.37.refs_0_, bf16[8,32,8,384]{3,2,1,0:T(8,128)(2,1)} %bitcast.39.refs_1_, bf16[896,2048]{1,0:T(8,128)(2,1)} %all-gather.2.cloned.1.call-done.refs_2_.weight_ref, ...), custom_call_target="tpu_custom_call" | custom-call | tf_op jit(solution)/shard_map/even_attention/pallas_call | solution.py:108
  (64 shorter events, 4.0 us)
Async XLA Ops:
  9.0 12.1 %all-to-all-start.3 = ((s32[16,1,128]{2,1,0:T(1,128)}), s32[16,1,128]{2,1,0:T(1,128)S(1)}, u32[]{:S(2)}, u32[]{:S(2)}) async-start(s32[16,1,128]{2,1,0:T(1,128)} %broadcast_in_dim.118), calls=%async_computation.3 | async-start | bytes 16384 | tf_op jit(solution)/shard_map/all_to_all | solution.py:347
  15.5 154.5 %all-gather.2.cloned.1.call-start = ((), (), s32[]{:S(2)}) async-start(), calls=%async_computation.11 | async-start | bytes 3899392 | tf_op jit(solution)/shard_map/all_gather | solution.py:351
  18.1 4.4 %copy-start.13 = (bf16[56,1024]{1,0:T(8,128)(2,1)S(1)}, bf16[56,1024]{1,0:T(8,128)(2,1)}, u32[]{:S(2)}) copy-start(bf16[56,1024]{1,0:T(8,128)(2,1)} %param.11) | copy-start | bytes 344068
  18.1 4.4 %copy-start.14 = (bf16[56,1024]{1,0:T(8,128)(2,1)S(1)}, bf16[56,1024]{1,0:T(8,128)(2,1)}, u32[]{:S(2)}) copy-start(bf16[56,1024]{1,0:T(8,128)(2,1)} %param.10) | copy-start | bytes 344068
  21.2 51.4 %collective-permute-start.9 = (bf16[8,16,8,896]{3,2,1,0:T(8,128)(2,1)}, bf16[8,16,8,896]{3,2,1,0:T(8,128)(2,1)}, u32[]{:S(2)}, u32[]{:S(2)}) collective-permute-start(bf16[8,16,8,896]{3,2,1,0:T(8,128)(2,1)} %get-tuple-element.77.refs_1_), channel_id=1, source_target_pairs={{0,1},{1,0},{2,3},{3,2},{4,5},{5,4},{6,7},{7,6},{8,9},{9,8},{10,11... | collective-permute-start | bytes 5505032 | tf_op jit(solution)/shard_map/ppermute | solution.py:381
  23.2 59.6 %all-to-all-start.4 = ((bf16[128,8,896]{2,1,0:T(8,128)(2,1)}), bf16[128,8,896]{2,1,0:T(8,128)(2,1)S(1)}, u32[]{:S(2)}, u32[]{:S(2)}) async-start(bf16[128,8,896]{2,1,0:T(8,128)(2,1)} %bitcast.72), calls=%async_computation.4 | async-start | bytes 3670016 | tf_op jit(solution)/shard_map/all_to_all | solution.py:328
  82.9 25.9 %all-to-all-start.5 = ((bf16[128,8,896]{2,1,0:T(8,128)(2,1)}), bf16[128,8,896]{2,1,0:T(8,128)(2,1)}, u32[]{:S(2)}, u32[]{:S(2)}) async-start(bf16[128,8,896]{2,1,0:T(8,128)(2,1)} %bitcast.71), calls=%async_computation.5 | async-start | bytes 3670016 | tf_op jit(solution)/shard_map/all_to_all | solution.py:328
  93.9 22.2 %collective-permute-start.11 = (bf16[46,8,896]{2,1,0:T(8,128)(2,1)}, bf16[46,8,896]{2,1,0:T(8,128)(2,1)S(1)}, u32[]{:S(2)}, u32[]{:S(2)}) collective-permute-start(bf16[46,8,896]{2,1,0:T(8,128)(2,1)} %get-tuple-element.81), channel_id=1, source_target_pairs={{0,8},{1,9},{2,10},{3,11},{4,12},{5,13},{6,14},{7,15},{8,16},{9,17... | collective-permute-start | bytes 1978376 | tf_op jit(solution)/shard_map/ppermute | solution.py:342
  95.1 59.3 %collective-permute-start.12 = (bf16[46,8,896]{2,1,0:T(8,128)(2,1)}, bf16[46,8,896]{2,1,0:T(8,128)(2,1)S(1)}, u32[]{:S(2)}, u32[]{:S(2)}) collective-permute-start(bf16[46,8,896]{2,1,0:T(8,128)(2,1)} %get-tuple-element.82), channel_id=1, source_target_pairs={{0,16},{1,17},{2,18},{3,19},{4,20},{5,21},{6,22},{7,23},{8,24},{9,... | collective-permute-start | bytes 1978376 | tf_op jit(solution)/shard_map/ppermute | solution.py:342
  96.3 60.9 %collective-permute-start.13 = (bf16[46,8,896]{2,1,0:T(8,128)(2,1)}, bf16[46,8,896]{2,1,0:T(8,128)(2,1)}, u32[]{:S(2)}, u32[]{:S(2)}) collective-permute-start(bf16[46,8,896]{2,1,0:T(8,128)(2,1)} %get-tuple-element.83), channel_id=1, source_target_pairs={{0,24},{1,25},{2,26},{3,27},{4,28},{5,29},{6,30},{7,31},{8,0},{9,1... | collective-permute-start | bytes 1978376 | tf_op jit(solution)/shard_map/ppermute | solution.py:342
  108.7 53.1 %all-to-all-start.6 = ((bf16[16,8,1024]{2,1,0:T(8,128)(2,1)}), bf16[16,8,1024]{2,1,0:T(8,128)(2,1)S(1)}, u32[]{:S(2)}, u32[]{:S(2)}) async-start(bf16[16,8,1024]{2,1,0:T(8,128)(2,1)} %bitcast.25), calls=%async_computation.6 | async-start | bytes 524288 | tf_op jit(solution)/shard_map/all_to_all | solution.py:400
  116.1 41.1 %copy-start.11 = (bf16[46,8,896]{2,1,0:T(8,128)(2,1)}, bf16[46,8,896]{2,1,0:T(8,128)(2,1)S(1)}, u32[]{:S(2)}) copy-start(bf16[46,8,896]{2,1,0:T(8,128)(2,1)S(1)} %collective-permute-done.11.refs_1_) | copy-start | bytes 1978372
  154.5 2.7 copy-start.12
  161.8 0.7 copy-start.2
  162.5 102.8 %all-to-all-start.7 = ((bf16[256,8,896]{2,1,0:T(8,128)(2,1)}), bf16[256,8,896]{2,1,0:T(8,128)(2,1)}, u32[]{:S(2)}, u32[]{:S(2)}) async-start(bf16[256,8,896]{2,1,0:T(8,128)(2,1)} %bitcast.67), calls=%async_computation.7 | async-start | bytes 7340032 | tf_op jit(solution)/shard_map/all_to_all | solution.py:328
  167.8 81.3 %collective-permute-start.10 = (bf16[8,16,8,896]{3,2,1,0:T(8,128)(2,1)}, bf16[8,16,8,896]{3,2,1,0:T(8,128)(2,1)}, u32[]{:S(2)}, u32[]{:S(2)}) collective-permute-start(bf16[8,16,8,896]{3,2,1,0:T(8,128)(2,1)} %get-tuple-element.80.refs_0_), channel_id=1, source_target_pairs={{0,1},{1,0},{2,3},{3,2},{4,5},{5,4},{6,7},{7,6},{8,9},{9,8},{10,11... | collective-permute-start | bytes 5505032 | tf_op jit(solution)/shard_map/ppermute | solution.py:381
  265.3 57.6 %all-to-all-start.8 = ((f32[16,8,1152]{2,1,0:T(8,128)}), f32[16,8,1152]{2,1,0:T(8,128)S(1)}, u32[]{:S(2)}, u32[]{:S(2)}) async-start(f32[16,8,1152]{2,1,0:T(8,128)} %bitcast.79), calls=%async_computation.8 | async-start | bytes 1179648 | tf_op jit(solution)/shard_map/all_to_all | solution.py:469
  275.9 33.2 %collective-permute-start.14 = (bf16[46,8,512]{2,1,0:T(8,128)(2,1)}, bf16[46,8,512]{2,1,0:T(8,128)(2,1)}, u32[]{:S(2)}, u32[]{:S(2)}) collective-permute-start(bf16[46,8,512]{2,1,0:T(8,128)(2,1)} %get-tuple-element.90), channel_id=1, source_target_pairs={{0,8},{1,9},{2,10},{3,11},{4,12},{5,13},{6,14},{7,15},{8,16},{9,17... | collective-permute-start | bytes 1130504 | tf_op jit(solution)/shard_map/ppermute | solution.py:342
  277.1 40.1 %collective-permute-start.15 = (bf16[46,8,512]{2,1,0:T(8,128)(2,1)}, bf16[46,8,512]{2,1,0:T(8,128)(2,1)}, u32[]{:S(2)}, u32[]{:S(2)}) collective-permute-start(bf16[46,8,512]{2,1,0:T(8,128)(2,1)} %get-tuple-element.91), channel_id=1, source_target_pairs={{0,16},{1,17},{2,18},{3,19},{4,20},{5,21},{6,22},{7,23},{8,24},{9,... | collective-permute-start | bytes 1130504 | tf_op jit(solution)/shard_map/ppermute | solution.py:342
  278.2 40.8 %collective-permute-start.16 = (bf16[46,8,512]{2,1,0:T(8,128)(2,1)}, bf16[46,8,512]{2,1,0:T(8,128)(2,1)}, u32[]{:S(2)}, u32[]{:S(2)}) collective-permute-start(bf16[46,8,512]{2,1,0:T(8,128)(2,1)} %get-tuple-element.92), channel_id=1, source_target_pairs={{0,24},{1,25},{2,26},{3,27},{4,28},{5,29},{6,30},{7,31},{8,0},{9,1... | collective-permute-start | bytes 1130504 | tf_op jit(solution)/shard_map/ppermute | solution.py:342
  322.9 41.4 %all-to-all-start.9 = ((bf16[256,8,512]{2,1,0:T(8,128)(2,1)}), bf16[256,8,512]{2,1,0:T(8,128)(2,1)}, u32[]{:S(2)}, u32[]{:S(2)}) async-start(bf16[256,8,512]{2,1,0:T(8,128)(2,1)} %bitcast.70), calls=%async_computation.9 | async-start | bytes 4194304 | tf_op jit(solution)/shard_map/all_to_all | solution.py:328
  333.6 8.2 %collective-permute-start.17 = (bf16[46,8,384]{2,1,0:T(8,128)(2,1)}, bf16[46,8,384]{2,1,0:T(8,128)(2,1)}, u32[]{:S(2)}, u32[]{:S(2)}) collective-permute-start(bf16[46,8,384]{2,1,0:T(8,128)(2,1)} %get-tuple-element.98), channel_id=1, source_target_pairs={{0,8},{1,9},{2,10},{3,11},{4,12},{5,13},{6,14},{7,15},{8,16},{9,17... | collective-permute-start | bytes 847880 | tf_op jit(solution)/shard_map/ppermute | solution.py:342
  333.6 24.5 %collective-permute-start.18 = (bf16[46,8,384]{2,1,0:T(8,128)(2,1)}, bf16[46,8,384]{2,1,0:T(8,128)(2,1)}, u32[]{:S(2)}, u32[]{:S(2)}) collective-permute-start(bf16[46,8,384]{2,1,0:T(8,128)(2,1)} %get-tuple-element.99), channel_id=1, source_target_pairs={{0,16},{1,17},{2,18},{3,19},{4,20},{5,21},{6,22},{7,23},{8,24},{9,... | collective-permute-start | bytes 847880 | tf_op jit(solution)/shard_map/ppermute | solution.py:342
  334.8 25.7 %collective-permute-start.19 = (bf16[46,8,384]{2,1,0:T(8,128)(2,1)}, bf16[46,8,384]{2,1,0:T(8,128)(2,1)}, u32[]{:S(2)}, u32[]{:S(2)}) collective-permute-start(bf16[46,8,384]{2,1,0:T(8,128)(2,1)} %get-tuple-element.100), channel_id=1, source_target_pairs={{0,24},{1,25},{2,26},{3,27},{4,28},{5,29},{6,30},{7,31},{8,0},{9,1... | collective-permute-start | bytes 847880 | tf_op jit(solution)/shard_map/ppermute | solution.py:342
  364.3 24.2 %all-to-all-start.10 = ((bf16[256,8,384]{2,1,0:T(8,128)(2,1)}), bf16[256,8,384]{2,1,0:T(8,128)(2,1)}, u32[]{:S(2)}, u32[]{:S(2)}) async-start(bf16[256,8,384]{2,1,0:T(8,128)(2,1)} %bitcast.75), calls=%async_computation.10 | async-start | bytes 3145728 | tf_op jit(solution)/shard_map/all_to_all | solution.py:328
Sparse Core Ops, SparseCore 0:
  23.4 49.3 all-gather.1

commit v8 on v7

--- a/solution.py
+++ b/solution.py
@@ -231,8 +231,8 @@
     rows_refs, (weight_ref, prior_ref, out_ref) = refs[:-3], refs[-3:]
     columns = query_ref.shape[1]
     heads = columns // DH
-    lanes, per_step, piece, width = rows_refs[0].shape
-    tokens = len(rows_refs) * lanes * piece
+    _, per_step, piece, width = rows_refs[0].shape
+    tokens = sum(ref.shape[0] for ref in rows_refs) * piece
     step = pl.program_id(0)
 
     @pl.when(step == 0)
@@ -241,7 +241,7 @@
 
     pieces = [ref[...] for ref in rows_refs]
     stacked = jnp.concatenate(
-        [p[:, r].reshape(lanes * piece, width) for r in range(per_step) for p in pieces], axis=0
+        [p[:, r].reshape(p.shape[0] * piece, width) for r in range(per_step) for p in pieces], axis=0
     )
     projected = jnp.dot(stacked, weight_ref[...], preferred_element_type=F32).astype(BF16)
     want = want_ref[...] - step * per_step
@@ -283,9 +283,8 @@
 
 def odd_attention(queries, want, rows, weights, prior):
     slots, columns = queries.shape
-    lanes, count, piece, width = rows[0].shape
+    _, count, piece, width = rows[0].shape
     per_step = math.gcd(count, 4)
-    row_spec = pl.BlockSpec((lanes, per_step, piece, width), lambda i: (0, i, 0, 0))
     return pl.pallas_call(
         odd_body,
         out_shape=jax.ShapeDtypeStruct(prior.shape, F32),
@@ -293,7 +292,7 @@
         in_specs=[
             pl.BlockSpec((slots, columns), lambda i: (0, 0)),
             pl.BlockSpec((slots, DH), lambda i: (0, 0)),
-            *[row_spec for _ in rows],
+            *[pl.BlockSpec((r.shape[0], per_step, piece, width), lambda i: (0, i, 0, 0)) for r in rows],
             pl.BlockSpec(weights.shape, lambda i: (0, 0)),
             pl.BlockSpec(prior.shape, lambda i: (0, 0)),
         ],
@@ -381,13 +380,23 @@
             shared.append(lax.ppermute(half, "mp", [(m, (m + k) % parts) for m in range(parts)]))
         return shared
 
-    late_shared = share(late_half, table)
-    second = [
-        lax.dynamic_index_in_dim(
-            half.reshape(group, parts, held, piece, width), part_index, 1, keepdims=False
-        )
-        for half in late_shared
-    ]
+    by_lane = late_half.reshape(group, parts, held, piece, width)
+    near = lax.dynamic_index_in_dim(by_lane, part_index, 1, keepdims=False)
+    if parts == 2:
+        other = lax.dynamic_index_in_dim(by_lane, 1 - part_index, 1, keepdims=False)
+        ahead = share(other, table)[1]
+        behind = share(near, ahead)[1]
+        late_rows = [(late_half,), (ahead, behind)]
+        second = [near, ahead]
+    else:
+        ahead = share(late_half, table)
+        late_rows = [(half,) for half in ahead]
+        second = [
+            lax.dynamic_index_in_dim(
+                half.reshape(group, parts, held, piece, width), part_index, 1, keepdims=False
+            )
+            for half in ahead
+        ]
     second = jnp.concatenate(second, axis=1).reshape(group * shard_rows, piece, width)
     part_groups = [
         [a * lanes + g * parts + m for g in range(group)] for a in range(planes) for m in range(parts)
@@ -395,12 +404,11 @@
     second, _ = lax.optimization_barrier((second, first))
     if group > 1:
         second = swap(second, part_groups)
-    early_shared = share(early_half, late_shared)
+    early_shared = share(early_half, ahead)
     odd_query, _ = lax.optimization_barrier((odd_query, second))
     odd_query = lax.all_to_all(odd_query, "db", 0, 0, tiled=True)
     odd_query = odd_query.reshape(shards * capacity, columns)
-    cut = (width // DH + 1) // 2 * DH
-    plane_pieces = [first, second[:, :, :cut], second[:, :, cut:]]
+    plane_pieces = [first, second]
 
     def stepped(row):
         step = (part_index + parts - row % shard_rows // held) % parts
@@ -459,7 +467,7 @@
         slot_want = slot_row - (part_index + parts - k) % parts * held
         slot_want = jnp.broadcast_to(slot_want.reshape(-1, 1), (shards * capacity, DH))
         odd_part = odd_attention(
-            odd_query, slot_want, (early_shared[k], late_shared[k]), weights, odd_part
+            odd_query, slot_want, (early_shared[k], *late_rows[k]), weights, odd_part
         )
 
     returned = []

time: 416 us -> 432 us (1.038)
  waiting for transfers between devices: 231 us -> 259 us
  starting transfers between devices: 55.7 us -> 48.2 us
    all_to_all x5 -> x4, waiting for transfers between devices: 22.3 us -> 36.8 us  [swap(): return lax.all_to_all(x, BOTH, 0, 0, axis_index_groups=groups, tiled=True)]
    ppermute x2 -> x3, waiting for transfers between devices: 104 us -> 118 us  [share(): lax.ppermute(half, 'mp', [(m, (m + k) % parts) for m in range(parts)])]
    all_to_all x5 -> x4, starting transfers between devices: 24.1 us -> 20 us  [swap(): return lax.all_to_all(x, BOTH, 0, 0, axis_index_groups=groups, tiled=True)]
    ppermute x9 -> x6, starting transfers between devices: 9.78 us -> 7.1 us  [across(): moved.append(lax.ppermute(blocks[k], BOTH, pairs))]
    pallas_call x3 -> x2, Pallas kernels: 12.3 us -> 9.67 us  [gather_rows(): pl.pallas_call(functools.partial(gather_body, count=len(sources)), out_sh...]
    ppermute x9 -> x6, waiting for transfers between devices: 105 us -> 104 us  [across(): moved.append(lax.ppermute(blocks[k], BOTH, pairs))]
  transfers between devices with their start and end apart: 20 -> 17, of which waited for: 13 -> 9; matrix products, arithmetic and copies ran while one was open for 6% -> 6% of each run, Pallas kernels for 16% -> 14%
where the time goes in v8:
time: 432 us; the launch traced here: 431 us
  waiting for transfers between devices  259 us (60%)
  Pallas kernels  80.8 us (19%)
  starting transfers between devices  48.2 us (11%)
  local copies, waits for them, and re-layouts  19.5 us (5%)
  between operations  14.2 us (3%)
  other arithmetic  9.08 us (2%)
    ppermute x3, waiting for transfers between devices, share(): lax.ppermute(half, 'mp', [(m, (m + k) % parts) for m in range(parts)])  118 us
    ppermute x6, waiting for transfers between devices, across(): moved.append(lax.ppermute(blocks[k], BOTH, pairs))  104 us
    all_to_all x4, waiting for transfers between devices, swap(): return lax.all_to_all(x, BOTH, 0, 0, axis_index_groups=groups, tiled=True)  36.8 us
    pallas_call x2, Pallas kernels, odd_attention(): pl.pallas_call(odd_body, out_shape=jax.ShapeDtypeStruct(prior.shape, F32)...  31 us
    all_to_all x4, starting transfers between devices, swap(): return lax.all_to_all(x, BOTH, 0, 0, axis_index_groups=groups, tiled=True)  20 us
    pallas_call x1, Pallas kernels, even_attention(): pl.pallas_call(functools.partial(even_body, per_step=per_step), out_shape...  19.5 us
    pallas_call x1, Pallas kernels, project(): pl.pallas_call(project_body, out_shape=jax.ShapeDtypeStruct((count * toke...  13.2 us
    pallas_call x2, Pallas kernels, gather_rows(): pl.pallas_call(functools.partial(gather_body, count=len(sources)), out_sh...  9.67 us
  transfers between devices with their start and end apart: 17, of which 9 were waited for; matrix products, arithmetic and copies ran while one was open for 6% of the time, Pallas kernels for 14%

profile of v8, /device:TPU:11, one launch (start us, length us, event | category | flops | bytes accessed | tf_op | source)
XLA Modules:
  0.0 430.9 jit_solution(13611114219256040043)
XLA Ops:
  6.5 0.8 copy.69
  7.3 0.1 reshape.192
  7.4 0.8 copy.70
  8.2 0.1 reshape.193
  8.3 0.6 broadcast_in_dim.118
  9.0 6.5 %all-to-all-start.2 = ((s32[16,1,128]{2,1,0:T(1,128)}), s32[16,1,128]{2,1,0:T(1,128)S(1)}, u32[]{:S(2)}, u32[]{:S(2)}) async-start(s32[16,1,128]{2,1,0:T(1,128)} %broadcast_in_dim.118), calls=%async_computation.2 | async-start | bytes 16384 | tf_op jit(solution)/shard_map/all_to_all | solution.py:346
  15.5 1.7 pad_maximum_fusion.1
  17.2 2.6 copy.96
  19.8 3.5 slice_bitcast_fusion
  23.4 4.3 all-to-all-start.3
  27.7 2.9 dynamic-slice_bitcast_fusion.1
  30.6 1.2 collective-permute-start.6
  31.8 1.0 slice.42
  33.1 0.2 copy.74
  33.3 0.1 add.170
  33.5 36.0 %collective-permute-done.6.refs_1_ = bf16[4,16,8,896]{3,2,1,0:T(8,128)(2,1)S(1)} collective-permute-done((bf16[4,16,8,896]{3,2,1,0:T(8,128)(2,1)}, bf16[4,16,8,896]{3,2,1,0:T(8,128)(2,1)S(1)}, u32[]{:S(2)}, u32[]{:S(2)}) %collective-permute-start.6) | collective-permute-done | bytes 917536 | tf_op jit(solution)/shard_map/ppermute | solution.py:380
  69.4 2.9 pad_maximum_fusion
  72.4 5.1 %all-to-all-start.4 = ((bf16[128,8,896]{2,1,0:T(8,128)(2,1)}), bf16[128,8,896]{2,1,0:T(8,128)(2,1)}, u32[]{:S(2)}, u32[]{:S(2)}) async-start(bf16[128,8,896]{2,1,0:T(8,128)(2,1)} %bitcast.70), calls=%async_computation.4 | async-start | bytes 3670016 | tf_op jit(solution)/shard_map/all_to_all | solution.py:327
  77.5 0.2 fusion
  77.9 0.1 convolution_convert_fusion
  78.1 0.9 select_reduce_fusion.1
  79.1 0.7 reshape.201.index_ref
  79.8 0.5 convert_reduce_fusion
  80.4 1.6 gather_fusion
  81.9 2.2 select_rows.2
  84.2 1.2 collective-permute-start.9
  85.4 1.2 collective-permute-start.10
  86.5 1.2 collective-permute-start.11
  87.7 10.9 %all-to-all-done.4.source_ref.refs_0_ = bf16[128,8,896]{2,1,0:T(8,128)(2,1)} async-done(((bf16[128,8,896]{2,1,0:T(8,128)(2,1)}), bf16[128,8,896]{2,1,0:T(8,128)(2,1)}, u32[]{:S(2)}, u32[]{:S(2)}) %all-to-all-start.4) | async-done | bytes 1835040 | tf_op jit(solution)/shard_map/all_to_all | solution.py:327
  98.6 6.4 %all-to-all-start.5 = ((bf16[16,8,1024]{2,1,0:T(8,128)(2,1)}), bf16[16,8,1024]{2,1,0:T(8,128)(2,1)S(1)}, u32[]{:S(2)}, u32[]{:S(2)}) async-start(bf16[16,8,1024]{2,1,0:T(8,128)(2,1)} %bitcast.21), calls=%async_computation.5 | async-start | bytes 524288 | tf_op jit(solution)/shard_map/all_to_all | solution.py:409
  105.0 0.2 select_reduce_fusion
  105.2 0.6 compare_select_fusion.12
  105.8 0.6 compare_select_fusion.13.index_ref
  106.4 38.3 %collective-permute-done.10.refs_2_ = bf16[46,8,896]{2,1,0:T(8,128)(2,1)} collective-permute-done((bf16[46,8,896]{2,1,0:T(8,128)(2,1)}, bf16[46,8,896]{2,1,0:T(8,128)(2,1)}, u32[]{:S(2)}, u32[]{:S(2)}) %collective-permute-start.10) | collective-permute-done | bytes 659488 | tf_op jit(solution)/shard_map/ppermute | solution.py:341
  144.7 2.7 collective-permute-done.11.refs_3_
  147.4 4.6 %gather_rows.6 = bf16[4,2,32,8,896]{4,3,2,1,0:T(8,128)(2,1)} custom-call(s32[128]{0:T(128)} %compare_select_fusion.13.index_ref, bf16[128,8,896]{2,1,0:T(8,128)(2,1)S(1)} %all-to-all-done.3.source_ref.refs_0_, bf16[46,8,896]{2,1,0:T(8,128)(2,1)} %copy-done.7, bf16[46,8,896]{2,1,0:T(8,128)(2,1)} %collective-permute-done.10.refs_2_, ...), custom_call_target="tpu_custom_call" | custom-call | tf_op jit(solution)/shard_map/gather_rows/pallas_call | solution.py:185
  152.1 0.7 copy-done.2
  152.8 5.0 %all-to-all-start.6 = ((bf16[256,8,896]{2,1,0:T(8,128)(2,1)}), bf16[256,8,896]{2,1,0:T(8,128)(2,1)}, u32[]{:S(2)}, u32[]{:S(2)}) async-start(bf16[256,8,896]{2,1,0:T(8,128)(2,1)} %bitcast.65), calls=%async_computation.6 | async-start | bytes 7340032 | tf_op jit(solution)/shard_map/all_to_all | solution.py:327
  157.8 1.2 collective-permute-start.7
  159.0 0.3 collective-permute-start.8
  159.5 0.4 select_reduce_fusion.2
  160.1 0.7 broadcast_in_dim.125.want_ref
  160.8 0.9 broadcast_in_dim.126.refs_3_
  161.6 15.5 %odd_attention.2.refs_4_ = f32[128,1152]{1,0:T(8,128)} custom-call(bf16[128,1024]{1,0:T(8,128)(2,1)} %bitcast.77, s32[128,128]{1,0:T(8,128)} %broadcast_in_dim.125.want_ref, bf16[8,16,8,896]{3,2,1,0:T(8,128)(2,1)} %get-tuple-element.65.refs_0_, bf16[8,16,8,896]{3,2,1,0:T(8,128)(2,1)} %get-tuple-element.87.refs_1_, ...), custom_call_target="tpu_custom_call" | custom-call | tf_op jit(solution)/shard_map/odd_attention/pallas_call | solution.py:288
  177.1 81.6 %collective-permute-done.8.refs_2_ = bf16[4,16,8,896]{3,2,1,0:T(8,128)(2,1)} collective-permute-done((bf16[4,16,8,896]{3,2,1,0:T(8,128)(2,1)S(1)}, bf16[4,16,8,896]{3,2,1,0:T(8,128)(2,1)}, u32[]{:S(2)}, u32[]{:S(2)}) %collective-permute-start.8) | collective-permute-done | bytes 917536 | tf_op jit(solution)/shard_map/ppermute | solution.py:380
  258.7 0.7 broadcast_in_dim.124.want_ref
  259.4 15.5 %odd_attention.3 = f32[128,1152]{1,0:T(8,128)} custom-call(bf16[128,1024]{1,0:T(8,128)(2,1)} %bitcast.78, s32[128,128]{1,0:T(8,128)} %broadcast_in_dim.124.want_ref, bf16[8,16,8,896]{3,2,1,0:T(8,128)(2,1)} %collective-permute-done.7.refs_0_, bf16[4,16,8,896]{3,2,1,0:T(8,128)(2,1)} %copy-done, bf16[4,16,8,896]{3,2,1,0:T(8,128)(2,1)} %collective-permute-done.8.refs_2_, ...), custom_call_target="tpu_custom_call" | custom-call | tf_op jit(solution)/shard_map/odd_attention/pallas_call | solution.py:288
  275.0 5.6 %all-to-all-start.7 = ((f32[16,8,1152]{2,1,0:T(8,128)}), f32[16,8,1152]{2,1,0:T(8,128)S(1)}, u32[]{:S(2)}, u32[]{:S(2)}) async-start(f32[16,8,1152]{2,1,0:T(8,128)} %bitcast.76), calls=%async_computation.7 | async-start | bytes 1179648 | tf_op jit(solution)/shard_map/all_to_all | solution.py:477
  280.6 0.7 reshape.204.index_ref
  281.2 3.7 select_rows.3
  285.0 1.2 collective-permute-start.12
  286.1 1.2 collective-permute-start.13
  287.3 1.2 collective-permute-start.14
  288.5 47.4 %collective-permute-done.12.refs_1_ = bf16[46,8,896]{2,1,0:T(8,128)(2,1)S(1)} collective-permute-done((bf16[46,8,896]{2,1,0:T(8,128)(2,1)}, bf16[46,8,896]{2,1,0:T(8,128)(2,1)S(1)}, u32[]{:S(2)}, u32[]{:S(2)}) %collective-permute-start.12) | collective-permute-done | bytes 659488 | tf_op jit(solution)/shard_map/ppermute | solution.py:341
  335.9 14.1 %collective-permute-done.13.refs_2_ = bf16[46,8,896]{2,1,0:T(8,128)(2,1)} collective-permute-done((bf16[46,8,896]{2,1,0:T(8,128)(2,1)}, bf16[46,8,896]{2,1,0:T(8,128)(2,1)}, u32[]{:S(2)}, u32[]{:S(2)}) %collective-permute-start.13) | collective-permute-done | bytes 659488 | tf_op jit(solution)/shard_map/ppermute | solution.py:341
  350.0 1.9 collective-permute-done.14.refs_3_
  351.9 5.0 %gather_rows.7 = bf16[4,2,32,8,896]{4,3,2,1,0:T(8,128)(2,1)} custom-call(s32[128]{0:T(128)} %get-tuple-element.81.index_ref, bf16[128,8,896]{2,1,0:T(8,128)(2,1)} %all-to-all-done.4.source_ref.refs_0_, bf16[46,8,896]{2,1,0:T(8,128)(2,1)} %copy-done.8, bf16[46,8,896]{2,1,0:T(8,128)(2,1)} %collective-permute-done.13.refs_2_, ...), custom_call_target="tpu_custom_call" | custom-call | tf_op jit(solution)/shard_map/gather_rows/pallas_call | solution.py:185
  357.0 5.6 %all-to-all-start.8 = ((bf16[256,8,896]{2,1,0:T(8,128)(2,1)}), bf16[256,8,896]{2,1,0:T(8,128)(2,1)}, u32[]{:S(2)}, u32[]{:S(2)}) async-start(bf16[256,8,896]{2,1,0:T(8,128)(2,1)} %bitcast.67), calls=%async_computation.8 | async-start | bytes 7340032 | tf_op jit(solution)/shard_map/all_to_all | solution.py:327
  362.5 0.1 convert_reduce_fusion.1
  362.7 0.7 select_reduce_fusion.5
  364.0 13.2 %project.3.refs_2_ = bf16[2048,2048]{1,0:T(8,128)(2,1)} custom-call(bf16[8,32,8,896]{3,2,1,0:T(8,128)(2,1)} %bitcast.35.rows_ref, bf16[896,2048]{1,0:T(8,128)(2,1)} %all-gather.2.cloned.1.call-done.refs_2_.refs_3_.weight_ref.refs_1_), custom_call_target="tpu_custom_call" | custom-call | tf_op jit(solution)/shard_map/project/pallas_call | solution.py:48
  377.2 1.4 combine.3.refs_3_
  378.6 25.9 %all-to-all-done.8 = bf16[256,8,896]{2,1,0:T(8,128)(2,1)} async-done(((bf16[256,8,896]{2,1,0:T(8,128)(2,1)}), bf16[256,8,896]{2,1,0:T(8,128)(2,1)}, u32[]{:S(2)}, u32[]{:S(2)}) %all-to-all-start.8) | async-done | bytes 3670048 | tf_op jit(solution)/shard_map/all_to_all | solution.py:327
  404.5 19.5 %even_attention.3 = bf16[2048,1024]{1,0:T(8,128)(2,1)} custom-call(bf16[2048,1024]{1,0:T(8,128)(2,1)} %query_ref.1, bf16[8,32,8,896]{3,2,1,0:T(8,128)(2,1)} %bitcast.34.refs_0_, bf16[896,2048]{1,0:T(8,128)(2,1)} %all-gather.2.cloned.1.call-done.refs_2_.refs_3_.weight_ref.refs_1_, bf16[2048,2048]{1,0:T(8,128)(2,1)} %project.3.refs_2_, f32[16,1024]{1,0:T(8,128)} %combine.3.refs_3_), custom_call_target="tpu_custom_call" | custom-call | tf_op jit(solution)/shard_map/even_attention/pallas_call | solution.py:108
  (53 shorter events, 1.5 us)
Async XLA Ops:
  9.0 14.4 %all-to-all-start.2 = ((s32[16,1,128]{2,1,0:T(1,128)}), s32[16,1,128]{2,1,0:T(1,128)S(1)}, u32[]{:S(2)}, u32[]{:S(2)}) async-start(s32[16,1,128]{2,1,0:T(1,128)} %broadcast_in_dim.118), calls=%async_computation.2 | async-start | bytes 16384 | tf_op jit(solution)/shard_map/all_to_all | solution.py:346
  15.5 144.6 %all-gather.2.cloned.1.call-start = ((), (), s32[]{:S(2)}) async-start(), calls=%async_computation.9 | async-start | bytes 3899392 | tf_op jit(solution)/shard_map/all_gather | solution.py:350
  23.4 48.9 %all-to-all-start.3 = ((bf16[128,8,896]{2,1,0:T(8,128)(2,1)}), bf16[128,8,896]{2,1,0:T(8,128)(2,1)S(1)}, u32[]{:S(2)}, u32[]{:S(2)}) async-start(bf16[128,8,896]{2,1,0:T(8,128)(2,1)} %bitcast.71), calls=%async_computation.3 | async-start | bytes 3670016 | tf_op jit(solution)/shard_map/all_to_all | solution.py:327
  30.6 38.8 %collective-permute-start.6 = (bf16[4,16,8,896]{3,2,1,0:T(8,128)(2,1)}, bf16[4,16,8,896]{3,2,1,0:T(8,128)(2,1)S(1)}, u32[]{:S(2)}, u32[]{:S(2)}) collective-permute-start(bf16[4,16,8,896]{3,2,1,0:T(8,128)(2,1)} %get-tuple-element.62), channel_id=1, source_target_pairs={{0,1},{1,0},{2,3},{3,2},{4,5},{5,4},{6,7},{7,6},{8,9},{9,8},{10,11... | collective-permute-start | bytes 2752520 | tf_op jit(solution)/shard_map/ppermute | solution.py:380
  69.4 2.9 copy-start
  72.4 26.3 %all-to-all-start.4 = ((bf16[128,8,896]{2,1,0:T(8,128)(2,1)}), bf16[128,8,896]{2,1,0:T(8,128)(2,1)}, u32[]{:S(2)}, u32[]{:S(2)}) async-start(bf16[128,8,896]{2,1,0:T(8,128)(2,1)} %bitcast.70), calls=%async_computation.4 | async-start | bytes 3670016 | tf_op jit(solution)/shard_map/all_to_all | solution.py:327
  84.2 22.2 %collective-permute-start.9 = (bf16[46,8,896]{2,1,0:T(8,128)(2,1)}, bf16[46,8,896]{2,1,0:T(8,128)(2,1)S(1)}, u32[]{:S(2)}, u32[]{:S(2)}) collective-permute-start(bf16[46,8,896]{2,1,0:T(8,128)(2,1)} %get-tuple-element.67), channel_id=1, source_target_pairs={{0,8},{1,9},{2,10},{3,11},{4,12},{5,13},{6,14},{7,15},{8,16},{9,17... | collective-permute-start | bytes 1978376 | tf_op jit(solution)/shard_map/ppermute | solution.py:341
  85.4 59.3 %collective-permute-start.10 = (bf16[46,8,896]{2,1,0:T(8,128)(2,1)}, bf16[46,8,896]{2,1,0:T(8,128)(2,1)}, u32[]{:S(2)}, u32[]{:S(2)}) collective-permute-start(bf16[46,8,896]{2,1,0:T(8,128)(2,1)} %get-tuple-element.68), channel_id=1, source_target_pairs={{0,16},{1,17},{2,18},{3,19},{4,20},{5,21},{6,22},{7,23},{8,24},{9,... | collective-permute-start | bytes 1978376 | tf_op jit(solution)/shard_map/ppermute | solution.py:341
  86.5 60.9 %collective-permute-start.11 = (bf16[46,8,896]{2,1,0:T(8,128)(2,1)}, bf16[46,8,896]{2,1,0:T(8,128)(2,1)}, u32[]{:S(2)}, u32[]{:S(2)}) collective-permute-start(bf16[46,8,896]{2,1,0:T(8,128)(2,1)} %get-tuple-element.69), channel_id=1, source_target_pairs={{0,24},{1,25},{2,26},{3,27},{4,28},{5,29},{6,30},{7,31},{8,0},{9,1... | collective-permute-start | bytes 1978376 | tf_op jit(solution)/shard_map/ppermute | solution.py:341
  98.6 53.4 %all-to-all-start.5 = ((bf16[16,8,1024]{2,1,0:T(8,128)(2,1)}), bf16[16,8,1024]{2,1,0:T(8,128)(2,1)S(1)}, u32[]{:S(2)}, u32[]{:S(2)}) async-start(bf16[16,8,1024]{2,1,0:T(8,128)(2,1)} %bitcast.21), calls=%async_computation.5 | async-start | bytes 524288 | tf_op jit(solution)/shard_map/all_to_all | solution.py:409
  106.4 41.1 %copy-start.7 = (bf16[46,8,896]{2,1,0:T(8,128)(2,1)}, bf16[46,8,896]{2,1,0:T(8,128)(2,1)S(1)}, u32[]{:S(2)}) copy-start(bf16[46,8,896]{2,1,0:T(8,128)(2,1)S(1)} %collective-permute-done.9.refs_1_) | copy-start | bytes 1978372
  152.1 0.7 copy-start.2
  152.1 6.9 %copy-start.1 = (bf16[4,16,8,896]{3,2,1,0:T(8,128)(2,1)S(1)}, bf16[4,16,8,896]{3,2,1,0:T(8,128)(2,1)}, u32[]{:S(2)}) copy-start(bf16[4,16,8,896]{3,2,1,0:T(8,128)(2,1)} %get-tuple-element.66) | copy-start | bytes 2752516
  152.8 122.2 %all-to-all-start.6 = ((bf16[256,8,896]{2,1,0:T(8,128)(2,1)}), bf16[256,8,896]{2,1,0:T(8,128)(2,1)}, u32[]{:S(2)}, u32[]{:S(2)}) async-start(bf16[256,8,896]{2,1,0:T(8,128)(2,1)} %bitcast.65), calls=%async_computation.6 | async-start | bytes 7340032 | tf_op jit(solution)/shard_map/all_to_all | solution.py:327
  157.8 101.0 %collective-permute-start.7 = (bf16[8,16,8,896]{3,2,1,0:T(8,128)(2,1)}, bf16[8,16,8,896]{3,2,1,0:T(8,128)(2,1)}, u32[]{:S(2)}, u32[]{:S(2)}) collective-permute-start(bf16[8,16,8,896]{3,2,1,0:T(8,128)(2,1)} %get-tuple-element.65.refs_0_), channel_id=1, source_target_pairs={{0,1},{1,0},{2,3},{3,2},{4,5},{5,4},{6,7},{7,6},{8,9},{9,8},{10,11... | collective-permute-start | bytes 5505032 | tf_op jit(solution)/shard_map/ppermute | solution.py:380
  159.0 99.8 %collective-permute-start.8 = (bf16[4,16,8,896]{3,2,1,0:T(8,128)(2,1)S(1)}, bf16[4,16,8,896]{3,2,1,0:T(8,128)(2,1)}, u32[]{:S(2)}, u32[]{:S(2)}) collective-permute-start(bf16[4,16,8,896]{3,2,1,0:T(8,128)(2,1)S(1)} %copy-done.1), channel_id=1, source_target_pairs={{0,1},{1,0},{2,3},{3,2},{4,5},{5,4},{6,7},{7,6},{8,9},{9,8},{10,11... | collective-permute-start | bytes 2752520 | tf_op jit(solution)/shard_map/ppermute | solution.py:380
  275.0 82.0 %all-to-all-start.7 = ((f32[16,8,1152]{2,1,0:T(8,128)}), f32[16,8,1152]{2,1,0:T(8,128)S(1)}, u32[]{:S(2)}, u32[]{:S(2)}) async-start(f32[16,8,1152]{2,1,0:T(8,128)} %bitcast.76), calls=%async_computation.7 | async-start | bytes 1179648 | tf_op jit(solution)/shard_map/all_to_all | solution.py:477
  285.0 50.9 %collective-permute-start.12 = (bf16[46,8,896]{2,1,0:T(8,128)(2,1)}, bf16[46,8,896]{2,1,0:T(8,128)(2,1)S(1)}, u32[]{:S(2)}, u32[]{:S(2)}) collective-permute-start(bf16[46,8,896]{2,1,0:T(8,128)(2,1)} %get-tuple-element.76), channel_id=1, source_target_pairs={{0,8},{1,9},{2,10},{3,11},{4,12},{5,13},{6,14},{7,15},{8,16},{9,17... | collective-permute-start | bytes 1978376 | tf_op jit(solution)/shard_map/ppermute | solution.py:341
  286.1 63.9 %collective-permute-start.13 = (bf16[46,8,896]{2,1,0:T(8,128)(2,1)}, bf16[46,8,896]{2,1,0:T(8,128)(2,1)}, u32[]{:S(2)}, u32[]{:S(2)}) collective-permute-start(bf16[46,8,896]{2,1,0:T(8,128)(2,1)} %get-tuple-element.77), channel_id=1, source_target_pairs={{0,16},{1,17},{2,18},{3,19},{4,20},{5,21},{6,22},{7,23},{8,24},{9,... | collective-permute-start | bytes 1978376 | tf_op jit(solution)/shard_map/ppermute | solution.py:341
  287.3 64.6 %collective-permute-start.14 = (bf16[46,8,896]{2,1,0:T(8,128)(2,1)}, bf16[46,8,896]{2,1,0:T(8,128)(2,1)}, u32[]{:S(2)}, u32[]{:S(2)}) collective-permute-start(bf16[46,8,896]{2,1,0:T(8,128)(2,1)} %get-tuple-element.78), channel_id=1, source_target_pairs={{0,24},{1,25},{2,26},{3,27},{4,28},{5,29},{6,30},{7,31},{8,0},{9,1... | collective-permute-start | bytes 1978376 | tf_op jit(solution)/shard_map/ppermute | solution.py:341
  335.9 16.0 %copy-start.8 = (bf16[46,8,896]{2,1,0:T(8,128)(2,1)}, bf16[46,8,896]{2,1,0:T(8,128)(2,1)S(1)}, u32[]{:S(2)}) copy-start(bf16[46,8,896]{2,1,0:T(8,128)(2,1)S(1)} %collective-permute-done.12.refs_1_) | copy-start | bytes 1978372
  357.0 47.5 %all-to-all-start.8 = ((bf16[256,8,896]{2,1,0:T(8,128)(2,1)}), bf16[256,8,896]{2,1,0:T(8,128)(2,1)}, u32[]{:S(2)}, u32[]{:S(2)}) async-start(bf16[256,8,896]{2,1,0:T(8,128)(2,1)} %bitcast.67), calls=%async_computation.8 | async-start | bytes 7340032 | tf_op jit(solution)/shard_map/all_to_all | solution.py:327
Sparse Core Ops, SparseCore 0:
  18.6 52.6 all-gather.1

commit v9 on v8

--- a/solution.py
+++ b/solution.py
@@ -15,6 +15,7 @@
 LANES = 8
 CHUNKS = 2
 MOST_SHIFTS = 8
+MOST_DEALS = 16
 LOW = (SPAN - 1) // 16 * 16
 FAST_SLOTS = 46
 BF16 = jnp.bfloat16
@@ -341,6 +342,15 @@
             moved.append(lax.ppermute(blocks[k], BOTH, pairs))
         return moved
 
+    def deal(blocks, sign):
+        if shards > MOST_DEALS:
+            return lax.all_to_all(blocks, "db", 0, 0, tiled=True)
+        dealt = [blocks[:1]]
+        for k in range(1, shards):
+            pairs = [(d, (d + sign * k) % shards) for d in range(shards)]
+            dealt.append(lax.ppermute(blocks[k : k + 1], "db", pairs))
+        return jnp.concatenate(dealt, axis=0)
+
     table = jnp.concatenate([nbr_shard.reshape(-1), nbr_row.reshape(-1)])
     table = jnp.broadcast_to(table[None, None], (shards, 1, table.shape[0]))
     table = lax.all_to_all(table, "db", 0, 0, tiled=True)
@@ -364,7 +374,11 @@
         odd_rank[:, None, :] == jnp.arange(capacity, dtype=jnp.int32)[None, :, None]
     )
     slot_row = jnp.sum(jnp.where(arriving, odd_row[:, None, :] + 1, 0), axis=2) - 1
-    my_slot = lax.dynamic_index_in_dim(odd_shard * capacity + odd_rank, db_index, 0, keepdims=False)
+    place_of = odd_shard
+    if shards <= MOST_DEALS:
+        place_of = (odd_shard + shards - db_index) % shards
+        slot_row = jnp.take(slot_row, (db_index + shards - jnp.arange(shards)) % shards, axis=0, mode="clip")
+    my_slot = lax.dynamic_index_in_dim(place_of * capacity + odd_rank, db_index, 0, keepdims=False)
     slots = jnp.arange(shards * capacity, dtype=jnp.int32)
     chosen = my_slot[None, :] == slots[:, None]
     sender = jnp.sum(jnp.where(chosen, (earlier // neighbours).astype(jnp.int32)[None, :], 0), axis=1)
@@ -405,8 +419,8 @@
     if group > 1:
         second = swap(second, part_groups)
     early_shared = share(early_half, ahead)
-    odd_query, _ = lax.optimization_barrier((odd_query, second))
-    odd_query = lax.all_to_all(odd_query, "db", 0, 0, tiled=True)
+    odd_query, _ = lax.optimization_barrier((odd_query, second if shards > MOST_DEALS else first))
+    odd_query = deal(odd_query, 1)
     odd_query = odd_query.reshape(shards * capacity, columns)
     plane_pieces = [first, second]
 
@@ -457,7 +471,7 @@
                 sending, _ = lax.optimization_barrier((sending, received[-1]))
             received.append(across(sending))
             outgoing = gather_rows(index[min(chunk, 1)], received[-1], group, parts)
-            outgoing, _ = lax.optimization_barrier((outgoing, after if arrived else odd_query))
+            outgoing, _ = lax.optimization_barrier((outgoing, after if arrived else first))
             arrived.append(swap(outgoing, plane_groups))
             after = arrived[-1] if chunk else between(arrived[-1])
         return [a.reshape(lanes, wanted, piece, a.shape[2]) for a in arrived]
@@ -473,10 +487,12 @@
     returned = []
 
     def send_back(after):
-        part, _ = lax.optimization_barrier((odd_part, after))
-        part = lax.all_to_all(part.reshape(shards, capacity, columns + DH), "db", 0, 0, tiled=True)
+        part = odd_part.reshape(shards, capacity, columns + DH)
+        if shards > MOST_DEALS:
+            part, _ = lax.optimization_barrier((part, after))
+        part = deal(part, -1)
         returned.append(part)
-        return part
+        return part if shards > MOST_DEALS else after
 
     def attend(select, index, between, odd_rows):
         early, *late = exchange(plane_pieces, select, index, between)

time: 432 us -> 445 us (1.030)
  starting transfers between devices: 48.2 us -> 114 us
  waiting for transfers between devices: 259 us -> 201 us
    ppermute x3, waiting for transfers between devices: 118 us -> 35.5 us  [share(): lax.ppermute(half, 'mp', [(m, (m + k) % parts) for m in range(parts)])]
    ppermute x0 -> x30, starting transfers between devices: none -> 76.6 us  [deal(): dealt.append(lax.ppermute(blocks[k:k + 1], 'db', pairs))]
    ppermute x0 -> x30, waiting for transfers between devices: none -> 52.8 us  [deal(): dealt.append(lax.ppermute(blocks[k:k + 1], 'db', pairs))]
    all_to_all x4, waiting for transfers between devices: 36.8 us -> 0.01 us  [swap(): return lax.all_to_all(x, BOTH, 0, 0, axis_index_groups=groups, tiled=True)]
    all_to_all x2 -> x0, starting transfers between devices: 11.9 us -> none  [the longest x1 6.4 us: local(): odd_query = lax.all_to_all(odd_query, 'db', 0, 0, tiled=True)]
    ppermute x6, waiting for transfers between devices: 104 us -> 113 us  [across(): moved.append(lax.ppermute(blocks[k], BOTH, pairs))]
  transfers between devices with their start and end apart: 17 -> 45, of which waited for: 9 -> 25; matrix products, arithmetic and copies ran while one was open for 6% -> 6% of each run, Pallas kernels for 14% -> 14%
where the time goes in v9:
time: 445 us; the launch traced here: 440 us
  waiting for transfers between devices  201 us (45%)
  starting transfers between devices  114 us (26%)
  Pallas kernels  80.9 us (18%)
  local copies, waits for them, and re-layouts  20.5 us (5%)
  between operations  14.5 us (3%)
  other arithmetic  9.06 us (2%)
    ppermute x6, waiting for transfers between devices, across(): moved.append(lax.ppermute(blocks[k], BOTH, pairs))  113 us
    ppermute x30, starting transfers between devices, deal(): dealt.append(lax.ppermute(blocks[k:k + 1], 'db', pairs))  76.6 us
    ppermute x30, waiting for transfers between devices, deal(): dealt.append(lax.ppermute(blocks[k:k + 1], 'db', pairs))  52.8 us
    ppermute x3, waiting for transfers between devices, share(): lax.ppermute(half, 'mp', [(m, (m + k) % parts) for m in range(parts)])  35.5 us
    pallas_call x2, Pallas kernels, odd_attention(): pl.pallas_call(odd_body, out_shape=jax.ShapeDtypeStruct(prior.shape, F32)...  31.1 us
    all_to_all x4, starting transfers between devices, swap(): return lax.all_to_all(x, BOTH, 0, 0, axis_index_groups=groups, tiled=True)  20.7 us
    pallas_call x1, Pallas kernels, even_attention(): pl.pallas_call(functools.partial(even_body, per_step=per_step), out_shape...  19.6 us
    pallas_call x1, Pallas kernels, project(): pl.pallas_call(project_body, out_shape=jax.ShapeDtypeStruct((count * toke...  13.1 us
  transfers between devices with their start and end apart: 45, of which 25 were waited for; matrix products, arithmetic and copies ran while one was open for 6% of the time, Pallas kernels for 14%

profile of v9, /device:TPU:11, one launch (start us, length us, event | category | flops | bytes accessed | tf_op | source)
XLA Modules:
  0.0 440.1 jit_solution(4584765922862284433)
XLA Ops:
  9.0 6.5 %all-to-all-start.2 = ((s32[16,1,128]{2,1,0:T(1,128)}), s32[16,1,128]{2,1,0:T(1,128)S(1)}, u32[]{:S(2)}, u32[]{:S(2)}) async-start(s32[16,1,128]{2,1,0:T(1,128)} %broadcast_in_dim.120), calls=%async_computation.2 | async-start | bytes 16384 | tf_op jit(solution)/shard_map/all_to_all | solution.py:356
  15.5 1.7 pad_maximum_fusion.1
  17.2 2.6 copy.96
  19.8 3.6 slice_bitcast_fusion.16
  23.6 4.3 all-to-all-start.3
  28.9 2.9 dynamic-slice_bitcast_fusion.1
  31.9 1.2 collective-permute-start.6
  34.0 35.5 %collective-permute-done.6.refs_1_ = bf16[4,16,8,896]{3,2,1,0:T(8,128)(2,1)S(1)} collective-permute-done((bf16[4,16,8,896]{3,2,1,0:T(8,128)(2,1)}, bf16[4,16,8,896]{3,2,1,0:T(8,128)(2,1)S(1)}, u32[]{:S(2)}, u32[]{:S(2)}) %collective-permute-start.6) | collective-permute-done | bytes 917536 | tf_op jit(solution)/shard_map/ppermute | solution.py:394
  69.6 2.9 pad_maximum_fusion
  72.5 5.2 %all-to-all-start.4 = ((bf16[128,8,896]{2,1,0:T(8,128)(2,1)}), bf16[128,8,896]{2,1,0:T(8,128)(2,1)}, u32[]{:S(2)}, u32[]{:S(2)}) async-start(bf16[128,8,896]{2,1,0:T(8,128)(2,1)} %bitcast.105), calls=%async_computation.4 | async-start | bytes 3670016 | tf_op jit(solution)/shard_map/all_to_all | solution.py:328
  80.4 2.3 select_rows.3
  82.8 1.2 collective-permute-start.39
  84.0 1.2 collective-permute-start.40
  85.2 1.1 collective-permute-start.41
  87.1 11.9 %collective-permute-done.39.refs_1_ = bf16[46,8,896]{2,1,0:T(8,128)(2,1)S(1)} collective-permute-done((bf16[46,8,896]{2,1,0:T(8,128)(2,1)}, bf16[46,8,896]{2,1,0:T(8,128)(2,1)S(1)}, u32[]{:S(2)}, u32[]{:S(2)}) %collective-permute-start.39) | collective-permute-done | bytes 659488 | tf_op jit(solution)/shard_map/ppermute | solution.py:342
  99.0 41.5 %collective-permute-done.40.refs_2_ = bf16[46,8,896]{2,1,0:T(8,128)(2,1)S(1)} collective-permute-done((bf16[46,8,896]{2,1,0:T(8,128)(2,1)}, bf16[46,8,896]{2,1,0:T(8,128)(2,1)S(1)}, u32[]{:S(2)}, u32[]{:S(2)}) %collective-permute-start.40) | collective-permute-done | bytes 659488 | tf_op jit(solution)/shard_map/ppermute | solution.py:342
  140.5 2.7 collective-permute-done.41.refs_3_
  143.2 4.7 %gather_rows.7 = bf16[4,2,32,8,896]{4,3,2,1,0:T(8,128)(2,1)} custom-call(s32[128]{0:T(128)} %get-tuple-element.79.index_ref, bf16[128,8,896]{2,1,0:T(8,128)(2,1)S(1)} %all-to-all-done.3.source_ref.refs_0_, bf16[46,8,896]{2,1,0:T(8,128)(2,1)} %copy-done.7, bf16[46,8,896]{2,1,0:T(8,128)(2,1)} %copy-done.8, bf16[46,8,896]{2,1,0:T(8,128)(2,1)} %collective-permute-done.41.refs_3_), custom_call_target="tpu_custom_call" | custom-call | tf_op jit(solution)/shard_map/gather_rows/pallas_call | solution.py:186
  147.9 5.0 %all-to-all-start.5 = ((bf16[256,8,896]{2,1,0:T(8,128)(2,1)}), bf16[256,8,896]{2,1,0:T(8,128)(2,1)}, u32[]{:S(2)}, u32[]{:S(2)}) async-start(bf16[256,8,896]{2,1,0:T(8,128)(2,1)} %bitcast.100), calls=%async_computation.5 | async-start | bytes 7340032 | tf_op jit(solution)/shard_map/all_to_all | solution.py:328
  155.2 1.3 collective-permute-start.22
  159.8 1.1 collective-permute-start.20
  160.9 31.8 %collective-permute-start.8 = (bf16[1,8,1024]{2,1,0:T(8,128)(2,1)S(1)}, bf16[1,8,1024]{2,1,0:T(8,128)(2,1)S(1)}, u32[]{:S(2)}, u32[]{:S(2)}) collective-permute-start(bf16[1,8,1024]{2,1,0:T(8,128)(2,1)S(1)} %get-tuple-element.122), channel_id=1, source_target_pairs={{0,4},{2,6},{4,8},{6,10},{8,12},{10,14},{12,16},{14,18},{16,20},{1... | collective-permute-start | bytes 49160 | tf_op jit(solution)/shard_map/ppermute | solution.py:351
  192.7 2.5 collective-permute-done.8
  195.2 2.5 collective-permute-start.9
  197.7 2.0 collective-permute-done.9
  199.7 1.8 collective-permute-start.10
  201.5 2.8 collective-permute-done.10
  204.3 5.1 %collective-permute-start.11 = (bf16[1,8,1024]{2,1,0:T(8,128)(2,1)S(1)}, bf16[1,8,1024]{2,1,0:T(8,128)(2,1)S(1)}, u32[]{:S(2)}, u32[]{:S(2)}) collective-permute-start(bf16[1,8,1024]{2,1,0:T(8,128)(2,1)S(1)} %get-tuple-element.119), channel_id=1, source_target_pairs={{0,10},{2,12},{4,14},{6,16},{8,18},{10,20},{12,22},{14,24},{16,26}... | collective-permute-start | bytes 49160 | tf_op jit(solution)/shard_map/ppermute | solution.py:351
  210.5 3.8 collective-permute-done.12
  214.3 2.4 collective-permute-start.13
  216.7 6.4 %collective-permute-done.13 = bf16[1,8,1024]{2,1,0:T(8,128)(2,1)S(1)} collective-permute-done((bf16[1,8,1024]{2,1,0:T(8,128)(2,1)S(1)}, bf16[1,8,1024]{2,1,0:T(8,128)(2,1)S(1)}, u32[]{:S(2)}, u32[]{:S(2)}) %collective-permute-start.13) | collective-permute-done | bytes 16416 | tf_op jit(solution)/shard_map/ppermute | solution.py:351
  223.1 1.5 collective-permute-start.19
  224.6 2.0 collective-permute-done.14
  226.6 3.8 collective-permute-start.15
  231.6 3.7 select_rows.2
  235.7 2.8 collective-permute-start.43
  239.4 9.4 %collective-permute-done.42.refs_1_ = bf16[46,8,896]{2,1,0:T(8,128)(2,1)} collective-permute-done((bf16[46,8,896]{2,1,0:T(8,128)(2,1)}, bf16[46,8,896]{2,1,0:T(8,128)(2,1)}, u32[]{:S(2)}, u32[]{:S(2)}) %collective-permute-start.42) | collective-permute-done | bytes 659488 | tf_op jit(solution)/shard_map/ppermute | solution.py:342
  248.9 41.6 %collective-permute-done.43.refs_2_ = bf16[46,8,896]{2,1,0:T(8,128)(2,1)} collective-permute-done((bf16[46,8,896]{2,1,0:T(8,128)(2,1)}, bf16[46,8,896]{2,1,0:T(8,128)(2,1)}, u32[]{:S(2)}, u32[]{:S(2)}) %collective-permute-start.43) | collective-permute-done | bytes 659488 | tf_op jit(solution)/shard_map/ppermute | solution.py:342
  290.4 5.4 %collective-permute-done.44.refs_3_ = bf16[46,8,896]{2,1,0:T(8,128)(2,1)} collective-permute-done((bf16[46,8,896]{2,1,0:T(8,128)(2,1)}, bf16[46,8,896]{2,1,0:T(8,128)(2,1)}, u32[]{:S(2)}, u32[]{:S(2)}) %collective-permute-start.44) | collective-permute-done | bytes 659488 | tf_op jit(solution)/shard_map/ppermute | solution.py:342
  295.8 5.0 %gather_rows.6 = bf16[4,2,32,8,896]{4,3,2,1,0:T(8,128)(2,1)} custom-call(s32[128]{0:T(128)} %get-tuple-element.82.index_ref, bf16[128,8,896]{2,1,0:T(8,128)(2,1)} %all-to-all-done.4.source_ref.refs_0_, bf16[46,8,896]{2,1,0:T(8,128)(2,1)} %collective-permute-done.42.refs_1_, bf16[46,8,896]{2,1,0:T(8,128)(2,1)} %collective-permute-done.43.refs_2_, ...), custom_call_target="tpu_custom_call" | custom-call | tf_op jit(solution)/shard_map/gather_rows/pallas_call | solution.py:186
  300.9 6.2 %all-to-all-start.6 = ((bf16[256,8,896]{2,1,0:T(8,128)(2,1)}), bf16[256,8,896]{2,1,0:T(8,128)(2,1)}, u32[]{:S(2)}, u32[]{:S(2)}) async-start(bf16[256,8,896]{2,1,0:T(8,128)(2,1)} %bitcast.101), calls=%async_computation.6 | async-start | bytes 7340032 | tf_op jit(solution)/shard_map/all_to_all | solution.py:328
  308.7 15.5 %odd_attention.2.refs_4_ = f32[128,1152]{1,0:T(8,128)} custom-call(bf16[128,1024]{1,0:T(8,128)(2,1)} %bitcast.111, s32[128,128]{1,0:T(8,128)} %broadcast_in_dim.127.want_ref, bf16[8,16,8,896]{3,2,1,0:T(8,128)(2,1)} %get-tuple-element.64.refs_0_, bf16[8,16,8,896]{3,2,1,0:T(8,128)(2,1)} %get-tuple-element.88.refs_1_, ...), custom_call_target="tpu_custom_call" | custom-call | tf_op jit(solution)/shard_map/odd_attention/pallas_call | solution.py:289
  325.0 15.5 %odd_attention.3 = f32[128,1152]{1,0:T(8,128)} custom-call(bf16[128,1024]{1,0:T(8,128)(2,1)} %bitcast.112, s32[128,128]{1,0:T(8,128)} %broadcast_in_dim.126.want_ref, bf16[8,16,8,896]{3,2,1,0:T(8,128)(2,1)} %collective-permute-done.22.refs_0_, bf16[4,16,8,896]{3,2,1,0:T(8,128)(2,1)} %copy-done, bf16[4,16,8,896]{3,2,1,0:T(8,128)(2,1)} %collective-permute-done.23.refs_2_, ...), custom_call_target="tpu_custom_call" | custom-call | tf_op jit(solution)/shard_map/odd_attention/pallas_call | solution.py:289
  340.5 1.1 slice_bitcast_fusion
  342.8 2.3 collective-permute-start.38
  345.1 3.4 collective-permute-start.35
  348.5 13.1 %project.3.refs_2_ = bf16[2048,2048]{1,0:T(8,128)(2,1)} custom-call(bf16[8,32,8,896]{3,2,1,0:T(8,128)(2,1)} %bitcast.51.rows_ref, bf16[896,2048]{1,0:T(8,128)(2,1)} %all-gather.2.cloned.1.call-done.refs_2_.refs_3_.weight_ref.refs_1_), custom_call_target="tpu_custom_call" | custom-call | tf_op jit(solution)/shard_map/project/pallas_call | solution.py:49
  361.6 3.7 collective-permute-done.25
  365.3 1.4 collective-permute-start.26
  366.8 2.6 collective-permute-done.26
  369.3 1.7 collective-permute-start.27
  371.0 2.4 collective-permute-done.27
  373.4 6.1 %collective-permute-start.28 = (f32[1,8,1152]{2,1,0:T(8,128)S(1)}, f32[1,8,1152]{2,1,0:T(8,128)S(1)}, u32[]{:S(2)}, u32[]{:S(2)}) collective-permute-start(f32[1,8,1152]{2,1,0:T(8,128)S(1)} %get-tuple-element.104), channel_id=1, source_target_pairs={{0,22},{2,24},{4,26},{6,28},{8,30},{10,0},{12,2},{14,4},{16,6},{18... | collective-permute-start | bytes 110600 | tf_op jit(solution)/shard_map/ppermute | solution.py:351
  379.5 1.1 collective-permute-done.28
  380.6 4.9 %collective-permute-done.29 = f32[1,8,1152]{2,1,0:T(8,128)S(1)} collective-permute-done((f32[1,8,1152]{2,1,0:T(8,128)S(1)}, f32[1,8,1152]{2,1,0:T(8,128)S(1)}, u32[]{:S(2)}, u32[]{:S(2)}) %collective-permute-start.29) | collective-permute-done | bytes 36896 | tf_op jit(solution)/shard_map/ppermute | solution.py:351
  386.3 8.5 %collective-permute-done.30 = f32[1,8,1152]{2,1,0:T(8,128)S(1)} collective-permute-done((f32[1,8,1152]{2,1,0:T(8,128)S(1)}, f32[1,8,1152]{2,1,0:T(8,128)S(1)}, u32[]{:S(2)}, u32[]{:S(2)}) %collective-permute-start.30) | collective-permute-done | bytes 36896 | tf_op jit(solution)/shard_map/ppermute | solution.py:351
  394.9 3.7 collective-permute-done.31
  398.6 5.4 %collective-permute-start.32 = (f32[1,8,1152]{2,1,0:T(8,128)S(1)}, f32[1,8,1152]{2,1,0:T(8,128)S(1)}, u32[]{:S(2)}, u32[]{:S(2)}) collective-permute-start(f32[1,8,1152]{2,1,0:T(8,128)S(1)} %get-tuple-element.100), channel_id=1, source_target_pairs={{0,14},{2,16},{4,18},{6,20},{8,22},{10,24},{12,26},{14,28},{16,30}... | collective-permute-start | bytes 110600 | tf_op jit(solution)/shard_map/ppermute | solution.py:351
  403.9 1.1 collective-permute-done.32
  405.8 2.9 collective-permute-done.33
  408.7 2.4 collective-permute-start.34
  411.1 1.1 collective-permute-done.34
  412.3 1.4 combine.3.refs_3_
  413.7 19.6 %even_attention.3 = bf16[2048,1024]{1,0:T(8,128)(2,1)} custom-call(bf16[2048,1024]{1,0:T(8,128)(2,1)} %query_ref.1, bf16[8,32,8,896]{3,2,1,0:T(8,128)(2,1)} %bitcast.50.refs_0_, bf16[896,2048]{1,0:T(8,128)(2,1)} %all-gather.2.cloned.1.call-done.refs_2_.refs_3_.weight_ref.refs_1_, bf16[2048,2048]{1,0:T(8,128)(2,1)} %project.3.refs_2_, f32[16,1024]{1,0:T(8,128)} %combine.3.refs_3_), custom_call_target="tpu_custom_call" | custom-call | tf_op jit(solution)/shard_map/even_attention/pallas_call | solution.py:109
  (148 shorter events, 21.9 us)
Async XLA Ops:
  9.0 14.5 %all-to-all-start.2 = ((s32[16,1,128]{2,1,0:T(1,128)}), s32[16,1,128]{2,1,0:T(1,128)S(1)}, u32[]{:S(2)}, u32[]{:S(2)}) async-start(s32[16,1,128]{2,1,0:T(1,128)} %broadcast_in_dim.120), calls=%async_computation.2 | async-start | bytes 16384 | tf_op jit(solution)/shard_map/all_to_all | solution.py:356
  15.5 291.7 %all-gather.2.cloned.1.call-start = ((), (), s32[]{:S(2)}) async-start(), calls=%async_computation.7 | async-start | bytes 3899392 | tf_op jit(solution)/shard_map/all_gather | solution.py:360
  23.6 48.9 %all-to-all-start.3 = ((bf16[128,8,896]{2,1,0:T(8,128)(2,1)}), bf16[128,8,896]{2,1,0:T(8,128)(2,1)S(1)}, u32[]{:S(2)}, u32[]{:S(2)}) async-start(bf16[128,8,896]{2,1,0:T(8,128)(2,1)} %bitcast.106), calls=%async_computation.3 | async-start | bytes 3670016 | tf_op jit(solution)/shard_map/all_to_all | solution.py:328
  31.9 37.6 %collective-permute-start.6 = (bf16[4,16,8,896]{3,2,1,0:T(8,128)(2,1)}, bf16[4,16,8,896]{3,2,1,0:T(8,128)(2,1)S(1)}, u32[]{:S(2)}, u32[]{:S(2)}) collective-permute-start(bf16[4,16,8,896]{3,2,1,0:T(8,128)(2,1)} %get-tuple-element.61), channel_id=1, source_target_pairs={{0,1},{1,0},{2,3},{3,2},{4,5},{5,4},{6,7},{7,6},{8,9},{9,8},{10,11... | collective-permute-start | bytes 2752520 | tf_op jit(solution)/shard_map/ppermute | solution.py:394
  69.6 2.9 copy-start
  72.5 75.4 %all-to-all-start.4 = ((bf16[128,8,896]{2,1,0:T(8,128)(2,1)}), bf16[128,8,896]{2,1,0:T(8,128)(2,1)}, u32[]{:S(2)}, u32[]{:S(2)}) async-start(bf16[128,8,896]{2,1,0:T(8,128)(2,1)} %bitcast.105), calls=%async_computation.4 | async-start | bytes 3670016 | tf_op jit(solution)/shard_map/all_to_all | solution.py:328
  82.8 16.2 %collective-permute-start.39 = (bf16[46,8,896]{2,1,0:T(8,128)(2,1)}, bf16[46,8,896]{2,1,0:T(8,128)(2,1)S(1)}, u32[]{:S(2)}, u32[]{:S(2)}) collective-permute-start(bf16[46,8,896]{2,1,0:T(8,128)(2,1)} %get-tuple-element.69), channel_id=1, source_target_pairs={{0,8},{1,9},{2,10},{3,11},{4,12},{5,13},{6,14},{7,15},{8,16},{9,17... | collective-permute-start | bytes 1978376 | tf_op jit(solution)/shard_map/ppermute | solution.py:342
  84.0 56.5 %collective-permute-start.40 = (bf16[46,8,896]{2,1,0:T(8,128)(2,1)}, bf16[46,8,896]{2,1,0:T(8,128)(2,1)S(1)}, u32[]{:S(2)}, u32[]{:S(2)}) collective-permute-start(bf16[46,8,896]{2,1,0:T(8,128)(2,1)} %get-tuple-element.70), channel_id=1, source_target_pairs={{0,16},{1,17},{2,18},{3,19},{4,20},{5,21},{6,22},{7,23},{8,24},{9,... | collective-permute-start | bytes 1978376 | tf_op jit(solution)/shard_map/ppermute | solution.py:342
  85.2 58.0 %collective-permute-start.41 = (bf16[46,8,896]{2,1,0:T(8,128)(2,1)}, bf16[46,8,896]{2,1,0:T(8,128)(2,1)}, u32[]{:S(2)}, u32[]{:S(2)}) collective-permute-start(bf16[46,8,896]{2,1,0:T(8,128)(2,1)} %get-tuple-element.71), channel_id=1, source_target_pairs={{0,24},{1,25},{2,26},{3,27},{4,28},{5,29},{6,30},{7,31},{8,0},{9,1... | collective-permute-start | bytes 1978376 | tf_op jit(solution)/shard_map/ppermute | solution.py:342
  99.0 44.2 %copy-start.7 = (bf16[46,8,896]{2,1,0:T(8,128)(2,1)}, bf16[46,8,896]{2,1,0:T(8,128)(2,1)S(1)}, u32[]{:S(2)}) copy-start(bf16[46,8,896]{2,1,0:T(8,128)(2,1)S(1)} %collective-permute-done.39.refs_1_) | copy-start | bytes 1978372
  140.5 2.7 copy-start.8
  147.9 153.0 %all-to-all-start.5 = ((bf16[256,8,896]{2,1,0:T(8,128)(2,1)}), bf16[256,8,896]{2,1,0:T(8,128)(2,1)}, u32[]{:S(2)}, u32[]{:S(2)}) async-start(bf16[256,8,896]{2,1,0:T(8,128)(2,1)} %bitcast.100), calls=%async_computation.5 | async-start | bytes 7340032 | tf_op jit(solution)/shard_map/all_to_all | solution.py:328
  152.8 5.8 %copy-start.1 = (bf16[4,16,8,896]{3,2,1,0:T(8,128)(2,1)S(1)}, bf16[4,16,8,896]{3,2,1,0:T(8,128)(2,1)}, u32[]{:S(2)}) copy-start(bf16[4,16,8,896]{3,2,1,0:T(8,128)(2,1)} %get-tuple-element.65) | copy-start | bytes 2752516
  155.2 169.1 %collective-permute-start.22 = (bf16[8,16,8,896]{3,2,1,0:T(8,128)(2,1)}, bf16[8,16,8,896]{3,2,1,0:T(8,128)(2,1)}, u32[]{:S(2)}, u32[]{:S(2)}) collective-permute-start(bf16[8,16,8,896]{3,2,1,0:T(8,128)(2,1)} %get-tuple-element.64.refs_0_), channel_id=1, source_target_pairs={{0,1},{1,0},{2,3},{3,2},{4,5},{5,4},{6,7},{7,6},{8,9},{9,8},{10,11... | collective-permute-start | bytes 5505032 | tf_op jit(solution)/shard_map/ppermute | solution.py:394
  156.4 4.4 %collective-permute-start.7 = (bf16[1,8,1024]{2,1,0:T(8,128)(2,1)S(1)}, bf16[1,8,1024]{2,1,0:T(8,128)(2,1)S(1)}, u32[]{:S(2)}, u32[]{:S(2)}) collective-permute-start(bf16[1,8,1024]{2,1,0:T(8,128)(2,1)S(1)} %get-tuple-element.123), channel_id=1, source_target_pairs={{0,2},{2,4},{4,6},{6,8},{8,10},{10,12},{12,14},{14,16},{16,18},{18... | collective-permute-start | bytes 49160 | tf_op jit(solution)/shard_map/ppermute | solution.py:351
  158.6 165.7 %collective-permute-start.23 = (bf16[4,16,8,896]{3,2,1,0:T(8,128)(2,1)S(1)}, bf16[4,16,8,896]{3,2,1,0:T(8,128)(2,1)}, u32[]{:S(2)}, u32[]{:S(2)}) collective-permute-start(bf16[4,16,8,896]{3,2,1,0:T(8,128)(2,1)S(1)} %copy-done.1), channel_id=1, source_target_pairs={{0,1},{1,0},{2,3},{3,2},{4,5},{5,4},{6,7},{7,6},{8,9},{9,8},{10,11... | collective-permute-start | bytes 2752520 | tf_op jit(solution)/shard_map/ppermute | solution.py:394
  158.9 64.2 %collective-permute-start.21 = (bf16[1,8,1024]{2,1,0:T(8,128)(2,1)S(1)}, bf16[1,8,1024]{2,1,0:T(8,128)(2,1)S(1)}, u32[]{:S(2)}, u32[]{:S(2)}) collective-permute-start(bf16[1,8,1024]{2,1,0:T(8,128)(2,1)S(1)} %get-tuple-element.109), channel_id=1, source_target_pairs={{0,30},{2,0},{4,2},{6,4},{8,6},{10,8},{12,10},{14,12},{16,14},{18,... | collective-permute-start | bytes 49160 | tf_op jit(solution)/shard_map/ppermute | solution.py:351
  159.8 70.6 %collective-permute-start.20 = (bf16[1,8,1024]{2,1,0:T(8,128)(2,1)S(1)}, bf16[1,8,1024]{2,1,0:T(8,128)(2,1)S(1)}, u32[]{:S(2)}, u32[]{:S(2)}) collective-permute-start(bf16[1,8,1024]{2,1,0:T(8,128)(2,1)S(1)} %get-tuple-element.110), channel_id=1, source_target_pairs={{0,28},{2,30},{4,0},{6,2},{8,4},{10,6},{12,8},{14,10},{16,12},{18,... | collective-permute-start | bytes 49160 | tf_op jit(solution)/shard_map/ppermute | solution.py:351
  160.9 34.3 %collective-permute-start.8 = (bf16[1,8,1024]{2,1,0:T(8,128)(2,1)S(1)}, bf16[1,8,1024]{2,1,0:T(8,128)(2,1)S(1)}, u32[]{:S(2)}, u32[]{:S(2)}) collective-permute-start(bf16[1,8,1024]{2,1,0:T(8,128)(2,1)S(1)} %get-tuple-element.122), channel_id=1, source_target_pairs={{0,4},{2,6},{4,8},{6,10},{8,12},{10,14},{12,16},{14,18},{16,20},{1... | collective-permute-start | bytes 49160 | tf_op jit(solution)/shard_map/ppermute | solution.py:351
  195.2 4.5 %collective-permute-start.9 = (bf16[1,8,1024]{2,1,0:T(8,128)(2,1)S(1)}, bf16[1,8,1024]{2,1,0:T(8,128)(2,1)S(1)}, u32[]{:S(2)}, u32[]{:S(2)}) collective-permute-start(bf16[1,8,1024]{2,1,0:T(8,128)(2,1)S(1)} %get-tuple-element.121), channel_id=1, source_target_pairs={{0,6},{2,8},{4,10},{6,12},{8,14},{10,16},{12,18},{14,20},{16,22},{... | collective-permute-start | bytes 49160 | tf_op jit(solution)/shard_map/ppermute | solution.py:351
  199.7 4.6 %collective-permute-start.10 = (bf16[1,8,1024]{2,1,0:T(8,128)(2,1)S(1)}, bf16[1,8,1024]{2,1,0:T(8,128)(2,1)S(1)}, u32[]{:S(2)}, u32[]{:S(2)}) collective-permute-start(bf16[1,8,1024]{2,1,0:T(8,128)(2,1)S(1)} %get-tuple-element.120), channel_id=1, source_target_pairs={{0,8},{2,10},{4,12},{6,14},{8,16},{10,18},{12,20},{14,22},{16,24},... | collective-permute-start | bytes 49160 | tf_op jit(solution)/shard_map/ppermute | solution.py:351
  204.3 6.0 %collective-permute-start.11 = (bf16[1,8,1024]{2,1,0:T(8,128)(2,1)S(1)}, bf16[1,8,1024]{2,1,0:T(8,128)(2,1)S(1)}, u32[]{:S(2)}, u32[]{:S(2)}) collective-permute-start(bf16[1,8,1024]{2,1,0:T(8,128)(2,1)S(1)} %get-tuple-element.119), channel_id=1, source_target_pairs={{0,10},{2,12},{4,14},{6,16},{8,18},{10,20},{12,22},{14,24},{16,26}... | collective-permute-start | bytes 49160 | tf_op jit(solution)/shard_map/ppermute | solution.py:351
  210.3 4.0 collective-permute-start.12
  214.3 8.8 %collective-permute-start.13 = (bf16[1,8,1024]{2,1,0:T(8,128)(2,1)S(1)}, bf16[1,8,1024]{2,1,0:T(8,128)(2,1)S(1)}, u32[]{:S(2)}, u32[]{:S(2)}) collective-permute-start(bf16[1,8,1024]{2,1,0:T(8,128)(2,1)S(1)} %get-tuple-element.117), channel_id=1, source_target_pairs={{0,14},{2,16},{4,18},{6,20},{8,22},{10,24},{12,26},{14,28},{16,30}... | collective-permute-start | bytes 49160 | tf_op jit(solution)/shard_map/ppermute | solution.py:351
  223.1 3.5 collective-permute-start.14
  223.1 7.3 %collective-permute-start.19 = (bf16[1,8,1024]{2,1,0:T(8,128)(2,1)S(1)}, bf16[1,8,1024]{2,1,0:T(8,128)(2,1)S(1)}, u32[]{:S(2)}, u32[]{:S(2)}) collective-permute-start(bf16[1,8,1024]{2,1,0:T(8,128)(2,1)S(1)} %get-tuple-element.111), channel_id=1, source_target_pairs={{0,26},{2,28},{4,30},{6,0},{8,2},{10,4},{12,6},{14,8},{16,10},{18,... | collective-permute-start | bytes 49160 | tf_op jit(solution)/shard_map/ppermute | solution.py:351
  226.6 4.7 %collective-permute-start.15 = (bf16[1,8,1024]{2,1,0:T(8,128)(2,1)S(1)}, bf16[1,8,1024]{2,1,0:T(8,128)(2,1)S(1)}, u32[]{:S(2)}, u32[]{:S(2)}) collective-permute-start(bf16[1,8,1024]{2,1,0:T(8,128)(2,1)S(1)} %get-tuple-element.115), channel_id=1, source_target_pairs={{0,18},{2,20},{4,22},{6,24},{8,26},{10,28},{12,30},{14,0},{16,2},{... | collective-permute-start | bytes 49160 | tf_op jit(solution)/shard_map/ppermute | solution.py:351
  230.4 5.0 %collective-permute-start.18 = (bf16[1,8,1024]{2,1,0:T(8,128)(2,1)S(1)}, bf16[1,8,1024]{2,1,0:T(8,128)(2,1)S(1)}, u32[]{:S(2)}, u32[]{:S(2)}) collective-permute-start(bf16[1,8,1024]{2,1,0:T(8,128)(2,1)S(1)} %get-tuple-element.112), channel_id=1, source_target_pairs={{0,24},{2,26},{4,28},{6,30},{8,0},{10,2},{12,4},{14,6},{16,8},{18,... | collective-permute-start | bytes 49160 | tf_op jit(solution)/shard_map/ppermute | solution.py:351
  230.4 5.3 %collective-permute-start.17 = (bf16[1,8,1024]{2,1,0:T(8,128)(2,1)S(1)}, bf16[1,8,1024]{2,1,0:T(8,128)(2,1)S(1)}, u32[]{:S(2)}, u32[]{:S(2)}) collective-permute-start(bf16[1,8,1024]{2,1,0:T(8,128)(2,1)S(1)} %get-tuple-element.113), channel_id=1, source_target_pairs={{0,22},{2,24},{4,26},{6,28},{8,30},{10,0},{12,2},{14,4},{16,6},{18... | collective-permute-start | bytes 49160 | tf_op jit(solution)/shard_map/ppermute | solution.py:351
  231.3 7.3 %collective-permute-start.16 = (bf16[1,8,1024]{2,1,0:T(8,128)(2,1)S(1)}, bf16[1,8,1024]{2,1,0:T(8,128)(2,1)S(1)}, u32[]{:S(2)}, u32[]{:S(2)}) collective-permute-start(bf16[1,8,1024]{2,1,0:T(8,128)(2,1)S(1)} %get-tuple-element.114), channel_id=1, source_target_pairs={{0,20},{2,22},{4,24},{6,26},{8,28},{10,30},{12,0},{14,2},{16,4},{1... | collective-permute-start | bytes 49160 | tf_op jit(solution)/shard_map/ppermute | solution.py:351
  235.4 13.5 %collective-permute-start.42 = (bf16[46,8,896]{2,1,0:T(8,128)(2,1)}, bf16[46,8,896]{2,1,0:T(8,128)(2,1)}, u32[]{:S(2)}, u32[]{:S(2)}) collective-permute-start(bf16[46,8,896]{2,1,0:T(8,128)(2,1)} %get-tuple-element.73), channel_id=1, source_target_pairs={{0,8},{1,9},{2,10},{3,11},{4,12},{5,13},{6,14},{7,15},{8,16},{9,17... | collective-permute-start | bytes 1978376 | tf_op jit(solution)/shard_map/ppermute | solution.py:342
  235.7 54.7 %collective-permute-start.43 = (bf16[46,8,896]{2,1,0:T(8,128)(2,1)}, bf16[46,8,896]{2,1,0:T(8,128)(2,1)}, u32[]{:S(2)}, u32[]{:S(2)}) collective-permute-start(bf16[46,8,896]{2,1,0:T(8,128)(2,1)} %get-tuple-element.74), channel_id=1, source_target_pairs={{0,16},{1,17},{2,18},{3,19},{4,20},{5,21},{6,22},{7,23},{8,24},{9,... | collective-permute-start | bytes 1978376 | tf_op jit(solution)/shard_map/ppermute | solution.py:342
  238.6 57.3 %collective-permute-start.44 = (bf16[46,8,896]{2,1,0:T(8,128)(2,1)}, bf16[46,8,896]{2,1,0:T(8,128)(2,1)}, u32[]{:S(2)}, u32[]{:S(2)}) collective-permute-start(bf16[46,8,896]{2,1,0:T(8,128)(2,1)} %get-tuple-element.75), channel_id=1, source_target_pairs={{0,24},{1,25},{2,26},{3,27},{4,28},{5,29},{6,30},{7,31},{8,0},{9,1... | collective-permute-start | bytes 1978376 | tf_op jit(solution)/shard_map/ppermute | solution.py:342
  239.4 61.5 %copy-start.6 = (bf16[16,8,1024]{2,1,0:T(8,128)(2,1)}, bf16[16,8,1024]{2,1,0:T(8,128)(2,1)S(1)}, u32[]{:S(2)}) copy-start(bf16[16,8,1024]{2,1,0:T(8,128)(2,1)S(1)} %constant_dynamic-update-slice_fusion) | copy-start | bytes 786436
  300.9 112.8 %all-to-all-start.6 = ((bf16[256,8,896]{2,1,0:T(8,128)(2,1)}), bf16[256,8,896]{2,1,0:T(8,128)(2,1)}, u32[]{:S(2)}, u32[]{:S(2)}) async-start(bf16[256,8,896]{2,1,0:T(8,128)(2,1)} %bitcast.101), calls=%async_computation.6 | async-start | bytes 7340032 | tf_op jit(solution)/shard_map/all_to_all | solution.py:328
  341.6 20.0 %collective-permute-start.24 = (f32[1,8,1152]{2,1,0:T(8,128)S(1)}, f32[1,8,1152]{2,1,0:T(8,128)S(1)}, u32[]{:S(2)}, u32[]{:S(2)}) collective-permute-start(f32[1,8,1152]{2,1,0:T(8,128)S(1)} %get-tuple-element.108), channel_id=1, source_target_pairs={{0,30},{2,0},{4,2},{6,4},{8,6},{10,8},{12,10},{14,12},{16,14},{18,... | collective-permute-start | bytes 110600 | tf_op jit(solution)/shard_map/ppermute | solution.py:351
  342.8 69.4 %collective-permute-start.38 = (f32[1,8,1152]{2,1,0:T(8,128)S(1)}, f32[1,8,1152]{2,1,0:T(8,128)S(1)}, u32[]{:S(2)}, u32[]{:S(2)}) collective-permute-start(f32[1,8,1152]{2,1,0:T(8,128)S(1)} %get-tuple-element.94), channel_id=1, source_target_pairs={{0,2},{2,4},{4,6},{6,8},{8,10},{10,12},{12,14},{14,16},{16,18},{18... | collective-permute-start | bytes 110600 | tf_op jit(solution)/shard_map/ppermute | solution.py:351
  345.1 67.1 %collective-permute-start.37 = (f32[1,8,1152]{2,1,0:T(8,128)S(1)}, f32[1,8,1152]{2,1,0:T(8,128)S(1)}, u32[]{:S(2)}, u32[]{:S(2)}) collective-permute-start(f32[1,8,1152]{2,1,0:T(8,128)S(1)} %get-tuple-element.95), channel_id=1, source_target_pairs={{0,4},{2,6},{4,8},{6,10},{8,12},{10,14},{12,16},{14,18},{16,20},{1... | collective-permute-start | bytes 110600 | tf_op jit(solution)/shard_map/ppermute | solution.py:351
  345.1 67.1 %collective-permute-start.36 = (f32[1,8,1152]{2,1,0:T(8,128)S(1)}, f32[1,8,1152]{2,1,0:T(8,128)S(1)}, u32[]{:S(2)}, u32[]{:S(2)}) collective-permute-start(f32[1,8,1152]{2,1,0:T(8,128)S(1)} %get-tuple-element.96), channel_id=1, source_target_pairs={{0,6},{2,8},{4,10},{6,12},{8,14},{10,16},{12,18},{14,20},{16,22},{... | collective-permute-start | bytes 110600 | tf_op jit(solution)/shard_map/ppermute | solution.py:351
  345.1 67.1 %collective-permute-start.35 = (f32[1,8,1152]{2,1,0:T(8,128)S(1)}, f32[1,8,1152]{2,1,0:T(8,128)S(1)}, u32[]{:S(2)}, u32[]{:S(2)}) collective-permute-start(f32[1,8,1152]{2,1,0:T(8,128)S(1)} %get-tuple-element.97), channel_id=1, source_target_pairs={{0,8},{2,10},{4,12},{6,14},{8,16},{10,18},{12,20},{14,22},{16,24},... | collective-permute-start | bytes 110600 | tf_op jit(solution)/shard_map/ppermute | solution.py:351
  348.5 65.2 %copy-start.9 = (s32[128]{0:T(128)S(1)}, s32[128]{0:T(128)}, u32[]{:S(2)}) copy-start(s32[128]{0:T(128)} %get-tuple-element.83) | copy-start | bytes 1540
  361.6 3.7 collective-permute-start.25
  365.3 4.0 collective-permute-start.26
  369.3 4.1 collective-permute-start.27
  373.4 7.2 %collective-permute-start.28 = (f32[1,8,1152]{2,1,0:T(8,128)S(1)}, f32[1,8,1152]{2,1,0:T(8,128)S(1)}, u32[]{:S(2)}, u32[]{:S(2)}) collective-permute-start(f32[1,8,1152]{2,1,0:T(8,128)S(1)} %get-tuple-element.104), channel_id=1, source_target_pairs={{0,22},{2,24},{4,26},{6,28},{8,30},{10,0},{12,2},{14,4},{16,6},{18... | collective-permute-start | bytes 110600 | tf_op jit(solution)/shard_map/ppermute | solution.py:351
  380.6 4.9 %collective-permute-start.29 = (f32[1,8,1152]{2,1,0:T(8,128)S(1)}, f32[1,8,1152]{2,1,0:T(8,128)S(1)}, u32[]{:S(2)}, u32[]{:S(2)}) collective-permute-start(f32[1,8,1152]{2,1,0:T(8,128)S(1)} %get-tuple-element.103), channel_id=1, source_target_pairs={{0,20},{2,22},{4,24},{6,26},{8,28},{10,30},{12,0},{14,2},{16,4},{1... | collective-permute-start | bytes 110600 | tf_op jit(solution)/shard_map/ppermute | solution.py:351
  385.5 9.4 %collective-permute-start.30 = (f32[1,8,1152]{2,1,0:T(8,128)S(1)}, f32[1,8,1152]{2,1,0:T(8,128)S(1)}, u32[]{:S(2)}, u32[]{:S(2)}) collective-permute-start(f32[1,8,1152]{2,1,0:T(8,128)S(1)} %get-tuple-element.102), channel_id=1, source_target_pairs={{0,18},{2,20},{4,22},{6,24},{8,26},{10,28},{12,30},{14,0},{16,2},{... | collective-permute-start | bytes 110600 | tf_op jit(solution)/shard_map/ppermute | solution.py:351
  394.8 3.7 collective-permute-start.31
  398.6 6.4 %collective-permute-start.32 = (f32[1,8,1152]{2,1,0:T(8,128)S(1)}, f32[1,8,1152]{2,1,0:T(8,128)S(1)}, u32[]{:S(2)}, u32[]{:S(2)}) collective-permute-start(f32[1,8,1152]{2,1,0:T(8,128)S(1)} %get-tuple-element.100), channel_id=1, source_target_pairs={{0,14},{2,16},{4,18},{6,20},{8,22},{10,24},{12,26},{14,28},{16,30}... | collective-permute-start | bytes 110600 | tf_op jit(solution)/shard_map/ppermute | solution.py:351
  405.0 3.7 collective-permute-start.33
  408.7 3.5 collective-permute-start.34
Sparse Core Ops, SparseCore 0:
  18.6 52.6 all-gather.1
